TPU v7x, 32 devices: a whole 2x2x4 slice. The times are simulated.
32 devices in a mesh: groups: 2 (over x), mesh: 16 (over z, y, core).
Axes of the slice: x: 2, y: 2, z: 4, core: 2. Of those that a mesh axis runs over, the one named last changes fastest.
Arguments:
- state: float32 [3, 64, 32768], P(None, None, ('groups', 'mesh')), parts along dimension 2, may hold values from -6 to 6
- depth: float32 [32768], P(('groups', 'mesh')), parts along dimension 0, may hold values from 0.5 to 4
- coef: float32 [2, 6, 32768], P(None, None, ('groups', 'mesh')), parts along dimension 2, may hold values from -2 to 2
- wet_faces: int32 [6, 32768], P(None, ('groups', 'mesh')), parts along dimension 1, may hold values 0 or 1
- conn: int32 [6, 32768], P(None, ('groups', 'mesh')), parts along dimension 1, may hold values from 0 to 1535, as said below
- send_list: int32 [2, 8192], P(None, ('groups', 'mesh')), parts along dimension 1, may hold values from 0 to 1023, as said below
- obs_nodes: int32 [3, 32768], P(None, ('groups', 'mesh')), parts along dimension 1, may hold values from 0 to 1023
- obs_weight: float32 [3, 32768], P(None, ('groups', 'mesh')), parts along dimension 1, may hold values from 0 to 1, as said below
- obs_value: float32 [32768], P(('groups', 'mesh')), parts along dimension 0, may hold values from -9 to 9
- obs_error: float32 [32768], P(('groups', 'mesh')), parts along dimension 0, may hold values from 0.5 to 2
- loc_ids: int32 [32, 512], P(('groups', 'mesh')), parts along dimension 0, may hold values from 0 to 16383, as said below
- loc_len: int32 [32], P(('groups', 'mesh')), parts along dimension 0, may hold values from 64 to 512, as said below
- loc_weight: float32 [32, 512], P(('groups', 'mesh')), parts along dimension 0, may hold values from 0.05 to 1
Outputs:
- analysis: float32 [3, 64, 32768], P(None, None, ('groups', 'mesh')), parts along dimension 2
There are 2 independent parts, one for each index of `groups`. A program takes and returns all parts, laid end to end along the dimension named above; each array names one. Nothing has to cross between parts.
Inputs may be any that keep to these rules, and one draw needn't show every extreme that they name: `conn`: for each partition: below 1024 a local node; 1024 + p is slot p of the lower partition's list toward it, 1280 + p slot p of the higher partition's list toward it; the first partition names no lower slot and the last no higher one. `send_list`: each partition's two lists hold 256 distinct local node numbers each. `obs_weight`: the three weights of an observation are positive and sum to one. `loc_ids`: the entries of a patch's list are distinct and name observations held by the patch's partition or the two beside it. `loc_len`: patch 0 has a list of length 512.
All inputs are finite; a program needn't handle non-finite values. No bound on the sum of `wet_faces` on one device may be relied on, other than what follows from the above.
Results may differ from a plain program's by a relative error of at most 0.0003.
Values sent between devices are 32-bit elements; how exact they have to be, the bound alone decides.
No kernel may reach another device: no remote copies, remote signals or barrier semaphores. Data moves between devices by JAX's collectives and lax.ppermute only.
A program may use at most 64 MiB of HBM per device.

v0:
```python
import functools
import math

import jax
import jax.numpy as jnp
from jax import lax
from jax.experimental import pallas as pl
from jax.experimental.pallas import tpu as pltpu
from jax.sharding import PartitionSpec as P

STEPS = 2
DT = 0.1
LANES = 128
ROWS = 8
F32 = jnp.float32
BF16 = jnp.bfloat16
TOPMOST = lax.Precision.HIGHEST


def halves(value):
    high = value.astype(BF16)
    return high, (value - high.astype(F32)).astype(BF16)


def stacked(value):
    high, low = halves(value)
    return jnp.concatenate([high, low], axis=0)


def product(stack, high, low):
    rows = stack.shape[0] // 2
    total = jnp.dot(stack, high, preferred_element_type=F32) + jnp.dot(stack, low, preferred_element_type=F32)
    return total[:rows] + total[rows:]


def pick_lanes(sources, indices, targets):
    rows, extent = sources.shape
    plans = []
    for index, target in zip(indices, targets):
        for start in range(0, index.shape[1], LANES):
            wide = jnp.broadcast_to(index[:, start : start + LANES], (ROWS, LANES))
            plans.append((wide & (LANES - 1), wide >> 7, target, start))

    def group(step, carry):
        first = pl.multiple_of(step * ROWS, ROWS)
        for lane, tile, (ref, row0, col0), start in plans:
            total = jnp.zeros((ROWS, LANES), F32)
            for place in range(extent // LANES):
                block = sources[pl.ds(first, ROWS), place * LANES : (place + 1) * LANES]
                found = jnp.take_along_axis(block, lane, axis=1, mode="promise_in_bounds")
                total = jnp.where(tile == place, found, total)
            ref[pl.ds(row0 + first, ROWS), col0 + start : col0 + start + LANES] = total
        return carry

    lax.fori_loop(0, rows // ROWS, group, 0, unroll=2)


def merged(targets, weights):
    targets = list(targets)
    weights = [list(group) for group in weights]
    count = len(targets)
    for first in range(count):
        for second in range(first + 1, count):
            same = targets[first] == targets[second]
            for group in weights:
                group[first] = group[first] + jnp.where(same, group[second], 0.0)
                group[second] = jnp.where(same, 0.0, group[second])
    return weights


def build_operator(targets, weights, outputs, begin, extent, column):
    count = len(targets)
    tall = 2 * ROWS
    wanted = [jnp.broadcast_to(t - begin, (tall, LANES)).astype(jnp.int16) for t in targets]
    parts = []
    for group in weights:
        for w in group:
            high = w.astype(BF16).astype(F32)
            parts.append(
                (
                    jnp.broadcast_to(high, (tall, LANES)).astype(BF16),
                    jnp.broadcast_to(w - high, (tall, LANES)).astype(BF16),
                )
            )

    def block(step, rows):
        first = pl.multiple_of(step * tall, tall)
        values = [jnp.zeros((tall, LANES), BF16) for _ in range(2 * len(weights))]
        for slot in range(count - 1, -1, -1):
            hit = wanted[slot] == rows
            for g in range(len(weights)):
                high, low = parts[g * count + slot]
                values[2 * g] = jnp.where(hit, high, values[2 * g])
                values[2 * g + 1] = jnp.where(hit, low, values[2 * g + 1])
        for value, ref in zip(values, outputs):
            ref[pl.ds(first, tall), column : column + LANES] = value
        return rows + jnp.int16(tall)

    start = lax.broadcasted_iota(jnp.int32, (tall, LANES), 0).astype(jnp.int16)
    lax.fori_loop(0, extent // tall, block, start, unroll=4)


def send_flow_kernel(state, lists, ids, lower, upper):
    members, width = state.shape[1], lists.shape[1]
    for which, ref in enumerate((lower, upper)):
        for part in range(2):
            pick_lanes(state.at[1 + part], [lists[which : which + 1, :]], [(ref, part * members, 0)])
        block = jnp.zeros((ref.shape[0] - 2 * members, width), F32)
        row = lax.broadcasted_iota(jnp.int32, block.shape, 0)
        for piece in range(ids.shape[1] // width):
            numbers = ids[:, piece * width : (piece + 1) * width].astype(F32)
            block = jnp.where(row == piece, jnp.broadcast_to(numbers, block.shape), block)
        ref[2 * members :, :] = block


def prepare_kernel(state, coef, wet, conn, eh, el, nh, nl, geh, gel, gnh, gnl, totals, partial):
    slots, nodes = conn.shape
    ghosts = geh.shape[0]
    for column in range(0, nodes, LANES):
        cut = slice(column, column + LANES)
        targets = [conn[s : s + 1, cut] for s in range(slots)]
        faces = [wet[s : s + 1, cut].astype(F32) for s in range(slots)]
        weights = [[faces[s] * coef[d, s : s + 1, cut] for s in range(slots)] for d in range(2)]
        for d in range(2):
            totals[d : d + 1, cut] = sum(weights[d][1:], weights[d][0])
        weights = merged(targets, weights)
        build_operator(targets, weights, (eh, el, nh, nl), 0, nodes, column)
        build_operator(targets, weights, (geh, gel, gnh, gnl), nodes, ghosts, column)
    partial[...] = (
        product(stacked(state[1]), eh[...], el[...])
        + product(stacked(state[2]), nh[...], nl[...])
        - state[1] * totals[0:1, :]
        - state[2] * totals[1:2, :]
    )


def ghost_flow(lower, upper, part, members):
    rows = slice(part * members, (part + 1) * members)
    return jnp.concatenate([lower[rows, :], upper[rows, :]], axis=1)


def level_kernel(level, partial, depth, lower, upper, geh, gel, gnh, gnl, lists, new_level, to_lower, to_upper):
    members = level.shape[0]
    divergence = (
        partial[...]
        + product(stacked(ghost_flow(lower, upper, 0, members)), geh[...], gel[...])
        + product(stacked(ghost_flow(lower, upper, 1, members)), gnh[...], gnl[...])
    )
    new_level[...] = level[...] - DT * depth[...] * divergence
    pick_lanes(new_level, [lists[0:1, :], lists[1:2, :]], [(to_lower, 0, 0), (to_upper, 0, 0)])


def last_level_kernel(
    level, partial, depth, lower, upper, geh, gel, gnh, gnl, lists, sampling_high, sampling_low, new_level, to_lower, to_upper
):
    members, width = level.shape[0], lists.shape[1]
    entries = to_lower.shape[1] - width
    level_kernel(level, partial, depth, lower, upper, geh, gel, gnh, gnl, lists, new_level, to_lower, to_upper)
    seen = product(
        stacked(new_level[...]), sampling_high[:, : 2 * entries], sampling_low[:, : 2 * entries]
    )
    to_lower[:, width:] = seen[:, :entries]
    to_upper[:, width:] = seen[:, entries:]


def slope_kernel(level, eh, el, nh, nl, totals, east, north):
    stack = stacked(level[...])
    east[...] = product(stack, eh[...], el[...]) - level[...] * totals[0:1, :]
    north[...] = product(stack, nh[...], nl[...]) - level[...] * totals[1:2, :]


def sampling_kernel(
    place, lower, upper, ids, obs_nodes, obs_weight, obs_value, obs_error, high, low, tables, numbers, scratch, found
):
    members_rows = lower.shape[0]
    entries = ids.shape[1]
    width = lower.shape[1]
    obs_count = obs_nodes.shape[1]
    base = place[0] * obs_count
    corners = obs_nodes.shape[0]
    precision = 1.0 / (obs_error[...] * obs_error[...])
    scratch[0:corners, :] = obs_nodes[...].astype(F32)
    scratch[corners : 2 * corners, :] = obs_weight[...]
    scratch[2 * corners : 2 * corners + 1, :] = obs_value[...]
    scratch[2 * corners + 1 : 2 * corners + 2, :] = precision
    first = members_rows - ROWS
    for piece in range(entries // width):
        cut = slice(piece * width, (piece + 1) * width)
        numbers[0:1, cut] = lower[first + piece : first + piece + 1, :].astype(jnp.int32)
        numbers[1:2, cut] = upper[first + piece : first + piece + 1, :].astype(jnp.int32)
    numbers[2:3, :] = ids[...]
    for owner in range(3):
        for start in range(0, entries, LANES):
            index = numbers[owner : owner + 1, start : start + LANES] - base
            own = (index >= 0) & (index < obs_count)
            index = jnp.where(own, index, 0)
            pick_lanes(scratch, [index], [(found, 0, 0)])
            targets = [found[c : c + 1, :].astype(jnp.int32) for c in range(corners)]
            weights = [jnp.where(own, found[corners + c : corners + c + 1, :], 0.0) for c in range(corners)]
            weights = merged(targets, [weights])
            build_operator(targets, weights, (high, low), 0, high.shape[0], owner * entries + start)
            for extra in range(2):
                row = 2 * corners + extra
                tables[2 * owner + extra : 2 * owner + extra + 1, start : start + LANES] = jnp.where(
                    own, found[row : row + 1, :], 0.0
                )


def flow_kernel(
    flow, east, north, lower, upper, geh, gel, gnh, gnl, lists, tables, new_flow, to_lower, to_upper
):
    members, width = east.shape[0], lists.shape[1]
    stack = stacked(jnp.concatenate([lower[...], upper[...]], axis=1))
    new_flow[0] = flow[0] - DT * (east[...] + product(stack, geh[...], gel[...]))
    new_flow[1] = flow[1] - DT * (north[...] + product(stack, gnh[...], gnl[...]))
    entries = tables.shape[1]
    for which, ref in enumerate((to_lower, to_upper)):
        for part in range(2):
            pick_lanes(new_flow.at[part], [lists[which : which + 1, :]], [(ref, part * members, 0)])
        block = jnp.zeros((ref.shape[0] - 2 * members, width), F32)
        row = lax.broadcasted_iota(jnp.int32, block.shape, 0)
        pieces = entries // width
        for extra in range(2):
            for piece in range(pieces):
                values = tables[2 * which + extra : 2 * which + extra + 1, piece * width : (piece + 1) * width]
                block = jnp.where(row == extra * pieces + piece, jnp.broadcast_to(values, block.shape), block)
        ref[2 * members :, :] = block


def divergence_kernel(flow, eh, el, nh, nl, totals, partial):
    partial[...] = (
        product(stacked(flow[0]), eh[...], el[...])
        + product(stacked(flow[1]), nh[...], nl[...])
        - flow[0] * totals[0:1, :]
        - flow[1] * totals[1:2, :]
    )


def last_slope_kernel(level, eh, el, nh, nl, totals, sampling_high, sampling_low, east, north, seen):
    slope_kernel(level, eh, el, nh, nl, totals, east, north)
    entries = seen.shape[1]
    seen[...] = product(
        stacked(level[...]), sampling_high[:, 2 * entries :], sampling_low[:, 2 * entries :]
    )


def inverse_factor(gram):
    size = gram.shape[0]
    row = lax.broadcasted_iota(jnp.int32, (size, size), 0)
    col = lax.broadcasted_iota(jnp.int32, (size, size), 1)
    unit = (row == col).astype(F32)
    table = jnp.concatenate([gram, unit], axis=1)
    blocks = [table[b : b + ROWS, :] for b in range(0, size, ROWS)]
    inner = lax.broadcasted_iota(jnp.int32, (ROWS, 2 * size), 0)
    for pivot in range(size):
        home, spot = divmod(pivot, ROWS)
        line = blocks[home][spot : spot + 1, :]
        scaled = line / line[:, pivot : pivot + 1]
        for b in range(home, len(blocks)):
            factor = blocks[b][:, pivot : pivot + 1]
            change = factor * scaled
            if b == home:
                change = jnp.where(inner > spot, change, 0.0)
            blocks[b] = blocks[b] - change
    table = jnp.concatenate(blocks, axis=0)
    diagonal = jnp.sum(jnp.where(row == col, table[:, :size], 0.0), axis=1, keepdims=True)
    return table[:, size:] * lax.rsqrt(diagonal)


def analysis_kernel(
    length, flow, level, east, north, seen, lower, upper, tables, early_lower, early_upper, loc_weight,
    geh, gel, gnh, gnl, out, fields,
):
    members, nodes = level.shape
    entries = seen.shape[1]
    width = lower.shape[1] - entries
    stack = stacked(jnp.concatenate([lower[:, :width], upper[:, :width]], axis=1))
    fields[0] = level[...]
    fields[1] = flow[0] - DT * (east[...] + product(stack, geh[...], gel[...]))
    fields[2] = flow[1] - DT * (north[...] + product(stack, gnh[...], gnl[...]))
    observed = seen[...] + lower[:, width:] + upper[:, width:]
    obs_mean = jnp.mean(observed, axis=0, keepdims=True)
    anomalies = observed - obs_mean
    pieces = entries // width
    first = early_lower.shape[0] - ROWS

    def received(extra):
        rows = [first + extra * pieces + piece for piece in range(pieces)]
        return jnp.concatenate([early_lower[r : r + 1, :] + early_upper[r : r + 1, :] for r in rows], axis=1)

    value = tables[4:5, :] + received(0)
    precision = tables[5:6, :] + received(1)
    live = lax.broadcasted_iota(jnp.int32, (1, entries), 1) < length[0]
    weight = jnp.where(live, precision * loc_weight[...], 0.0)
    pull = jnp.broadcast_to(weight * (value - obs_mean), (ROWS, entries))
    left = jnp.concatenate([anomalies * weight, pull], axis=0)
    sums = lax.dot_general(left, anomalies, (((1,), (1,)), ((), ())), precision=TOPMOST, preferred_element_type=F32)
    row = lax.broadcasted_iota(jnp.int32, (members, members), 0)
    col = lax.broadcasted_iota(jnp.int32, (members, members), 1)
    gram = sums[:members] + jnp.where(row == col, members - 1.0, 0.0)
    rhs = sums[members : members + 1]
    inverse = inverse_factor(gram)
    halfway = jnp.sum(inverse * rhs, axis=1, keepdims=True)
    mean_w = jnp.sum(inverse * halfway, axis=0, keepdims=True)
    blend = stacked(math.sqrt(members - 1.0) * inverse + mean_w)
    for part in range(3):
        field = fields[part]
        average = jnp.mean(field, axis=0, keepdims=True)
        high, low = halves(field - average)
        out[part] = average + product(blend, high, low)


def call(kernel, outs, args, name, scalars=0, scratch=(), flops=0):
    in_specs = [pl.BlockSpec(memory_space=pltpu.SMEM)] * scalars + [
        pl.BlockSpec(memory_space=pltpu.VMEM)
    ] * (len(args) - scalars)
    held = sum(math.prod(a.shape) * a.dtype.itemsize for a in list(args) + list(outs))
    return pl.pallas_call(
        kernel,
        out_shape=outs,
        in_specs=in_specs,
        out_specs=[pl.BlockSpec(memory_space=pltpu.VMEM)] * len(outs),
        scratch_shapes=scratch,
        name=name,
        cost_estimate=pl.CostEstimate(flops=flops, bytes_accessed=held, transcendentals=0),
    )(*args)


def shape(*dims, dtype=F32):
    return jax.ShapeDtypeStruct(dims, dtype)


def exchange(to_lower, to_upper):
    count = lax.axis_size("mesh")
    ahead = [(i, (i + 1) % count) for i in range(count)]
    back = [(target, source) for source, target in ahead]
    from_lower = lax.ppermute(to_upper, "mesh", ahead)
    from_upper = lax.ppermute(to_lower, "mesh", back)
    return from_lower, from_upper


def local(
    state,
    depth,
    coef,
    wet_faces,
    conn,
    send_list,
    obs_nodes,
    obs_weight,
    obs_value,
    obs_error,
    loc_ids,
    loc_len,
    loc_weight,
):
    members, nodes = state.shape[1:]
    width = send_list.shape[1]
    entries = loc_ids.shape[1]
    ghosts = 2 * width
    assert loc_ids.shape[0] == 1
    depth = depth[None]
    place = lax.axis_index("mesh").astype(jnp.int32)[None]
    work = 8 * members * nodes * nodes

    flow_rows = 2 * members + ROWS
    sent = call(
        send_flow_kernel, [shape(flow_rows, width)] * 2, [state, send_list, loc_ids], "send_flow"
    )
    from_lower, from_upper = exchange(*sent)
    big = [shape(nodes, nodes, dtype=BF16)] * 4
    small = [shape(ghosts, nodes, dtype=BF16)] * 4
    made = call(
        prepare_kernel,
        big + small + [shape(2, nodes), shape(members, nodes)],
        [state, coef, wet_faces, conn],
        "prepare",
        flops=4 * work,
    )
    operators, ghost_operators, totals, partial = made[:4], made[4:8], made[8], made[9]
    level, flow = state[0], state[1:]
    early = (from_lower, from_upper)
    for step in range(STEPS):
        last = step == STEPS - 1
        columns = width + (entries if last else 0)
        outs = [shape(members, nodes)] + [shape(members, columns)] * 2
        args = [level, partial, depth, from_lower, from_upper, *ghost_operators, send_list]
        if last:
            level, *sent = call(last_level_kernel, outs, args + [sampling_high, sampling_low], "last_level", flops=work)
        else:
            level, *sent = call(level_kernel, outs, args, "level", flops=work)
        from_lower, from_upper = exchange(*sent)
        slopes = [shape(members, nodes)] * 2
        args = [level, *operators, totals]
        if last:
            east, north, seen = call(
                last_slope_kernel,
                slopes + [shape(members, entries)],
                args + [sampling_high, sampling_low],
                "last_slope",
                flops=2 * work,
            )
            break
        east, north = call(slope_kernel, slopes, args, "slope", flops=2 * work)
        if step == 0:
            sampling_high, sampling_low, tables = call(
                sampling_kernel,
                [shape(nodes, 3 * entries, dtype=BF16)] * 2 + [shape(ROWS, entries)],
                [place, *early, loc_ids, obs_nodes, obs_weight, obs_value[None], obs_error[None]],
                "sampling",
                scalars=1,
                scratch=[
                    pltpu.VMEM((ROWS, entries), jnp.int32),
                    pltpu.VMEM((ROWS, obs_nodes.shape[1]), F32),
                    pltpu.VMEM((ROWS, LANES), F32),
                ],
                flops=work,
            )
        flow, *sent = call(
            flow_kernel,
            [shape(2, members, nodes)] + [shape(flow_rows, width)] * 2,
            [flow, east, north, from_lower, from_upper, *ghost_operators, send_list, tables],
            "flow",
            flops=work,
        )
        from_lower, from_upper = exchange(*sent)
        told = (from_lower, from_upper)
        (partial,) = call(
            divergence_kernel, [shape(members, nodes)], [flow, *operators, totals], "divergence", flops=2 * work
        )
    (out,) = call(
        analysis_kernel,
        [shape(3, members, nodes)],
        [
            loc_len,
            flow,
            level,
            east,
            north,
            seen,
            from_lower,
            from_upper,
            tables,
            *told,
            loc_weight,
            *ghost_operators,
        ],
        "analysis",
        scalars=1,
        scratch=[pltpu.VMEM((3, members, nodes), F32)],
        flops=work,
    )
    return out


def solution(mesh):
    spread = ("groups", "mesh")
    in_specs = (
        P(None, None, spread),
        P(spread),
        P(None, None, spread),
        P(None, spread),
        P(None, spread),
        P(None, spread),
        P(None, spread),
        P(None, spread),
        P(spread),
        P(spread),
        P(spread, None),
        P(spread),
        P(spread, None),
    )
    out_specs = P(None, None, spread)
    return jax.shard_map(local, mesh=mesh, in_specs=in_specs, out_specs=out_specs, check_vma=False)
```

profile of v0, /device:TPU:0, one launch (start us, length us, event | category | flops | bytes accessed | tf_op | source)
XLA Modules:
  0.0 95.0 jit_solution(8993685870791442207)
XLA Ops:
  0.0 3.6 %send_flow.1 = (f32[136,256]{1,0:T(8,128)}, f32[136,256]{1,0:T(8,128)}) custom-call(f32[3,64,1024]{2,1,0:T(8,128)} %state.3, s32[2,256]{1,0:T(2,128)} %lists.7, s32[1,512]{1,0:T(1,128)} %ids.3), custom_call_target="tpu_custom_call" | custom-call | bytes 1069056 | tf_op jit(solution)/shard_map/send_flow/pallas_call | solution.py:318
  3.6 0.5 collective-permute-start
  4.1 5.0 %collective-permute-start.1 = (f32[136,256]{1,0:T(8,128)}, f32[136,256]{1,0:T(8,128)S(1)}, u32[]{:S(2)}, u32[]{:S(2)}) collective-permute-start(f32[136,256]{1,0:T(8,128)} %get-tuple-element.36), channel_id=1, source_target_pairs={{1,0},{2,1},{3,2},{4,3},{5,4},{6,5},{7,6},{8,7},{9,8},{10,9},{11,1... | collective-permute-start | bytes 417800 | tf_op jit(solution)/shard_map/ppermute | solution.py:338
  9.1 1.7 %slice_bitcast_fusion.level = f32[64,1024]{1,0:T(8,128)} fusion(f32[3,64,1024]{2,1,0:T(8,128)} %state.3), kind=kLoop, calls=%fused_computation | loop fusion | bytes 524288 | tf_op jit(solution)/shard_map/squeeze | solution.py:381
  10.8 1.9 %slice.6.flow = f32[2,64,1024]{2,1,0:T(8,128)} slice(f32[3,64,1024]{2,1,0:T(8,128)} %state.3), slice={[1:3], [0:64], [0:1024]} | slice | bytes 1048576 | tf_op jit(solution)/shard_map/slice | solution.py:381
  12.6 0.6 copy.14.coef
  13.3 10.8 %prepare.1 = (bf16[1024,1024]{1,0:T(8,128)(2,1)}, bf16[1024,1024]{1,0:T(8,128)(2,1)}, bf16[1024,1024]{1,0:T(8,128)(2,1)}, bf16[1024,1024]{1,0:T(8,128)(2,1)}, bf...) custom-call(f32[3,64,1024]{2,1,0:T(8,128)} %state.3, ...), custom_call_target="tpu_custom_call" | custom-call | flops 2147483648 | bytes 13737984 | tf_op jit(solution)/shard_map/prepare/pallas_call | solution.py:318
  24.1 0.6 copy-done.4
  24.7 0.1 copy-done.5
  24.8 4.5 %level.1 = (f32[64,1024]{1,0:T(8,128)}, f32[64,256]{1,0:T(8,128)}, f32[64,256]{1,0:T(8,128)}) custom-call(f32[64,1024]{1,0:T(8,128)} %slice_bitcast_fusion.level, f32[64,1024]{1,0:T(8,128)} %get-tuple-element.34.partial, f32[1,1024]{1,0:T(1,128)} %bitcast.6, f32[136,256]{1,0:T(8,128)} %copy-done.4, f32[136,256]{1,0:T(8,128)} %copy-done.5, ...), custom_call_target="tpu_custom_call" | custom-call | flops 536870912 | bytes 5396480 | tf_op jit(solution)/shard_map/level/pallas_call | solution.py:318
  29.3 4.4 %collective-permute-start.3 = (f32[64,256]{1,0:T(8,128)}, f32[64,256]{1,0:T(8,128)S(1)}, u32[]{:S(2)}, u32[]{:S(2)}) collective-permute-start(f32[64,256]{1,0:T(8,128)} %get-tuple-element.50), channel_id=1, source_target_pairs={{1,0},{2,1},{3,2},{4,3},{5,4},{6,5},{7,6},{8,7},{9,8},{10,9},{11,1... | collective-permute-start | bytes 196616 | tf_op jit(solution)/shard_map/ppermute | solution.py:338
  33.8 5.5 %slope.1 = (f32[64,1024]{1,0:T(8,128)}, f32[64,1024]{1,0:T(8,128)}) custom-call(f32[64,1024]{1,0:T(8,128)} %get-tuple-element.41.level, bf16[1024,1024]{1,0:T(8,128)(2,1)} %get-tuple-element.42.eh, bf16[1024,1024]{1,0:T(8,128)(2,1)} %get-tuple-element.43.el, bf16[1024,1024]{1,0:T(8,128)(2,1)} %get-tuple-element.44.nh, ...), custom_call_target="tpu_custom_call" | custom-call | flops 1073741824 | bytes 9183232 | tf_op jit(solution)/shard_map/slope/pallas_call | solution.py:318
  39.3 6.9 %sampling.1 = (bf16[1024,1536]{1,0:T(8,128)(2,1)}, bf16[1024,1536]{1,0:T(8,128)(2,1)}, f32[8,512]{1,0:T(8,128)}) custom-call(s32[1]{0:T(128)} %bitcast.2.place, f32[136,256]{1,0:T(8,128)} %copy-done.4, f32[136,256]{1,0:T(8,128)} %copy-done.5, s32[1,512]{1,0:T(1,128)} %ids.3, s32[3,1024]{1,0:T(4,128)} %obs_nodes.1, f32[3,1024]{1,0:T(4,128)} %obs_weight.1, ...), custom_call_target="tpu_custom_call" | custom-call | flops 536870912 | bytes 6621188 | tf_op jit(solution)/shard_map/sampling/pallas_call | solution.py:318
  46.2 0.6 copy-done.6
  46.9 5.9 %flow.1 = (f32[2,64,1024]{2,1,0:T(8,128)}, f32[136,256]{1,0:T(8,128)}, f32[136,256]{1,0:T(8,128)}) custom-call(f32[2,64,1024]{2,1,0:T(8,128)} %slice.6.flow, f32[64,1024]{1,0:T(8,128)} %get-tuple-element.47.east, f32[64,1024]{1,0:T(8,128)} %get-tuple-element.48.north, f32[64,256]{1,0:T(8,128)} %copy-done.6, f32[64,256]{1,0:T(8,128)} %copy-done.7, ...), custom_call_target="tpu_custom_call" | custom-call | flops 536870912 | bytes 6195200 | tf_op jit(solution)/shard_map/flow/pallas_call | solution.py:318
  52.8 4.4 %collective-permute-start.5 = (f32[136,256]{1,0:T(8,128)}, f32[136,256]{1,0:T(8,128)S(1)}, u32[]{:S(2)}, u32[]{:S(2)}) collective-permute-start(f32[136,256]{1,0:T(8,128)} %get-tuple-element.54), channel_id=1, source_target_pairs={{1,0},{2,1},{3,2},{4,3},{5,4},{6,5},{7,6},{8,7},{9,8},{10,9},{11,1... | collective-permute-start | bytes 417800 | tf_op jit(solution)/shard_map/ppermute | solution.py:338
  57.2 5.6 %divergence.1.partial = f32[64,1024]{1,0:T(8,128)} custom-call(f32[2,64,1024]{2,1,0:T(8,128)} %get-tuple-element.52.flow, bf16[1024,1024]{1,0:T(8,128)(2,1)} %get-tuple-element.42.eh, bf16[1024,1024]{1,0:T(8,128)(2,1)} %get-tuple-element.43.el, bf16[1024,1024]{1,0:T(8,128)(2,1)} %get-tuple-element.44.nh, bf16[1024,1024]{1,0:T(8,128)(2,1)} %get-tuple-element.45.nl, ...), custom_call_target="tpu_custom_call" | custom-call | flops 1073741824 | bytes 9183232 | tf_op jit(solution)/shard_map/divergence/pallas_call | solution.py:318
  62.8 0.6 copy-done
  63.5 7.2 %last_level.1 = (f32[64,1024]{1,0:T(8,128)}, f32[64,768]{1,0:T(8,128)}, f32[64,768]{1,0:T(8,128)}) custom-call(f32[64,1024]{1,0:T(8,128)} %get-tuple-element.41.level, f32[64,1024]{1,0:T(8,128)} %divergence.1.partial, f32[1,1024]{1,0:T(1,128)} %bitcast.7, f32[136,256]{1,0:T(8,128)} %copy-done, f32[136,256]{1,0:T(8,128)} %copy-done.1, ...), custom_call_target="tpu_custom_call" | custom-call | flops 536870912 | bytes 11950080 | tf_op jit(solution)/shard_map/last_level/pallas_call | solution.py:318
  70.7 4.4 %collective-permute-start.7 = (f32[64,768]{1,0:T(8,128)}, f32[64,768]{1,0:T(8,128)S(1)}, u32[]{:S(2)}, u32[]{:S(2)}) collective-permute-start(f32[64,768]{1,0:T(8,128)} %get-tuple-element.62), channel_id=1, source_target_pairs={{1,0},{2,1},{3,2},{4,3},{5,4},{6,5},{7,6},{8,7},{9,8},{10,9},{11,1... | collective-permute-start | bytes 589832 | tf_op jit(solution)/shard_map/ppermute | solution.py:338
  75.8 7.6 %last_slope.1 = (f32[64,1024]{1,0:T(8,128)}, f32[64,1024]{1,0:T(8,128)}, f32[64,512]{1,0:T(8,128)}) custom-call(f32[64,1024]{1,0:T(8,128)} %get-tuple-element.57.level, bf16[1024,1024]{1,0:T(8,128)(2,1)} %get-tuple-element.42.eh, bf16[1024,1024]{1,0:T(8,128)(2,1)} %get-tuple-element.43.el, bf16[1024,1024]{1,0:T(8,128)(2,1)} %get-tuple-element.44.nh, ...), custom_call_target="tpu_custom_call" | custom-call | flops 1073741824 | bytes 15605760 | tf_op jit(solution)/shard_map/last_slope/pallas_call | solution.py:318
  83.4 0.7 copy-done.2
  84.0 0.1 copy-done.3
  84.1 10.9 %analysis.1 = f32[3,64,1024]{2,1,0:T(8,128)} custom-call(s32[1]{0:T(128)S(6)} %copy.15.length, f32[2,64,1024]{2,1,0:T(8,128)} %get-tuple-element.52.flow, f32[64,1024]{1,0:T(8,128)} %get-tuple-element.57.level, f32[64,1024]{1,0:T(8,128)} %get-tuple-element.58.east, f32[64,1024]{1,0:T(8,128)} %get-tuple-element.59.north, f32[64,512]{1,0:T(8,128)} %get-tuple-element.60.seen, ...), custom_call_target="tpu_custom_call" | custom-call | flops 536870912 | bytes 7112708 | tf_op jit(solution)/shard_map/analysis/pallas_call | solution.py:318
  (23 shorter events, 0.1 us)
Async XLA Ops:
  0.0 12.6 %copy-start.8 = (f32[2,6,1024]{2,0,1:T(2,128)S(1)}, f32[2,6,1024]{2,0,1:T(2,128)}, u32[]{:S(2)}) copy-start(f32[2,6,1024]{2,0,1:T(2,128)} %param.15) | copy-start | bytes 147460
  3.6 20.5 %collective-permute-start = (f32[136,256]{1,0:T(8,128)}, f32[136,256]{1,0:T(8,128)S(1)}, u32[]{:S(2)}, u32[]{:S(2)}) collective-permute-start(f32[136,256]{1,0:T(8,128)} %get-tuple-element.35), channel_id=1, source_target_pairs={{0,1},{1,2},{2,3},{3,4},{4,5},{5,6},{6,7},{7,8},{8,9},{9,10},{10,1... | collective-permute-start | bytes 417800 | tf_op jit(solution)/shard_map/ppermute | solution.py:337
  4.1 20.0 %collective-permute-start.1 = (f32[136,256]{1,0:T(8,128)}, f32[136,256]{1,0:T(8,128)S(1)}, u32[]{:S(2)}, u32[]{:S(2)}) collective-permute-start(f32[136,256]{1,0:T(8,128)} %get-tuple-element.36), channel_id=1, source_target_pairs={{1,0},{2,1},{3,2},{4,3},{5,4},{6,5},{7,6},{8,7},{9,8},{10,9},{11,1... | collective-permute-start | bytes 417800 | tf_op jit(solution)/shard_map/ppermute | solution.py:338
  24.1 0.6 copy-start.4
  24.1 0.7 copy-start.5
  29.3 16.9 %collective-permute-start.2 = (f32[64,256]{1,0:T(8,128)}, f32[64,256]{1,0:T(8,128)S(1)}, u32[]{:S(2)}, u32[]{:S(2)}) collective-permute-start(f32[64,256]{1,0:T(8,128)} %get-tuple-element.49), channel_id=1, source_target_pairs={{0,1},{1,2},{2,3},{3,4},{4,5},{5,6},{6,7},{7,8},{8,9},{9,10},{10,1... | collective-permute-start | bytes 196616 | tf_op jit(solution)/shard_map/ppermute | solution.py:337
  29.3 16.9 %collective-permute-start.3 = (f32[64,256]{1,0:T(8,128)}, f32[64,256]{1,0:T(8,128)S(1)}, u32[]{:S(2)}, u32[]{:S(2)}) collective-permute-start(f32[64,256]{1,0:T(8,128)} %get-tuple-element.50), channel_id=1, source_target_pairs={{1,0},{2,1},{3,2},{4,3},{5,4},{6,5},{7,6},{8,7},{9,8},{10,9},{11,1... | collective-permute-start | bytes 196616 | tf_op jit(solution)/shard_map/ppermute | solution.py:338
  46.2 0.6 copy-start.6
  46.2 0.6 copy-start.7
  52.8 10.0 %collective-permute-start.4 = (f32[136,256]{1,0:T(8,128)}, f32[136,256]{1,0:T(8,128)S(1)}, u32[]{:S(2)}, u32[]{:S(2)}) collective-permute-start(f32[136,256]{1,0:T(8,128)} %get-tuple-element.53), channel_id=1, source_target_pairs={{0,1},{1,2},{2,3},{3,4},{4,5},{5,6},{6,7},{7,8},{8,9},{9,10},{10,1... | collective-permute-start | bytes 417800 | tf_op jit(solution)/shard_map/ppermute | solution.py:337
  52.8 10.0 %collective-permute-start.5 = (f32[136,256]{1,0:T(8,128)}, f32[136,256]{1,0:T(8,128)S(1)}, u32[]{:S(2)}, u32[]{:S(2)}) collective-permute-start(f32[136,256]{1,0:T(8,128)} %get-tuple-element.54), channel_id=1, source_target_pairs={{1,0},{2,1},{3,2},{4,3},{5,4},{6,5},{7,6},{8,7},{9,8},{10,9},{11,1... | collective-permute-start | bytes 417800 | tf_op jit(solution)/shard_map/ppermute | solution.py:338
  62.8 0.7 copy-start
  62.8 0.7 copy-start.1
  70.7 12.7 %collective-permute-start.6 = (f32[64,768]{1,0:T(8,128)}, f32[64,768]{1,0:T(8,128)S(1)}, u32[]{:S(2)}, u32[]{:S(2)}) collective-permute-start(f32[64,768]{1,0:T(8,128)} %get-tuple-element.61), channel_id=1, source_target_pairs={{0,1},{1,2},{2,3},{3,4},{4,5},{5,6},{6,7},{7,8},{8,9},{9,10},{10,1... | collective-permute-start | bytes 589832 | tf_op jit(solution)/shard_map/ppermute | solution.py:337
  70.7 12.7 %collective-permute-start.7 = (f32[64,768]{1,0:T(8,128)}, f32[64,768]{1,0:T(8,128)S(1)}, u32[]{:S(2)}, u32[]{:S(2)}) collective-permute-start(f32[64,768]{1,0:T(8,128)} %get-tuple-element.62), channel_id=1, source_target_pairs={{1,0},{2,1},{3,2},{4,3},{5,4},{6,5},{7,6},{8,7},{9,8},{10,9},{11,1... | collective-permute-start | bytes 589832 | tf_op jit(solution)/shard_map/ppermute | solution.py:338
  83.4 0.7 copy-start.2
  83.4 0.7 copy-start.3
where the time goes:
time: 95.3 us; the launch traced here: 95 us
  Pallas kernels  68.5 us (72%)
  starting transfers between devices  18.8 us (20%)
  local copies, waits for them, and re-layouts  6.95 us (7%)
    pallas_call x10, Pallas kernels, call(): pl.pallas_call(kernel, out_shape=outs, in_specs=in_specs, out_specs=[pl.B...  68.5 us
    ppermute x4, starting transfers between devices, exchange(): from_upper = lax.ppermute(to_lower, 'mesh', back)  18.3 us
    unnamed x19, local copies, waits for them, and re-layouts  3.4 us
  transfers between devices with their start and end apart: 8, of which 0 were waited for; matrix products, arithmetic and copies ran while one was open for 4% of the time, Pallas kernels for 38%

commit v1 on v0

--- a/solution.py
+++ b/solution.py
@@ -100,11 +100,16 @@
     lax.fori_loop(0, extent // tall, block, start, unroll=4)
 
 
-def send_flow_kernel(state, lists, ids, lower, upper):
+def chosen_lists(place, lists):
+    odd = place[0] & 1
+    return lists[pl.ds(1 - odd, 1), :], lists[pl.ds(odd, 1), :]
+
+
+def send_flow_kernel(place, state, lists, ids, near, far):
     members, width = state.shape[1], lists.shape[1]
-    for which, ref in enumerate((lower, upper)):
+    for ref, chosen in zip((near, far), chosen_lists(place, lists)):
         for part in range(2):
-            pick_lanes(state.at[1 + part], [lists[which : which + 1, :]], [(ref, part * members, 0)])
+            pick_lanes(state.at[1 + part], [chosen], [(ref, part * members, 0)])
         block = jnp.zeros((ref.shape[0] - 2 * members, width), F32)
         row = lax.broadcasted_iota(jnp.int32, block.shape, 0)
         for piece in range(ids.shape[1] // width):
@@ -113,12 +118,18 @@
         ref[2 * members :, :] = block
 
 
-def prepare_kernel(state, coef, wet, conn, eh, el, nh, nl, geh, gel, gnh, gnl, totals, partial):
+def prepare_kernel(place, state, coef, wet, conn, eh, el, nh, nl, geh, gel, gnh, gnl, totals, partial):
     slots, nodes = conn.shape
     ghosts = geh.shape[0]
+    turned = (1 - (place[0] & 1)) * (ghosts // 2)
     for column in range(0, nodes, LANES):
         cut = slice(column, column + LANES)
-        targets = [conn[s : s + 1, cut] for s in range(slots)]
+        targets = []
+        for s in range(slots):
+            raw = conn[s : s + 1, cut]
+            ghost = raw - nodes + turned
+            ghost = jnp.where(ghost >= ghosts, ghost - ghosts, ghost)
+            targets.append(jnp.where(raw < nodes, raw, nodes + ghost))
         faces = [wet[s : s + 1, cut].astype(F32) for s in range(slots)]
         weights = [[faces[s] * coef[d, s : s + 1, cut] for s in range(slots)] for d in range(2)]
         for d in range(2):
@@ -134,33 +145,33 @@
     )
 
 
-def ghost_flow(lower, upper, part, members):
+def ghost_flow(near, far, part, members):
     rows = slice(part * members, (part + 1) * members)
-    return jnp.concatenate([lower[rows, :], upper[rows, :]], axis=1)
-
-
-def level_kernel(level, partial, depth, lower, upper, geh, gel, gnh, gnl, lists, new_level, to_lower, to_upper):
+    return jnp.concatenate([near[rows, :], far[rows, :]], axis=1)
+
+
+def level_kernel(place, level, partial, depth, near, far, geh, gel, gnh, gnl, lists, new_level, to_near, to_far):
     members = level.shape[0]
     divergence = (
         partial[...]
-        + product(stacked(ghost_flow(lower, upper, 0, members)), geh[...], gel[...])
-        + product(stacked(ghost_flow(lower, upper, 1, members)), gnh[...], gnl[...])
+        + product(stacked(ghost_flow(near, far, 0, members)), geh[...], gel[...])
+        + product(stacked(ghost_flow(near, far, 1, members)), gnh[...], gnl[...])
     )
     new_level[...] = level[...] - DT * depth[...] * divergence
-    pick_lanes(new_level, [lists[0:1, :], lists[1:2, :]], [(to_lower, 0, 0), (to_upper, 0, 0)])
+    pick_lanes(new_level, chosen_lists(place, lists), [(to_near, 0, 0), (to_far, 0, 0)])
 
 
 def last_level_kernel(
-    level, partial, depth, lower, upper, geh, gel, gnh, gnl, lists, sampling_high, sampling_low, new_level, to_lower, to_upper
+    place, level, partial, depth, near, far, geh, gel, gnh, gnl, lists, sampling_high, sampling_low, new_level, to_near, to_far
 ):
     members, width = level.shape[0], lists.shape[1]
-    entries = to_lower.shape[1] - width
-    level_kernel(level, partial, depth, lower, upper, geh, gel, gnh, gnl, lists, new_level, to_lower, to_upper)
+    entries = to_near.shape[1] - width
+    level_kernel(place, level, partial, depth, near, far, geh, gel, gnh, gnl, lists, new_level, to_near, to_far)
     seen = product(
         stacked(new_level[...]), sampling_high[:, : 2 * entries], sampling_low[:, : 2 * entries]
     )
-    to_lower[:, width:] = seen[:, :entries]
-    to_upper[:, width:] = seen[:, entries:]
+    to_near[:, width:] = seen[:, :entries]
+    to_far[:, width:] = seen[:, entries:]
 
 
 def slope_kernel(level, eh, el, nh, nl, totals, east, north):
@@ -170,11 +181,11 @@
 
 
 def sampling_kernel(
-    place, lower, upper, ids, obs_nodes, obs_weight, obs_value, obs_error, high, low, tables, numbers, scratch, found
+    place, near, far, ids, obs_nodes, obs_weight, obs_value, obs_error, high, low, tables, numbers, scratch, found
 ):
-    members_rows = lower.shape[0]
+    members_rows = near.shape[0]
     entries = ids.shape[1]
-    width = lower.shape[1]
+    width = near.shape[1]
     obs_count = obs_nodes.shape[1]
     base = place[0] * obs_count
     corners = obs_nodes.shape[0]
@@ -186,8 +197,8 @@
     first = members_rows - ROWS
     for piece in range(entries // width):
         cut = slice(piece * width, (piece + 1) * width)
-        numbers[0:1, cut] = lower[first + piece : first + piece + 1, :].astype(jnp.int32)
-        numbers[1:2, cut] = upper[first + piece : first + piece + 1, :].astype(jnp.int32)
+        numbers[0:1, cut] = near[first + piece : first + piece + 1, :].astype(jnp.int32)
+        numbers[1:2, cut] = far[first + piece : first + piece + 1, :].astype(jnp.int32)
     numbers[2:3, :] = ids[...]
     for owner in range(3):
         for start in range(0, entries, LANES):
@@ -207,16 +218,17 @@
 
 
 def flow_kernel(
-    flow, east, north, lower, upper, geh, gel, gnh, gnl, lists, tables, new_flow, to_lower, to_upper
+    place, flow, east, north, near, far, geh, gel, gnh, gnl, lists, tables, new_flow, to_near, to_far
 ):
     members, width = east.shape[0], lists.shape[1]
-    stack = stacked(jnp.concatenate([lower[...], upper[...]], axis=1))
+    stack = stacked(jnp.concatenate([near[...], far[...]], axis=1))
     new_flow[0] = flow[0] - DT * (east[...] + product(stack, geh[...], gel[...]))
     new_flow[1] = flow[1] - DT * (north[...] + product(stack, gnh[...], gnl[...]))
     entries = tables.shape[1]
-    for which, ref in enumerate((to_lower, to_upper)):
+    chosen = chosen_lists(place, lists)
+    for which, ref in enumerate((to_near, to_far)):
         for part in range(2):
-            pick_lanes(new_flow.at[part], [lists[which : which + 1, :]], [(ref, part * members, 0)])
+            pick_lanes(new_flow.at[part], [chosen[which]], [(ref, part * members, 0)])
         block = jnp.zeros((ref.shape[0] - 2 * members, width), F32)
         row = lax.broadcasted_iota(jnp.int32, block.shape, 0)
         pieces = entries // width
@@ -268,25 +280,25 @@
 
 
 def analysis_kernel(
-    length, flow, level, east, north, seen, lower, upper, tables, early_lower, early_upper, loc_weight,
+    length, flow, level, east, north, seen, near, far, tables, early_near, early_far, loc_weight,
     geh, gel, gnh, gnl, out, fields,
 ):
     members, nodes = level.shape
     entries = seen.shape[1]
-    width = lower.shape[1] - entries
-    stack = stacked(jnp.concatenate([lower[:, :width], upper[:, :width]], axis=1))
+    width = near.shape[1] - entries
+    stack = stacked(jnp.concatenate([near[:, :width], far[:, :width]], axis=1))
     fields[0] = level[...]
     fields[1] = flow[0] - DT * (east[...] + product(stack, geh[...], gel[...]))
     fields[2] = flow[1] - DT * (north[...] + product(stack, gnh[...], gnl[...]))
-    observed = seen[...] + lower[:, width:] + upper[:, width:]
+    observed = seen[...] + near[:, width:] + far[:, width:]
     obs_mean = jnp.mean(observed, axis=0, keepdims=True)
     anomalies = observed - obs_mean
     pieces = entries // width
-    first = early_lower.shape[0] - ROWS
+    first = early_near.shape[0] - ROWS
 
     def received(extra):
         rows = [first + extra * pieces + piece for piece in range(pieces)]
-        return jnp.concatenate([early_lower[r : r + 1, :] + early_upper[r : r + 1, :] for r in rows], axis=1)
+        return jnp.concatenate([early_near[r : r + 1, :] + early_far[r : r + 1, :] for r in rows], axis=1)
 
     value = tables[4:5, :] + received(0)
     precision = tables[5:6, :] + received(1)
@@ -310,18 +322,21 @@
         out[part] = average + product(blend, high, low)
 
 
-def call(kernel, outs, args, name, scalars=0, scratch=(), flops=0):
-    in_specs = [pl.BlockSpec(memory_space=pltpu.SMEM)] * scalars + [
-        pl.BlockSpec(memory_space=pltpu.VMEM)
-    ] * (len(args) - scalars)
+def call(kernel, outs, args, name, scalars=0, scratch=(), flops=0, final=False, limit=16):
+    vmem = pl.BlockSpec(memory_space=pltpu.VMEM)
+    in_specs = [pl.BlockSpec(memory_space=pltpu.SMEM)] * scalars + [vmem] * (len(args) - scalars)
     held = sum(math.prod(a.shape) * a.dtype.itemsize for a in list(args) + list(outs))
+    if not final:
+        outs = [pltpu.VMEM(o.shape, o.dtype) for o in outs]
+    args = list(args[:scalars]) + [pltpu.with_memory_space_constraint(a, pltpu.VMEM) for a in args[scalars:]]
     return pl.pallas_call(
         kernel,
         out_shape=outs,
         in_specs=in_specs,
-        out_specs=[pl.BlockSpec(memory_space=pltpu.VMEM)] * len(outs),
+        out_specs=[vmem] * len(outs),
         scratch_shapes=scratch,
         name=name,
+        compiler_params=pltpu.CompilerParams(vmem_limit_bytes=limit << 20),
         cost_estimate=pl.CostEstimate(flops=flops, bytes_accessed=held, transcendentals=0),
     )(*args)
 
@@ -330,13 +345,12 @@
     return jax.ShapeDtypeStruct(dims, dtype)
 
 
-def exchange(to_lower, to_upper):
+def exchange(to_near, to_far):
     count = lax.axis_size("mesh")
-    ahead = [(i, (i + 1) % count) for i in range(count)]
-    back = [(target, source) for source, target in ahead]
-    from_lower = lax.ppermute(to_upper, "mesh", ahead)
-    from_upper = lax.ppermute(to_lower, "mesh", back)
-    return from_lower, from_upper
+    pairs = [(i, i ^ 1) for i in range(count)]
+    others = [(i, (((i + 1) % count) ^ 1) - 1) for i in range(count)]
+    others = [(source, target % count) for source, target in others]
+    return lax.ppermute(to_near, "mesh", pairs), lax.ppermute(to_far, "mesh", others)
 
 
 def local(
@@ -365,31 +379,32 @@
 
     flow_rows = 2 * members + ROWS
     sent = call(
-        send_flow_kernel, [shape(flow_rows, width)] * 2, [state, send_list, loc_ids], "send_flow"
-    )
-    from_lower, from_upper = exchange(*sent)
+        send_flow_kernel, [shape(flow_rows, width)] * 2, [place, state, send_list, loc_ids], "send_flow", scalars=1
+    )
+    from_near, from_far = exchange(*sent)
     big = [shape(nodes, nodes, dtype=BF16)] * 4
     small = [shape(ghosts, nodes, dtype=BF16)] * 4
     made = call(
         prepare_kernel,
         big + small + [shape(2, nodes), shape(members, nodes)],
-        [state, coef, wet_faces, conn],
+        [place, state, coef, wet_faces, conn],
         "prepare",
+        scalars=1,
         flops=4 * work,
     )
     operators, ghost_operators, totals, partial = made[:4], made[4:8], made[8], made[9]
     level, flow = state[0], state[1:]
-    early = (from_lower, from_upper)
+    early = (from_near, from_far)
     for step in range(STEPS):
         last = step == STEPS - 1
         columns = width + (entries if last else 0)
         outs = [shape(members, nodes)] + [shape(members, columns)] * 2
-        args = [level, partial, depth, from_lower, from_upper, *ghost_operators, send_list]
+        args = [place, level, partial, depth, from_near, from_far, *ghost_operators, send_list]
         if last:
-            level, *sent = call(last_level_kernel, outs, args + [sampling_high, sampling_low], "last_level", flops=work)
+            level, *sent = call(last_level_kernel, outs, args + [sampling_high, sampling_low], "last_level", scalars=1, flops=work)
         else:
-            level, *sent = call(level_kernel, outs, args, "level", flops=work)
-        from_lower, from_upper = exchange(*sent)
+            level, *sent = call(level_kernel, outs, args, "level", scalars=1, flops=work)
+        from_near, from_far = exchange(*sent)
         slopes = [shape(members, nodes)] * 2
         args = [level, *operators, totals]
         if last:
@@ -419,12 +434,13 @@
         flow, *sent = call(
             flow_kernel,
             [shape(2, members, nodes)] + [shape(flow_rows, width)] * 2,
-            [flow, east, north, from_lower, from_upper, *ghost_operators, send_list, tables],
+            [place, flow, east, north, from_near, from_far, *ghost_operators, send_list, tables],
             "flow",
+            scalars=1,
             flops=work,
         )
-        from_lower, from_upper = exchange(*sent)
-        told = (from_lower, from_upper)
+        from_near, from_far = exchange(*sent)
+        told = (from_near, from_far)
         (partial,) = call(
             divergence_kernel, [shape(members, nodes)], [flow, *operators, totals], "divergence", flops=2 * work
         )
@@ -438,8 +454,8 @@
             east,
             north,
             seen,
-            from_lower,
-            from_upper,
+            from_near,
+            from_far,
             tables,
             *told,
             loc_weight,
@@ -449,6 +465,7 @@
         scalars=1,
         scratch=[pltpu.VMEM((3, members, nodes), F32)],
         flops=work,
+        final=True,
     )
     return out
 

time: 95.3 us -> 53.2 us (0.56)
  Pallas kernels: 68.5 us -> 29.5 us
  waiting for transfers between devices: 0.02 us -> 7.66 us
  starting transfers between devices: 18.8 us -> 12.3 us
  local copies, waits for them, and re-layouts: 6.95 us -> 2.62 us
    pallas_call x10, Pallas kernels: 68.5 us -> 29.5 us  [call(): pl.pallas_call(kernel, out_shape=outs, in_specs=in_specs, out_specs=[vmem...]
    ppermute x8, waiting for transfers between devices: 0.02 us -> 7.66 us  [the longest x4 7.65 us: exchange(): lax.ppermute(to_far, 'mesh', others)]
    ppermute x8, starting transfers between devices: 18.8 us -> 12.3 us  [the longest x4 11.6 us: exchange(): lax.ppermute(to_far, 'mesh', others)]
    slice x1, local copies, waits for them, and re-layouts: 1.88 us -> 0.04 us  [local(): level, flow = (state[0], state[1:])]
    squeeze x1, local copies, waits for them, and re-layouts: 1.67 us -> 0.02 us  [local(): level, flow = (state[0], state[1:])]
    unnamed x19 -> x29, local copies, waits for them, and re-layouts: 3.4 us -> 2.57 us
  transfers between devices with their start and end apart: 8 -> 8, of which waited for: 0 -> 3; matrix products, arithmetic and copies ran while one was open for 4% -> 0% of each run, Pallas kernels for 38% -> 25%
where the time goes in v1:
time: 53.2 us; the launch traced here: 53 us
  Pallas kernels  29.5 us (55%)
  starting transfers between devices  12.3 us (23%)
  waiting for transfers between devices  7.66 us (14%)
  local copies, waits for them, and re-layouts  2.62 us (5%)
  between operations  0.92 us (2%)
    pallas_call x10, Pallas kernels, call(): pl.pallas_call(kernel, out_shape=outs, in_specs=in_specs, out_specs=[vmem...  29.5 us
    ppermute x4, starting transfers between devices, exchange(): lax.ppermute(to_far, 'mesh', others)  11.6 us
    ppermute x4, waiting for transfers between devices, exchange(): lax.ppermute(to_far, 'mesh', others)  7.65 us
    unnamed x29, local copies, waits for them, and re-layouts  2.57 us
  transfers between devices with their start and end apart: 8, of which 3 were waited for; matrix products, arithmetic and copies ran while one was open for 0% of the time, Pallas kernels for 25%

profile of v1, /device:TPU:0, one launch (start us, length us, event | category | flops | bytes accessed | tf_op | source)
XLA Modules:
  0.0 53.0 jit_solution(1677416611193911734)
XLA Ops:
  0.0 1.1 %copy-done = f32[3,64,1024]{2,1,0:T(8,128)S(1)} copy-done((f32[3,64,1024]{2,1,0:T(8,128)S(1)}, f32[3,64,1024]{2,1,0:T(8,128)}, u32[]{:S(2)}) %copy-start) | copy-done | bytes 786456
  1.1 0.7 %copy-done.1 = s32[2,256]{1,0:T(2,128)S(1)} copy-done((s32[2,256]{1,0:T(2,128)S(1)}, s32[2,256]{1,0:T(2,128)}, u32[]{:S(2)}) %copy-start.1) | copy-done | bytes 2072
  1.8 0.7 %copy-done.4 = s32[1,512]{1,0:T(1,128)S(1)} copy-done((s32[1,512]{1,0:T(1,128)S(1)}, s32[1,512]{1,0:T(1,128)}, u32[]{:S(2)}) %copy-start.4) | copy-done | bytes 2072
  2.5 1.8 %send_flow.1 = (f32[136,256]{1,0:T(8,128)S(1)}, f32[136,256]{1,0:T(8,128)S(1)}) custom-call(s32[1]{0:T(128)} %bitcast.place, f32[3,64,1024]{2,1,0:T(8,128)S(1)} %copy-done, s32[2,256]{1,0:T(2,128)S(1)} %copy-done.1, s32[1,512]{1,0:T(1,128)S(1)} %copy-done.4), custom_call_target="tpu_custom_call" | custom-call | bytes 1069060 | tf_op jit(solution)/shard_map/send_flow/pallas_call | solution.py:332
  4.3 0.6 %collective-permute-start = (f32[136,256]{1,0:T(8,128)S(1)}, f32[136,256]{1,0:T(8,128)S(1)}, u32[]{:S(2)}, u32[]{:S(2)}) collective-permute-start(f32[136,256]{1,0:T(8,128)S(1)} %get-tuple-element.35), channel_id=1, source_target_pairs={{0,1},{1,0},{2,3},{3,2},{4,5},{5,4},{6,7},{7,6},{8,9},{9,8},{10,11... | collective-permute-start | bytes 417800 | tf_op jit(solution)/shard_map/ppermute | solution.py:353
  4.8 5.7 %collective-permute-start.1 = (f32[136,256]{1,0:T(8,128)S(1)}, f32[136,256]{1,0:T(8,128)S(1)}, u32[]{:S(2)}, u32[]{:S(2)}) collective-permute-start(f32[136,256]{1,0:T(8,128)S(1)} %get-tuple-element.36), channel_id=1, source_target_pairs={{0,15},{1,2},{2,1},{3,4},{4,3},{5,6},{6,5},{7,8},{8,7},{9,10},{10,... | collective-permute-start | bytes 417800 | tf_op jit(solution)/shard_map/ppermute | solution.py:353
  10.7 6.3 %prepare.1 = (bf16[1024,1024]{1,0:T(8,128)(2,1)S(1)}, bf16[1024,1024]{1,0:T(8,128)(2,1)S(1)}, bf16[1024,1024]{1,0:T(8,128)(2,1)S(1)}, bf16[1024,1024]{1,0:T(8,12...) custom-call(s32[1]{0:T(128)} %bitcast.place, ...), custom_call_target="tpu_custom_call" | custom-call | flops 2147483648 | bytes 13737988 | tf_op jit(solution)/shard_map/prepare/pallas_call | solution.py:332
  17.0 1.4 %level.1 = (f32[64,1024]{1,0:T(8,128)S(1)}, f32[64,256]{1,0:T(8,128)S(1)}, f32[64,256]{1,0:T(8,128)S(1)}) custom-call(s32[1]{0:T(128)} %bitcast.place, f32[64,1024]{1,0:T(8,128)S(1)} %slice_bitcast_fusion.level, f32[64,1024]{1,0:T(8,128)S(1)} %get-tuple-element.34.partial, f32[1,1024]{1,0:T(1,128)S(1)} %bitcast.6, f32[136,256]{1,0:T(8,128)S(1)} %collective-permute-done.near, ...), custom_call_target="tpu_custom_call" | custom-call | flops 536870912 | bytes 5396484 | tf_op jit(solution)/shard_map/level/pallas_call | solution.py:332
  18.4 0.1 collective-permute-start.2
  18.5 0.8 %collective-permute-start.3 = (f32[64,256]{1,0:T(8,128)S(1)}, f32[64,256]{1,0:T(8,128)S(1)}, u32[]{:S(2)}, u32[]{:S(2)}) collective-permute-start(f32[64,256]{1,0:T(8,128)S(1)} %get-tuple-element.50), channel_id=1, source_target_pairs={{0,15},{1,2},{2,1},{3,4},{4,3},{5,6},{6,5},{7,8},{8,7},{9,10},{10,... | collective-permute-start | bytes 196616 | tf_op jit(solution)/shard_map/ppermute | solution.py:353
  19.3 1.3 %slope.1 = (f32[64,1024]{1,0:T(8,128)S(1)}, f32[64,1024]{1,0:T(8,128)S(1)}) custom-call(f32[64,1024]{1,0:T(8,128)S(1)} %get-tuple-element.41.level, bf16[1024,1024]{1,0:T(8,128)(2,1)S(1)} %get-tuple-element.42.eh, bf16[1024,1024]{1,0:T(8,128)(2,1)S(1)} %get-tuple-element.43.el, bf16[1024,1024]{1,0:T(8,128)(2,1)S(1)} %get-tuple-element.44.nh, ...), custom_call_target="tpu_custom_call" | custom-call | flops 1073741824 | bytes 9183232 | tf_op jit(solution)/shard_map/slope/pallas_call | solution.py:332
  20.6 3.1 %sampling.1 = (bf16[1024,1536]{1,0:T(8,128)(2,1)S(1)}, bf16[1024,1536]{1,0:T(8,128)(2,1)S(1)}, f32[8,512]{1,0:T(8,128)S(1)}) custom-call(s32[1]{0:T(128)} %bitcast.place, f32[136,256]{1,0:T(8,128)S(1)} %collective-permute-done.near, f32[136,256]{1,0:T(8,128)S(1)} %collective-permute-done.1.far, s32[1,512]{1,0:T(1,128)S(1)} %copy-done.5, ...), custom_call_target="tpu_custom_call" | custom-call | flops 536870912 | bytes 6621188 | tf_op jit(solution)/shard_map/sampling/pallas_call | solution.py:332
  23.7 1.3 %collective-permute-done.3.far = f32[64,256]{1,0:T(8,128)S(1)} collective-permute-done((f32[64,256]{1,0:T(8,128)S(1)}, f32[64,256]{1,0:T(8,128)S(1)}, u32[]{:S(2)}, u32[]{:S(2)}) %collective-permute-start.3) | collective-permute-done | bytes 65568 | tf_op jit(solution)/shard_map/ppermute | solution.py:353
  25.0 2.5 %flow.1 = (f32[2,64,1024]{2,1,0:T(8,128)S(1)}, f32[136,256]{1,0:T(8,128)S(1)}, f32[136,256]{1,0:T(8,128)S(1)}) custom-call(s32[1]{0:T(128)} %bitcast.place, f32[2,64,1024]{2,1,0:T(8,128)S(1)} %slice.6.flow, f32[64,1024]{1,0:T(8,128)S(1)} %get-tuple-element.47.east, f32[64,1024]{1,0:T(8,128)S(1)} %get-tuple-element.48.north, ...), custom_call_target="tpu_custom_call" | custom-call | flops 536870912 | bytes 6195204 | tf_op jit(solution)/shard_map/flow/pallas_call | solution.py:332
  27.5 0.1 collective-permute-start.4
  27.6 2.6 %collective-permute-start.5 = (f32[136,256]{1,0:T(8,128)S(1)}, f32[136,256]{1,0:T(8,128)S(1)}, u32[]{:S(2)}, u32[]{:S(2)}) collective-permute-start(f32[136,256]{1,0:T(8,128)S(1)} %get-tuple-element.54), channel_id=1, source_target_pairs={{0,15},{1,2},{2,1},{3,4},{4,3},{5,6},{6,5},{7,8},{8,7},{9,10},{10,... | collective-permute-start | bytes 417800 | tf_op jit(solution)/shard_map/ppermute | solution.py:353
  30.1 1.3 %divergence.1.partial = f32[64,1024]{1,0:T(8,128)S(1)} custom-call(f32[2,64,1024]{2,1,0:T(8,128)S(1)} %get-tuple-element.52.flow, bf16[1024,1024]{1,0:T(8,128)(2,1)S(1)} %get-tuple-element.42.eh, bf16[1024,1024]{1,0:T(8,128)(2,1)S(1)} %get-tuple-element.43.el, bf16[1024,1024]{1,0:T(8,128)(2,1)S(1)} %get-tuple-element.44.nh, ...), custom_call_target="tpu_custom_call" | custom-call | flops 1073741824 | bytes 9183232 | tf_op jit(solution)/shard_map/divergence/pallas_call | solution.py:332
  31.4 3.4 %collective-permute-done.5.far.early_far = f32[136,256]{1,0:T(8,128)S(1)} collective-permute-done((f32[136,256]{1,0:T(8,128)S(1)}, f32[136,256]{1,0:T(8,128)S(1)}, u32[]{:S(2)}, u32[]{:S(2)}) %collective-permute-start.5) | collective-permute-done | bytes 139296 | tf_op jit(solution)/shard_map/ppermute | solution.py:353
  34.8 2.1 %last_level.1 = (f32[64,1024]{1,0:T(8,128)S(1)}, f32[64,768]{1,0:T(8,128)S(1)}, f32[64,768]{1,0:T(8,128)S(1)}) custom-call(s32[1]{0:T(128)} %bitcast.place, f32[64,1024]{1,0:T(8,128)S(1)} %get-tuple-element.41.level, f32[64,1024]{1,0:T(8,128)S(1)} %divergence.1.partial, f32[1,1024]{1,0:T(1,128)S(1)} %bitcast.7, ...), custom_call_target="tpu_custom_call" | custom-call | flops 536870912 | bytes 11950084 | tf_op jit(solution)/shard_map/last_level/pallas_call | solution.py:332
  36.9 0.1 collective-permute-start.6
  37.0 2.6 %collective-permute-start.7 = (f32[64,768]{1,0:T(8,128)S(1)}, f32[64,768]{1,0:T(8,128)S(1)}, u32[]{:S(2)}, u32[]{:S(2)}) collective-permute-start(f32[64,768]{1,0:T(8,128)S(1)} %get-tuple-element.62), channel_id=1, source_target_pairs={{0,15},{1,2},{2,1},{3,4},{4,3},{5,6},{6,5},{7,8},{8,7},{9,10},{10,... | collective-permute-start | bytes 589832 | tf_op jit(solution)/shard_map/ppermute | solution.py:353
  40.3 1.6 %last_slope.1 = (f32[64,1024]{1,0:T(8,128)S(1)}, f32[64,1024]{1,0:T(8,128)S(1)}, f32[64,512]{1,0:T(8,128)S(1)}) custom-call(f32[64,1024]{1,0:T(8,128)S(1)} %get-tuple-element.57.level, bf16[1024,1024]{1,0:T(8,128)(2,1)S(1)} %get-tuple-element.42.eh, bf16[1024,1024]{1,0:T(8,128)(2,1)S(1)} %get-tuple-element.43.el, ...), custom_call_target="tpu_custom_call" | custom-call | flops 1073741824 | bytes 15605760 | tf_op jit(solution)/shard_map/last_slope/pallas_call | solution.py:332
  41.9 3.0 %collective-permute-done.7.far = f32[64,768]{1,0:T(8,128)S(1)} collective-permute-done((f32[64,768]{1,0:T(8,128)S(1)}, f32[64,768]{1,0:T(8,128)S(1)}, u32[]{:S(2)}, u32[]{:S(2)}) %collective-permute-start.7) | collective-permute-done | bytes 196640 | tf_op jit(solution)/shard_map/ppermute | solution.py:353
  44.9 8.1 %analysis.1 = f32[3,64,1024]{2,1,0:T(8,128)} custom-call(s32[1]{0:T(128)S(6)} %copy.15.length, f32[2,64,1024]{2,1,0:T(8,128)S(1)} %get-tuple-element.52.flow, f32[64,1024]{1,0:T(8,128)S(1)} %get-tuple-element.57.level, f32[64,1024]{1,0:T(8,128)S(1)} %get-tuple-element.58.east, f32[64,1024]{1,0:T(8,128)S(1)} %get-tuple-element.59.north, ...), custom_call_target="tpu_custom_call" | custom-call | flops 536870912 | bytes 7112708 | tf_op jit(solution)/shard_map/analysis/pallas_call | solution.py:332
  (33 shorter events, 0.1 us)
Async XLA Ops:
  0.0 1.1 %copy-start = (f32[3,64,1024]{2,1,0:T(8,128)S(1)}, f32[3,64,1024]{2,1,0:T(8,128)}, u32[]{:S(2)}) copy-start(f32[3,64,1024]{2,1,0:T(8,128)} %state.3) | copy-start | bytes 2359300
  1.1 0.7 %copy-start.1 = (s32[2,256]{1,0:T(2,128)S(1)}, s32[2,256]{1,0:T(2,128)}, u32[]{:S(2)}) copy-start(s32[2,256]{1,0:T(2,128)} %lists.7) | copy-start | bytes 6148
  1.8 0.7 %copy-start.4 = (s32[1,512]{1,0:T(1,128)S(1)}, s32[1,512]{1,0:T(1,128)}, u32[]{:S(2)}) copy-start(s32[1,512]{1,0:T(1,128)} %ids.3) | copy-start | bytes 6148
  2.5 8.1 %copy-start.13 = (f32[2,6,1024]{2,0,1:T(2,128)S(1)}, f32[2,6,1024]{2,0,1:T(2,128)}, u32[]{:S(2)}) copy-start(f32[2,6,1024]{2,0,1:T(2,128)} %param.15) | copy-start | bytes 147460
  2.5 8.1 %copy-start.7 = (s32[6,1024]{1,0:T(8,128)S(1)}, s32[6,1024]{1,0:T(8,128)}, u32[]{:S(2)}) copy-start(s32[6,1024]{1,0:T(8,128)} %wet.1) | copy-start | bytes 73732
  2.5 8.1 %copy-start.8 = (s32[6,1024]{1,0:T(8,128)S(1)}, s32[6,1024]{1,0:T(8,128)}, u32[]{:S(2)}) copy-start(s32[6,1024]{1,0:T(8,128)} %conn.1) | copy-start | bytes 73732
  4.3 12.7 %collective-permute-start = (f32[136,256]{1,0:T(8,128)S(1)}, f32[136,256]{1,0:T(8,128)S(1)}, u32[]{:S(2)}, u32[]{:S(2)}) collective-permute-start(f32[136,256]{1,0:T(8,128)S(1)} %get-tuple-element.35), channel_id=1, source_target_pairs={{0,1},{1,0},{2,3},{3,2},{4,5},{5,4},{6,7},{7,6},{8,9},{9,8},{10,11... | collective-permute-start | bytes 417800 | tf_op jit(solution)/shard_map/ppermute | solution.py:353
  4.8 12.1 %collective-permute-start.1 = (f32[136,256]{1,0:T(8,128)S(1)}, f32[136,256]{1,0:T(8,128)S(1)}, u32[]{:S(2)}, u32[]{:S(2)}) collective-permute-start(f32[136,256]{1,0:T(8,128)S(1)} %get-tuple-element.36), channel_id=1, source_target_pairs={{0,15},{1,2},{2,1},{3,4},{4,3},{5,6},{6,5},{7,8},{8,7},{9,10},{10,... | collective-permute-start | bytes 417800 | tf_op jit(solution)/shard_map/ppermute | solution.py:353
  10.6 6.4 %copy-start.2 = (s32[2,256]{1,0:T(2,128)S(1)}, s32[2,256]{1,0:T(2,128)}, u32[]{:S(2)}) copy-start(s32[2,256]{1,0:T(2,128)} %lists.7) | copy-start | bytes 6148
  10.6 6.4 %copy-start.3 = (f32[1024]{0:T(1024)S(1)}, f32[1024]{0:T(1024)}, u32[]{:S(2)}) copy-start(f32[1024]{0:T(1024)} %param.14) | copy-start | bytes 12292
  18.4 5.3 %collective-permute-start.2 = (f32[64,256]{1,0:T(8,128)S(1)}, f32[64,256]{1,0:T(8,128)S(1)}, u32[]{:S(2)}, u32[]{:S(2)}) collective-permute-start(f32[64,256]{1,0:T(8,128)S(1)} %get-tuple-element.49), channel_id=1, source_target_pairs={{0,1},{1,0},{2,3},{3,2},{4,5},{5,4},{6,7},{7,6},{8,9},{9,8},{10,11... | collective-permute-start | bytes 196616 | tf_op jit(solution)/shard_map/ppermute | solution.py:353
  18.5 6.5 %collective-permute-start.3 = (f32[64,256]{1,0:T(8,128)S(1)}, f32[64,256]{1,0:T(8,128)S(1)}, u32[]{:S(2)}, u32[]{:S(2)}) collective-permute-start(f32[64,256]{1,0:T(8,128)S(1)} %get-tuple-element.50), channel_id=1, source_target_pairs={{0,15},{1,2},{2,1},{3,4},{4,3},{5,6},{6,5},{7,8},{8,7},{9,10},{10,... | collective-permute-start | bytes 196616 | tf_op jit(solution)/shard_map/ppermute | solution.py:353
  19.3 1.3 %copy-start.5 = (s32[1,512]{1,0:T(1,128)S(1)}, s32[1,512]{1,0:T(1,128)}, u32[]{:S(2)}) copy-start(s32[1,512]{1,0:T(1,128)} %ids.3) | copy-start | bytes 6148
  19.3 1.3 %copy-start.9 = (s32[3,1024]{1,0:T(4,128)S(1)}, s32[3,1024]{1,0:T(4,128)}, u32[]{:S(2)}) copy-start(s32[3,1024]{1,0:T(4,128)} %obs_nodes.1) | copy-start | bytes 36868
  19.3 1.3 %copy-start.10 = (f32[3,1024]{1,0:T(4,128)S(1)}, f32[3,1024]{1,0:T(4,128)}, u32[]{:S(2)}) copy-start(f32[3,1024]{1,0:T(4,128)} %obs_weight.1) | copy-start | bytes 36868
  19.3 1.4 %copy-start.11 = (f32[1024]{0:T(1024)S(1)}, f32[1024]{0:T(1024)}, u32[]{:S(2)}) copy-start(f32[1024]{0:T(1024)} %param.21) | copy-start | bytes 12292
  19.3 1.4 %copy-start.12 = (f32[1024]{0:T(1024)S(1)}, f32[1024]{0:T(1024)}, u32[]{:S(2)}) copy-start(f32[1024]{0:T(1024)} %param.22) | copy-start | bytes 12292
  27.5 3.9 %collective-permute-start.4 = (f32[136,256]{1,0:T(8,128)S(1)}, f32[136,256]{1,0:T(8,128)S(1)}, u32[]{:S(2)}, u32[]{:S(2)}) collective-permute-start(f32[136,256]{1,0:T(8,128)S(1)} %get-tuple-element.53), channel_id=1, source_target_pairs={{0,1},{1,0},{2,3},{3,2},{4,5},{5,4},{6,7},{7,6},{8,9},{9,8},{10,11... | collective-permute-start | bytes 417800 | tf_op jit(solution)/shard_map/ppermute | solution.py:353
  27.6 7.2 %collective-permute-start.5 = (f32[136,256]{1,0:T(8,128)S(1)}, f32[136,256]{1,0:T(8,128)S(1)}, u32[]{:S(2)}, u32[]{:S(2)}) collective-permute-start(f32[136,256]{1,0:T(8,128)S(1)} %get-tuple-element.54), channel_id=1, source_target_pairs={{0,15},{1,2},{2,1},{3,4},{4,3},{5,6},{6,5},{7,8},{8,7},{9,10},{10,... | collective-permute-start | bytes 417800 | tf_op jit(solution)/shard_map/ppermute | solution.py:353
  36.9 4.9 %collective-permute-start.6 = (f32[64,768]{1,0:T(8,128)S(1)}, f32[64,768]{1,0:T(8,128)S(1)}, u32[]{:S(2)}, u32[]{:S(2)}) collective-permute-start(f32[64,768]{1,0:T(8,128)S(1)} %get-tuple-element.61), channel_id=1, source_target_pairs={{0,1},{1,0},{2,3},{3,2},{4,5},{5,4},{6,7},{7,6},{8,9},{9,8},{10,11... | collective-permute-start | bytes 589832 | tf_op jit(solution)/shard_map/ppermute | solution.py:353
  37.0 7.9 %collective-permute-start.7 = (f32[64,768]{1,0:T(8,128)S(1)}, f32[64,768]{1,0:T(8,128)S(1)}, u32[]{:S(2)}, u32[]{:S(2)}) collective-permute-start(f32[64,768]{1,0:T(8,128)S(1)} %get-tuple-element.62), channel_id=1, source_target_pairs={{0,15},{1,2},{2,1},{3,4},{4,3},{5,6},{6,5},{7,8},{8,7},{9,10},{10,... | collective-permute-start | bytes 589832 | tf_op jit(solution)/shard_map/ppermute | solution.py:353
  40.3 4.6 %copy-start.6 = (f32[1,512]{1,0:T(1,128)S(1)}, f32[1,512]{1,0:T(1,128)}, u32[]{:S(2)}) copy-start(f32[1,512]{1,0:T(1,128)} %loc_weight.1) | copy-start | bytes 6148

commit v2 on v1

v2 whole, which is shorter than its diff:
```python
import math

import jax
import jax.numpy as jnp
from jax import lax
from jax.experimental import pallas as pl
from jax.experimental.pallas import tpu as pltpu
from jax.sharding import PartitionSpec as P

STEPS = 2
DT = 0.1
LANES = 128
ROWS = 8
F32 = jnp.float32
BF16 = jnp.bfloat16
TOPMOST = lax.Precision.HIGHEST


def halves(value):
    high = value.astype(BF16)
    return high, (value - high.astype(F32)).astype(BF16)


def stacked(value):
    high, low = halves(value)
    return jnp.concatenate([high, low], axis=0)


def product(stack, high, low, first=0, count=None):
    rows = stack.shape[0] // 2
    count = high.shape[0] if count is None else count
    pieces = []
    for tile in range(first, first + count, 2):
        total = 0.0
        for part in (high, low):
            block = jnp.concatenate([part[tile], part[tile + 1]], axis=1)
            total = total + jnp.dot(stack, block, preferred_element_type=F32)
        pieces.append(total[:rows] + total[rows:])
    return jnp.concatenate(pieces, axis=1)


def pick_lanes(sources, indices, targets):
    rows, extent = sources.shape
    plans = []
    for index, target in zip(indices, targets):
        for start in range(0, index.shape[1], LANES):
            wide = jnp.broadcast_to(index[:, start : start + LANES], (ROWS, LANES))
            plans.append((wide & (LANES - 1), wide >> 7, target, start))

    def group(step, carry):
        first = pl.multiple_of(step * ROWS, ROWS)
        for lane, tile, (ref, row0, col0), start in plans:
            total = jnp.zeros((ROWS, LANES), F32)
            for place in range(extent // LANES):
                block = sources[pl.ds(first, ROWS), place * LANES : (place + 1) * LANES]
                found = jnp.take_along_axis(block, lane, axis=1, mode="promise_in_bounds")
                total = jnp.where(tile == place, found, total)
            ref[pl.ds(row0 + first, ROWS), col0 + start : col0 + start + LANES] = total
        return carry

    lax.fori_loop(0, rows // ROWS, group, 0, unroll=4)


def merged(targets, weights):
    targets = list(targets)
    weights = [list(group) for group in weights]
    count = len(targets)
    for first in range(count):
        for second in range(first + 1, count):
            same = targets[first] == targets[second]
            for group in weights:
                group[first] = group[first] + jnp.where(same, group[second], 0.0)
                group[second] = jnp.where(same, 0.0, group[second])
    return weights


def build_operator(targets, weights, outputs, begin, extent, tile):
    count = len(targets)
    tall = 2 * ROWS
    wanted = [jnp.broadcast_to(t - begin, (tall, LANES)).astype(jnp.int16) for t in targets]
    parts = []
    for group in weights:
        for w in group:
            high = w.astype(BF16).astype(F32)
            parts.append(
                (
                    jnp.broadcast_to(high, (tall, LANES)).astype(BF16),
                    jnp.broadcast_to(w - high, (tall, LANES)).astype(BF16),
                )
            )

    def block(step, rows):
        first = pl.multiple_of(step * tall, tall)
        values = [jnp.zeros((tall, LANES), BF16) for _ in range(2 * len(weights))]
        for slot in range(count - 1, -1, -1):
            hit = wanted[slot] == rows
            for g in range(len(weights)):
                high, low = parts[g * count + slot]
                values[2 * g] = jnp.where(hit, high, values[2 * g])
                values[2 * g + 1] = jnp.where(hit, low, values[2 * g + 1])
        for value, ref in zip(values, outputs):
            ref[tile, pl.ds(first, tall), :] = value
        return rows + jnp.int16(tall)

    start = lax.broadcasted_iota(jnp.int32, (tall, LANES), 0).astype(jnp.int16)
    lax.fori_loop(0, extent // tall, block, start, unroll=8)


def chosen_lists(place, lists):
    odd = place[0] & 1
    return lists[pl.ds(1 - odd, 1), :], lists[pl.ds(odd, 1), :]


def live_weight(weight, length):
    entry = lax.broadcasted_iota(jnp.int32, weight.shape, 1)
    return jnp.where(entry < length, weight, 0.0)


def send_flow_kernel(place, length, *refs):
    count = (len(refs) - 3) // 2
    held, (near, far), kept, arrived = refs[:count], refs[count : count + 2], refs[count + 2 : -1], refs[-1]
    state_at, state, lists, ids, weight = held[0], kept[0], kept[1], kept[2], kept[3]
    members, width = state.shape[1], lists.shape[1]
    pairs = [(held[1], lists), (state_at.at[1], state.at[1]), (state_at.at[2], state.at[2])]
    pairs += list(zip(held[2:], kept[2:])) + [(state_at.at[0], state.at[0])]
    copies = [pltpu.make_async_copy(a, b, arrived.at[n]) for n, (a, b) in enumerate(pairs)]
    for copy in copies:
        copy.start()
    copies[0].wait()
    chosen = chosen_lists(place, lists)
    for part in range(2):
        copies[1 + part].wait()
        pick_lanes(state.at[1 + part], chosen, [(near, part * members, 0), (far, part * members, 0)])
    for copy in copies[3:]:
        copy.wait()
    block = jnp.zeros((near.shape[0] - 2 * members, width), F32)
    row = lax.broadcasted_iota(jnp.int32, block.shape, 0)
    pieces = ids.shape[1] // width
    for at, values in enumerate((ids[...].astype(F32), live_weight(weight[...], length[0]))):
        for piece in range(pieces):
            line = values[:, piece * width : (piece + 1) * width]
            block = jnp.where(row == at * pieces + piece, jnp.broadcast_to(line, block.shape), block)
    near[2 * members :, :] = block
    far[2 * members :, :] = block


def prepare_kernel(place, state, coef, wet, conn, eh, el, nh, nl, geh, gel, gnh, gnl, totals, partial):
    slots, nodes = conn.shape
    ghosts = geh.shape[1]
    turned = (1 - (place[0] & 1)) * (ghosts // 2)
    for column in range(0, nodes, LANES):
        cut = slice(column, column + LANES)
        targets = []
        for s in range(slots):
            raw = conn[s : s + 1, cut]
            ghost = raw - nodes + turned
            ghost = jnp.where(ghost >= ghosts, ghost - ghosts, ghost)
            targets.append(jnp.where(raw < nodes, raw, nodes + ghost))
        faces = [wet[s : s + 1, cut].astype(F32) for s in range(slots)]
        weights = [[faces[s] * coef[s, d : d + 1, cut] for s in range(slots)] for d in range(2)]
        for d in range(2):
            totals[d : d + 1, cut] = sum(weights[d][1:], weights[d][0])
        weights = merged(targets, weights)
        build_operator(targets, weights, (eh, el, nh, nl), 0, nodes, column // LANES)
        build_operator(targets, weights, (geh, gel, gnh, gnl), nodes, ghosts, column // LANES)
    partial[...] = (
        product(stacked(state[1]), eh, el)
        + product(stacked(state[2]), nh, nl)
        - state[1] * totals[0:1, :]
        - state[2] * totals[1:2, :]
    )


def ghost_flow(near, far, part, members):
    rows = slice(part * members, (part + 1) * members)
    return jnp.concatenate([near[rows, :], far[rows, :]], axis=1)


def level_kernel(place, held, partial, depth, near, far, geh, gel, gnh, gnl, lists, new_level, to_near, to_far):
    level = held.at[0] if len(held.shape) == 3 else held
    members = level.shape[0]
    divergence = (
        partial[...]
        + product(stacked(ghost_flow(near, far, 0, members)), geh, gel)
        + product(stacked(ghost_flow(near, far, 1, members)), gnh, gnl)
    )
    new_level[...] = level[...] - DT * depth[...] * divergence
    pick_lanes(new_level, chosen_lists(place, lists), [(to_near, 0, 0), (to_far, 0, 0)])


def list_sums(seen, value, weight):
    obs_mean = jnp.mean(seen, axis=0, keepdims=True)
    anomalies = seen - obs_mean
    pull = jnp.broadcast_to(weight * (value - obs_mean), (ROWS, seen.shape[1]))
    left = jnp.concatenate([anomalies * weight, pull], axis=0)
    return lax.dot_general(left, anomalies, (((1,), (1,)), ((), ())), precision=TOPMOST, preferred_element_type=F32)


def last_level_kernel(
    place, level, partial, depth, near, far, geh, gel, gnh, gnl, lists, high, low, tables, new_level, to_near, to_far
):
    members, width = new_level.shape[0], lists.shape[1]
    level_kernel(place, level, partial, depth, near, far, geh, gel, gnh, gnl, lists, new_level, to_near, to_far)
    tiles = high.shape[0] // 3
    stack = stacked(new_level[...])
    for which, ref in enumerate((to_near, to_far)):
        seen = product(stack, high, low, which * tiles, tiles)
        sums = list_sums(seen, tables[2 * which : 2 * which + 1, :], tables[2 * which + 1 : 2 * which + 2, :])
        ref[members:, :width] = jnp.zeros((ROWS, width), F32)
        ref[:, width:] = jnp.concatenate([sums, jnp.zeros((members + ROWS, LANES - members), F32)], axis=1)


def slope_kernel(level, eh, el, nh, nl, totals, east, north):
    stack = stacked(level[...])
    east[...] = product(stack, eh, el) - level[...] * totals[0:1, :]
    north[...] = product(stack, nh, nl) - level[...] * totals[1:2, :]


def sampling_kernel(
    place, length, near, far, ids, weight, obs_nodes, obs_weight, obs_value, obs_error, high, low, tables,
    numbers, strengths, scratch, found,
):
    entries, width = ids.shape[1], near.shape[1]
    corners, obs_count = obs_nodes.shape
    base = place[0] * obs_count
    scratch[0:corners, :] = obs_nodes[...].astype(F32)
    scratch[corners : 2 * corners, :] = obs_weight[...]
    scratch[2 * corners : 2 * corners + 1, :] = obs_value[...]
    scratch[2 * corners + 1 : 2 * corners + 2, :] = 1.0 / (obs_error[...] * obs_error[...])
    first = near.shape[0] - ROWS
    pieces = entries // width
    for piece in range(pieces):
        cut = slice(piece * width, (piece + 1) * width)
        for owner, ref in enumerate((near, far)):
            at = first + piece
            numbers[owner : owner + 1, cut] = ref[at : at + 1, :].astype(jnp.int32)
            strengths[owner : owner + 1, cut] = ref[at + pieces : at + pieces + 1, :]
    numbers[2:3, :] = ids[...]
    strengths[2:3, :] = live_weight(weight[...], length[0])
    tiles = entries // LANES
    places = [(owner, tile) for owner in range(3) for tile in range(tiles)]
    kept = {}
    for owner, tile in places:
        index = numbers[owner : owner + 1, tile * LANES : (tile + 1) * LANES] - base
        own = (index >= 0) & (index < obs_count)
        kept[owner, tile] = own, jnp.where(own, index, 0)
    pick_lanes(
        scratch,
        [kept[spot][1] for spot in places],
        [(found, 0, (owner * tiles + tile) * LANES) for owner, tile in places],
    )
    for owner, tile in places:
        at = owner * tiles + tile
        own = kept[owner, tile][0]
        here = found[:, at * LANES : (at + 1) * LANES]
        targets = [here[c : c + 1, :].astype(jnp.int32) for c in range(corners)]
        shares = [jnp.where(own, here[corners + c : corners + c + 1, :], 0.0) for c in range(corners)]
        shares = merged(targets, [shares])
        build_operator(targets, shares, (high, low), 0, high.shape[1], at)
        cut = slice(tile * LANES, (tile + 1) * LANES)
        force = here[2 * corners + 1 : 2 * corners + 2, :] * strengths[owner : owner + 1, cut]
        tables[2 * owner : 2 * owner + 1, cut] = here[2 * corners : 2 * corners + 1, :]
        tables[2 * owner + 1 : 2 * owner + 2, cut] = jnp.where(own, force, 0.0)


def flow_kernel(place, flow, east, north, near, far, geh, gel, gnh, gnl, lists, new_flow, to_near, to_far):
    members = east.shape[0]
    stack = stacked(jnp.concatenate([near[...], far[...]], axis=1))
    chosen = chosen_lists(place, lists)
    first = flow.shape[0] - 2
    new_flow[0] = flow[first] - DT * (east[...] + product(stack, geh, gel))
    new_flow[1] = flow[first + 1] - DT * (north[...] + product(stack, gnh, gnl))
    for part in range(2):
        pick_lanes(new_flow.at[part], chosen, [(to_near, part * members, 0), (to_far, part * members, 0)])


def divergence_kernel(flow, eh, el, nh, nl, totals, partial):
    partial[...] = (
        product(stacked(flow[0]), eh, el)
        + product(stacked(flow[1]), nh, nl)
        - flow[0] * totals[0:1, :]
        - flow[1] * totals[1:2, :]
    )


def last_slope_kernel(level, eh, el, nh, nl, totals, high, low, tables, east, north, sums):
    slope_kernel(level, eh, el, nh, nl, totals, east, north)
    tiles = high.shape[0] // 3
    seen = product(stacked(level[...]), high, low, 2 * tiles, tiles)
    sums[...] = list_sums(seen, tables[4:5, :], tables[5:6, :])


def pair_inverse(a, b, c):
    r = 1.0 / (a * c - b * b)
    return c * r, -(b * r), a * r


def pair_rows(a, b, c, first, second):
    m = b / a
    return first * lax.rsqrt(a), (second - m * first) * lax.rsqrt(c - m * b)


def inverse_factor(gram):
    size = gram.shape[0]
    wide = (ROWS, 2 * size)
    row = lax.broadcasted_iota(jnp.int32, (size, size), 0)
    col = lax.broadcasted_iota(jnp.int32, (size, size), 1)
    table = jnp.concatenate([gram, (row == col).astype(F32)], axis=1)
    blocks = [table[b : b + ROWS, :] for b in range(0, size, ROWS)]
    inner = lax.broadcasted_iota(jnp.int32, wide, 0)

    def spread(value):
        return jnp.broadcast_to(value, wide)

    done = []
    for home in range(len(blocks)):
        result = jnp.zeros(wide, F32)
        for spot in range(0, ROWS, 4):
            pivot = home * ROWS + spot
            lines = [spread(blocks[home][spot + i : spot + i + 1, :]) for i in range(4)]
            columns = [spread(blocks[home][:, pivot + i : pivot + i + 1]) for i in range(4)]

            def entry(i, j):
                return spread(columns[j][spot + i : spot + i + 1, :])

            head = entry(0, 0), entry(1, 0), entry(1, 1)
            p = pair_inverse(*head)
            b = [[entry(2 + i, j) for j in range(2)] for i in range(2)]
            t = [[b[i][0] * p[0] + b[i][1] * p[1], b[i][0] * p[1] + b[i][1] * p[2]] for i in range(2)]
            tail = (
                entry(2, 2) - (t[0][0] * b[0][0] + t[0][1] * b[0][1]),
                entry(3, 2) - (t[1][0] * b[0][0] + t[1][1] * b[0][1]),
                entry(3, 3) - (t[1][0] * b[1][0] + t[1][1] * b[1][1]),
            )
            rest = [lines[2 + i] - (t[i][0] * lines[0] + t[i][1] * lines[1]) for i in range(2)]
            q = pair_inverse(*tail)
            z2 = q[0] * rest[0] + q[1] * rest[1]
            z3 = q[1] * rest[0] + q[2] * rest[1]
            z0 = (p[0] * lines[0] + p[1] * lines[1]) - (t[0][0] * z2 + t[1][0] * z3)
            z1 = (p[1] * lines[0] + p[2] * lines[1]) - (t[0][1] * z2 + t[1][1] * z3)
            final = pair_rows(*head, lines[0], lines[1]) + pair_rows(*tail, rest[0], rest[1])
            for i, value in enumerate(final):
                result = jnp.where(inner == spot + i, value, result)
            for place in range(home, len(blocks)):
                factors = columns
                if place > home:
                    factors = [spread(blocks[place][:, pivot + i : pivot + i + 1]) for i in range(4)]
                elif spot + 4 == ROWS:
                    continue
                change = (factors[2] * z2 + factors[3] * z3) + (factors[0] * z0 + factors[1] * z1)
                if place == home:
                    change = jnp.where(inner >= spot + 4, change, 0.0)
                blocks[place] = blocks[place] - change
        done.append(result)
    return jnp.concatenate(done, axis=0)[:, size:]


def analysis_kernel(flow, level, east, north, sums, near, far, geh, gel, gnh, gnl, out, fields):
    members = level.shape[0]
    width = near.shape[1] - LANES
    total = sums[...] + near[:, width : width + members] + far[:, width : width + members]
    row = lax.broadcasted_iota(jnp.int32, (members, members), 0)
    col = lax.broadcasted_iota(jnp.int32, (members, members), 1)
    gram = total[:members] + jnp.where(row == col, members - 1.0, 0.0)
    rhs = total[members : members + 1]
    inverse = inverse_factor(gram)
    stack = stacked(jnp.concatenate([near[:members, :width], far[:members, :width]], axis=1))
    fields[0] = level[...]
    fields[1] = flow[0] - DT * (east[...] + product(stack, geh, gel))
    fields[2] = flow[1] - DT * (north[...] + product(stack, gnh, gnl))
    halfway = jnp.sum(inverse * rhs, axis=1, keepdims=True)
    mean_w = jnp.sum(inverse * halfway, axis=0, keepdims=True)
    blend = stacked(math.sqrt(members - 1.0) * inverse + mean_w)
    for part in range(3):
        field = fields[part]
        average = jnp.mean(field, axis=0, keepdims=True)
        high, low = halves(field - average)
        moved = jnp.dot(blend, high, preferred_element_type=F32) + jnp.dot(blend, low, preferred_element_type=F32)
        out[part] = average + moved[:members] + moved[members:]


def call(kernel, outs, args, scalars=0, scratch=(), flops=0, final=False, limit=16, raw=False):
    vmem = pl.BlockSpec(memory_space=pltpu.VMEM)
    in_specs = [pl.BlockSpec(memory_space=pltpu.SMEM)] * scalars + [pl.BlockSpec(memory_space=pltpu.HBM) if raw else vmem] * (len(args) - scalars)
    held = sum(math.prod(a.shape) * a.dtype.itemsize for a in list(args) + list(outs))
    if not final:
        outs = [pltpu.VMEM(o.shape, o.dtype) for o in outs]
    space = pltpu.HBM if raw else pltpu.VMEM
    args = list(args[:scalars]) + [pltpu.with_memory_space_constraint(a, space) for a in args[scalars:]]
    return pl.pallas_call(
        kernel,
        out_shape=outs,
        in_specs=in_specs,
        out_specs=[vmem] * len(outs),
        scratch_shapes=scratch,
        compiler_params=pltpu.CompilerParams(vmem_limit_bytes=limit << 20),
        cost_estimate=pl.CostEstimate(flops=flops, bytes_accessed=held, transcendentals=0),
    )(*args)


def shape(*dims, dtype=F32):
    return jax.ShapeDtypeStruct(dims, dtype)


def exchange(to_near, to_far):
    count = lax.axis_size("mesh")
    pairs = [(i, i ^ 1) for i in range(count)]
    others = [(i, (((i + 1) % count) ^ 1) - 1) for i in range(count)]
    others = [(source, target % count) for source, target in others]
    from_far = lax.ppermute(to_far, "mesh", others)
    from_near = lax.ppermute(to_near, "mesh", pairs)
    return from_near, from_far


def local(
    state,
    depth,
    coef,
    wet_faces,
    conn,
    send_list,
    obs_nodes,
    obs_weight,
    obs_value,
    obs_error,
    loc_ids,
    loc_len,
    loc_weight,
):
    members, nodes = state.shape[1:]
    width = send_list.shape[1]
    entries = loc_ids.shape[1]
    ghosts = 2 * width
    tiles = nodes // LANES
    assert loc_ids.shape[0] == 1
    depth = depth[None]
    place = lax.axis_index("mesh").astype(jnp.int32)[None]
    work = 8 * members * nodes * nodes

    brought = [state, send_list, loc_ids, loc_weight, depth, jnp.swapaxes(coef, 0, 1), wet_faces, conn]
    brought += [obs_nodes, obs_weight, obs_value[None], obs_error[None]]
    near, far, *brought = call(
        send_flow_kernel,
        [shape(2 * members + ROWS, width)] * 2 + [shape(*a.shape, dtype=a.dtype) for a in brought],
        [place, loc_len, *brought],
        scalars=2,
        scratch=[pltpu.SemaphoreType.DMA((len(brought) + 2,))],
        raw=True,
    )
    sent = [near, far]
    state, send_list, loc_ids, loc_weight, depth, coef, wet_faces, conn = brought[:8]
    obs_nodes, obs_weight, obs_value, obs_error = brought[8:]
    from_near, from_far = exchange(*sent)
    big = [shape(tiles, nodes, LANES, dtype=BF16)] * 4
    small = [shape(tiles, ghosts, LANES, dtype=BF16)] * 4
    made = call(
        prepare_kernel,
        big + small + [shape(2, nodes), shape(members, nodes)],
        [place, state, coef, wet_faces, conn],
        scalars=1,
        flops=4 * work,
    )
    operators, ghost_operators, totals, partial = made[:4], made[4:8], made[8], made[9]
    level = flow = state
    early = from_near, from_far
    for step in range(STEPS):
        last = step == STEPS - 1
        args = [place, level, partial, depth, from_near, from_far, *ghost_operators, send_list]
        kernel, extra, payload = level_kernel, [], shape(members, width)
        if last:
            kernel, extra, payload = last_level_kernel, list(sampling), shape(members + ROWS, width + LANES)
        level, *sent = call(kernel, [shape(members, nodes), payload, payload], args + extra, scalars=1, flops=work)
        from_near, from_far = exchange(*sent)
        slopes = [shape(members, nodes)] * 2
        args = [level, *operators, totals]
        if last:
            east, north, sums = call(
                last_slope_kernel, slopes + [shape(members + ROWS, members)], args + list(sampling), flops=2 * work
            )
            break
        east, north = call(slope_kernel, slopes, args, flops=2 * work)
        flow, *sent = call(
            flow_kernel,
            [shape(2, members, nodes)] + [shape(2 * members, width)] * 2,
            [place, flow, east, north, from_near, from_far, *ghost_operators, send_list],
            scalars=1,
            flops=work,
        )
        early, sent[0] = lax.optimization_barrier((early, sent[0]))
        from_near, from_far = exchange(*sent)
        (partial,) = call(divergence_kernel, [shape(members, nodes)], [flow, *operators, totals], flops=2 * work)
        sampling = call(
            sampling_kernel,
            [shape(3 * entries // LANES, nodes, LANES, dtype=BF16)] * 2 + [shape(ROWS, entries)],
            [place, loc_len, *early, loc_ids, loc_weight, obs_nodes, obs_weight, obs_value, obs_error],
            scalars=2,
            scratch=[
                pltpu.VMEM((ROWS, entries), jnp.int32),
                pltpu.VMEM((ROWS, entries), F32),
                pltpu.VMEM((ROWS, obs_nodes.shape[1]), F32),
                pltpu.VMEM((ROWS, 3 * entries), F32),
            ],
            flops=work,
        )
    (out,) = call(
        analysis_kernel,
        [shape(3, members, nodes)],
        [flow, level, east, north, sums, from_near, from_far, *ghost_operators],
        scratch=[pltpu.VMEM((3, members, nodes), F32)],
        flops=work,
        final=True,
    )
    return out


def solution(mesh):
    spread = ("groups", "mesh")
    in_specs = (
        P(None, None, spread),
        P(spread),
        P(None, None, spread),
        P(None, spread),
        P(None, spread),
        P(None, spread),
        P(None, spread),
        P(None, spread),
        P(spread),
        P(spread),
        P(spread, None),
        P(spread),
        P(spread, None),
    )
    out_specs = P(None, None, spread)
    return jax.shard_map(local, mesh=mesh, in_specs=in_specs, out_specs=out_specs, check_vma=False)
```

time: 53.2 us -> 46.7 us (0.88)
  Pallas kernels: 29.5 us -> 25.6 us
  local copies, waits for them, and re-layouts: 2.62 us -> 0 us
  waiting for transfers between devices: 7.66 us -> 9.53 us
  starting transfers between devices: 12.3 us -> 10.5 us
    pallas_call x10, Pallas kernels: 29.5 us -> 25.6 us  [call(): pl.pallas_call(kernel, out_shape=outs, in_specs=in_specs, out_specs=[vmem...]
    unnamed x29 -> x0, local copies, waits for them, and re-layouts: 2.57 us -> none
    ppermute x8, waiting for transfers between devices: 7.66 us -> 9.53 us  [the longest x4 9.52 us: exchange(): from_far = lax.ppermute(to_far, 'mesh', others)]
    ppermute x8, starting transfers between devices: 12.3 us -> 10.5 us  [the longest x4 9.78 us: exchange(): from_far = lax.ppermute(to_far, 'mesh', others)]
  transfers between devices with their start and end apart: 8 -> 8, of which waited for: 3 -> 3; matrix products, arithmetic and copies ran while one was open for 0% -> 0% of each run, Pallas kernels for 25% -> 27%
where the time goes in v2:
time: 46.7 us; the launch traced here: 46.5 us
  Pallas kernels  25.6 us (55%)
  starting transfers between devices  10.5 us (22%)
  waiting for transfers between devices  9.53 us (20%)
  between operations  0.78 us (2%)
    pallas_call x10, Pallas kernels, call(): pl.pallas_call(kernel, out_shape=outs, in_specs=in_specs, out_specs=[vmem...  25.6 us
    ppermute x4, starting transfers between devices, exchange(): from_far = lax.ppermute(to_far, 'mesh', others)  9.78 us
    ppermute x4, waiting for transfers between devices, exchange(): from_far = lax.ppermute(to_far, 'mesh', others)  9.52 us
  transfers between devices with their start and end apart: 8, of which 3 were waited for; matrix products, arithmetic and copies ran while one was open for 0% of the time, Pallas kernels for 27%

profile of v2, /device:TPU:0, one launch (start us, length us, event | category | flops | bytes accessed | tf_op | source)
XLA Modules:
  0.0 46.5 jit_solution(8340043911240828550)
XLA Ops:
  0.7 2.2 %shard_map.127 = (f32[136,256]{1,0:T(8,128)S(1)}, f32[136,256]{1,0:T(8,128)S(1)}, f32[3,64,1024]{2,1,0:T(8,128)S(1)}, s32[2,256]{1,0:T(2,128)S(1)}, s32[1,512]{1...) custom-call(s32[1]{0:T(128)} %bitcast.place, ...), custom_call_target="tpu_custom_call" | custom-call | bytes 2134024 | tf_op jit(solution)/shard_map/pallas_call | solution.py:390
  2.9 0.6 %collective-permute-start = (f32[136,256]{1,0:T(8,128)S(1)}, f32[136,256]{1,0:T(8,128)S(1)}, u32[]{:S(2)}, u32[]{:S(2)}) collective-permute-start(f32[136,256]{1,0:T(8,128)S(1)} %get-tuple-element.55), channel_id=1, source_target_pairs={{0,1},{1,0},{2,3},{3,2},{4,5},{5,4},{6,7},{7,6},{8,9},{9,8},{10,11... | collective-permute-start | bytes 417800 | tf_op jit(solution)/shard_map/ppermute | solution.py:411
  3.4 5.7 %collective-permute-start.1 = (f32[136,256]{1,0:T(8,128)S(1)}, f32[136,256]{1,0:T(8,128)S(1)}, u32[]{:S(2)}, u32[]{:S(2)}) collective-permute-start(f32[136,256]{1,0:T(8,128)S(1)} %get-tuple-element.56), channel_id=1, source_target_pairs={{0,15},{1,2},{2,1},{3,4},{4,3},{5,6},{6,5},{7,8},{8,7},{9,10},{10,... | collective-permute-start | bytes 417800 | tf_op jit(solution)/shard_map/ppermute | solution.py:410
  9.1 5.8 %shard_map.128 = (bf16[8,1024,128]{2,1,0:T(8,128)(2,1)S(1)}, bf16[8,1024,128]{2,1,0:T(8,128)(2,1)S(1)}, bf16[8,1024,128]{2,1,0:T(8,128)(2,1)S(1)}, bf16[8,1024,1...) custom-call(s32[1]{0:T(128)} %bitcast.place, ...), custom_call_target="tpu_custom_call" | custom-call | flops 2147483648 | bytes 13737988 | tf_op jit(solution)/shard_map/pallas_call | solution.py:390
  14.9 0.0 collective-permute-done.near
  15.0 1.3 %shard_map.129 = (f32[64,1024]{1,0:T(8,128)S(1)}, f32[64,256]{1,0:T(8,128)S(1)}, f32[64,256]{1,0:T(8,128)S(1)}) custom-call(s32[1]{0:T(128)} %bitcast.place, f32[3,64,1024]{2,1,0:T(8,128)S(1)} %get-tuple-element.49.state.held.flow, f32[64,1024]{1,0:T(8,128)S(1)} %get-tuple-element.53.partial, f32[1,1024]{1,0:T(1,128)S(1)} %get-tuple-element.54.depth, ...), custom_call_target="tpu_custom_call" | custom-call | flops 536870912 | bytes 5920772 | tf_op jit(solution)/shard_map/pallas_call | solution.py:390
  16.2 0.1 collective-permute-start.2
  16.3 1.4 %collective-permute-start.3 = (f32[64,256]{1,0:T(8,128)S(1)}, f32[64,256]{1,0:T(8,128)S(1)}, u32[]{:S(2)}, u32[]{:S(2)}) collective-permute-start(f32[64,256]{1,0:T(8,128)S(1)} %get-tuple-element.71), channel_id=1, source_target_pairs={{0,15},{1,2},{2,1},{3,4},{4,3},{5,6},{6,5},{7,8},{8,7},{9,10},{10,... | collective-permute-start | bytes 196616 | tf_op jit(solution)/shard_map/ppermute | solution.py:410
  17.7 1.3 %shard_map.130 = (f32[64,1024]{1,0:T(8,128)S(1)}, f32[64,1024]{1,0:T(8,128)S(1)}) custom-call(f32[64,1024]{1,0:T(8,128)S(1)} %get-tuple-element.62.level, bf16[8,1024,128]{2,1,0:T(8,128)(2,1)S(1)} %get-tuple-element.63.eh, bf16[8,1024,128]{2,1,0:T(8,128)(2,1)S(1)} %get-tuple-element.64.el, bf16[8,1024,128]{2,1,0:T(8,128)(2,1)S(1)} %get-tuple-element.65.nh, ...), custom_call_target="tpu_custom_call" | custom-call | flops 1073741824 | bytes 9183232 | tf_op jit(solution)/shard_map/pallas_call | solution.py:390
  19.0 0.0 collective-permute-done.2.near
  19.0 3.8 %collective-permute-done.3.far = f32[64,256]{1,0:T(8,128)S(1)} collective-permute-done((f32[64,256]{1,0:T(8,128)S(1)}, f32[64,256]{1,0:T(8,128)S(1)}, u32[]{:S(2)}, u32[]{:S(2)}) %collective-permute-start.3) | collective-permute-done | bytes 65568 | tf_op jit(solution)/shard_map/ppermute | solution.py:410
  22.7 1.8 %shard_map.131 = (f32[2,64,1024]{2,1,0:T(8,128)S(1)}, f32[128,256]{1,0:T(8,128)S(1)}, f32[128,256]{1,0:T(8,128)S(1)}) custom-call(s32[1]{0:T(128)} %bitcast.place, f32[3,64,1024]{2,1,0:T(8,128)S(1)} %get-tuple-element.49.state.held.flow, f32[64,1024]{1,0:T(8,128)S(1)} %get-tuple-element.68.east, f32[64,1024]{1,0:T(8,128)S(1)} %get-tuple-element.69.north, ...), custom_call_target="tpu_custom_call" | custom-call | flops 536870912 | bytes 6424580 | tf_op jit(solution)/shard_map/pallas_call | solution.py:390
  24.6 0.1 collective-permute-start.4
  24.6 1.4 %collective-permute-start.5 = (f32[128,256]{1,0:T(8,128)S(1)}, f32[128,256]{1,0:T(8,128)S(1)}, u32[]{:S(2)}, u32[]{:S(2)}) collective-permute-start(f32[128,256]{1,0:T(8,128)S(1)} %get-tuple-element.75), channel_id=1, source_target_pairs={{0,15},{1,2},{2,1},{3,4},{4,3},{5,6},{6,5},{7,8},{8,7},{9,10},{10,... | collective-permute-start | bytes 393224 | tf_op jit(solution)/shard_map/ppermute | solution.py:410
  26.0 2.3 %shard_map.133 = (bf16[12,1024,128]{2,1,0:T(8,128)(2,1)S(1)}, bf16[12,1024,128]{2,1,0:T(8,128)(2,1)S(1)}, f32[8,512]{1,0:T(8,128)S(1)}) custom-call(s32[1]{0:T(128)} %bitcast.place, s32[1]{0:T(128)S(6)} %copy.14.length, f32[136,256]{1,0:T(8,128)S(1)} %collective-permute-done.near, f32[136,256]{1,0:T(8,128)S(1)} %collective-permute-done.1.far, ...), custom_call_target="tpu_custom_call" | custom-call | flops 536870912 | bytes 6623240 | tf_op jit(solution)/shard_map/pallas_call | solution.py:390
  28.3 1.3 %shard_map.132.partial = f32[64,1024]{1,0:T(8,128)S(1)} custom-call(f32[2,64,1024]{2,1,0:T(8,128)S(1)} %get-tuple-element.72.flow, bf16[8,1024,128]{2,1,0:T(8,128)(2,1)S(1)} %get-tuple-element.63.eh, bf16[8,1024,128]{2,1,0:T(8,128)(2,1)S(1)} %get-tuple-element.64.el, bf16[8,1024,128]{2,1,0:T(8,128)(2,1)S(1)} %get-tuple-element.65.nh, ...), custom_call_target="tpu_custom_call" | custom-call | flops 1073741824 | bytes 9183232 | tf_op jit(solution)/shard_map/pallas_call | solution.py:390
  29.6 2.2 %collective-permute-done.5.far = f32[128,256]{1,0:T(8,128)S(1)} collective-permute-done((f32[128,256]{1,0:T(8,128)S(1)}, f32[128,256]{1,0:T(8,128)S(1)}, u32[]{:S(2)}, u32[]{:S(2)}) %collective-permute-start.5) | collective-permute-done | bytes 131104 | tf_op jit(solution)/shard_map/ppermute | solution.py:410
  31.8 2.9 %shard_map.134 = (f32[64,1024]{1,0:T(8,128)S(1)}, f32[72,384]{1,0:T(8,128)S(1)}, f32[72,384]{1,0:T(8,128)S(1)}) custom-call(s32[1]{0:T(128)} %bitcast.place, f32[64,1024]{1,0:T(8,128)S(1)} %get-tuple-element.62.level, f32[64,1024]{1,0:T(8,128)S(1)} %shard_map.132.partial, f32[1,1024]{1,0:T(1,128)S(1)} %get-tuple-element.54.depth, ...), custom_call_target="tpu_custom_call" | custom-call | flops 536870912 | bytes 11778052 | tf_op jit(solution)/shard_map/pallas_call | solution.py:390
  34.7 0.1 collective-permute-start.6
  34.8 1.4 %collective-permute-start.7 = (f32[72,384]{1,0:T(8,128)S(1)}, f32[72,384]{1,0:T(8,128)S(1)}, u32[]{:S(2)}, u32[]{:S(2)}) collective-permute-start(f32[72,384]{1,0:T(8,128)S(1)} %get-tuple-element.92), channel_id=1, source_target_pairs={{0,15},{1,2},{2,1},{3,4},{4,3},{5,6},{6,5},{7,8},{8,7},{9,10},{10,... | collective-permute-start | bytes 331784 | tf_op jit(solution)/shard_map/ppermute | solution.py:410
  36.1 2.0 %shard_map.135 = (f32[64,1024]{1,0:T(8,128)S(1)}, f32[64,1024]{1,0:T(8,128)S(1)}, f32[72,64]{1,0:T(8,128)S(1)}) custom-call(f32[64,1024]{1,0:T(8,128)S(1)} %get-tuple-element.87.level, bf16[8,1024,128]{2,1,0:T(8,128)(2,1)S(1)} %get-tuple-element.63.eh, bf16[8,1024,128]{2,1,0:T(8,128)(2,1)S(1)} %get-tuple-element.64.el, ...), custom_call_target="tpu_custom_call" | custom-call | flops 1073741824 | bytes 15509504 | tf_op jit(solution)/shard_map/pallas_call | solution.py:390
  38.2 0.0 collective-permute-done.6.near
  38.2 3.5 %collective-permute-done.7.far = f32[72,384]{1,0:T(8,128)S(1)} collective-permute-done((f32[72,384]{1,0:T(8,128)S(1)}, f32[72,384]{1,0:T(8,128)S(1)}, u32[]{:S(2)}, u32[]{:S(2)}) %collective-permute-start.7) | collective-permute-done | bytes 110624 | tf_op jit(solution)/shard_map/ppermute | solution.py:410
  41.7 4.8 %shard_map.136 = f32[3,64,1024]{2,1,0:T(8,128)} custom-call(f32[2,64,1024]{2,1,0:T(8,128)S(1)} %get-tuple-element.72.flow, f32[64,1024]{1,0:T(8,128)S(1)} %get-tuple-element.87.level, f32[64,1024]{1,0:T(8,128)S(1)} %get-tuple-element.88.east, f32[64,1024]{1,0:T(8,128)S(1)} %get-tuple-element.89.north, f32[72,64]{1,0:T(8,128)S(1)} %get-tuple-element.90.sums, ...), custom_call_target="tpu_custom_call" | custom-call | flops 536870912 | bytes 6531072 | tf_op jit(solution)/shard_map/pallas_call | solution.py:390
  (2 shorter events, 0.0 us)
Async XLA Ops:
  2.9 12.1 %collective-permute-start = (f32[136,256]{1,0:T(8,128)S(1)}, f32[136,256]{1,0:T(8,128)S(1)}, u32[]{:S(2)}, u32[]{:S(2)}) collective-permute-start(f32[136,256]{1,0:T(8,128)S(1)} %get-tuple-element.55), channel_id=1, source_target_pairs={{0,1},{1,0},{2,3},{3,2},{4,5},{5,4},{6,7},{7,6},{8,9},{9,8},{10,11... | collective-permute-start | bytes 417800 | tf_op jit(solution)/shard_map/ppermute | solution.py:411
  3.4 11.5 %collective-permute-start.1 = (f32[136,256]{1,0:T(8,128)S(1)}, f32[136,256]{1,0:T(8,128)S(1)}, u32[]{:S(2)}, u32[]{:S(2)}) collective-permute-start(f32[136,256]{1,0:T(8,128)S(1)} %get-tuple-element.56), channel_id=1, source_target_pairs={{0,15},{1,2},{2,1},{3,4},{4,3},{5,6},{6,5},{7,8},{8,7},{9,10},{10,... | collective-permute-start | bytes 417800 | tf_op jit(solution)/shard_map/ppermute | solution.py:410
  16.2 2.8 %collective-permute-start.2 = (f32[64,256]{1,0:T(8,128)S(1)}, f32[64,256]{1,0:T(8,128)S(1)}, u32[]{:S(2)}, u32[]{:S(2)}) collective-permute-start(f32[64,256]{1,0:T(8,128)S(1)} %get-tuple-element.70), channel_id=1, source_target_pairs={{0,1},{1,0},{2,3},{3,2},{4,5},{5,4},{6,7},{7,6},{8,9},{9,8},{10,11... | collective-permute-start | bytes 196616 | tf_op jit(solution)/shard_map/ppermute | solution.py:411
  16.3 6.5 %collective-permute-start.3 = (f32[64,256]{1,0:T(8,128)S(1)}, f32[64,256]{1,0:T(8,128)S(1)}, u32[]{:S(2)}, u32[]{:S(2)}) collective-permute-start(f32[64,256]{1,0:T(8,128)S(1)} %get-tuple-element.71), channel_id=1, source_target_pairs={{0,15},{1,2},{2,1},{3,4},{4,3},{5,6},{6,5},{7,8},{8,7},{9,10},{10,... | collective-permute-start | bytes 196616 | tf_op jit(solution)/shard_map/ppermute | solution.py:410
  24.6 5.0 %collective-permute-start.4 = (f32[128,256]{1,0:T(8,128)S(1)}, f32[128,256]{1,0:T(8,128)S(1)}, u32[]{:S(2)}, u32[]{:S(2)}) collective-permute-start(f32[128,256]{1,0:T(8,128)S(1)} %get-tuple-element.74), channel_id=1, source_target_pairs={{0,1},{1,0},{2,3},{3,2},{4,5},{5,4},{6,7},{7,6},{8,9},{9,8},{10,11... | collective-permute-start | bytes 393224 | tf_op jit(solution)/shard_map/ppermute | solution.py:411
  24.6 7.2 %collective-permute-start.5 = (f32[128,256]{1,0:T(8,128)S(1)}, f32[128,256]{1,0:T(8,128)S(1)}, u32[]{:S(2)}, u32[]{:S(2)}) collective-permute-start(f32[128,256]{1,0:T(8,128)S(1)} %get-tuple-element.75), channel_id=1, source_target_pairs={{0,15},{1,2},{2,1},{3,4},{4,3},{5,6},{6,5},{7,8},{8,7},{9,10},{10,... | collective-permute-start | bytes 393224 | tf_op jit(solution)/shard_map/ppermute | solution.py:410
  34.7 3.5 %collective-permute-start.6 = (f32[72,384]{1,0:T(8,128)S(1)}, f32[72,384]{1,0:T(8,128)S(1)}, u32[]{:S(2)}, u32[]{:S(2)}) collective-permute-start(f32[72,384]{1,0:T(8,128)S(1)} %get-tuple-element.91), channel_id=1, source_target_pairs={{0,1},{1,0},{2,3},{3,2},{4,5},{5,4},{6,7},{7,6},{8,9},{9,8},{10,11... | collective-permute-start | bytes 331784 | tf_op jit(solution)/shard_map/ppermute | solution.py:411
  34.8 6.9 %collective-permute-start.7 = (f32[72,384]{1,0:T(8,128)S(1)}, f32[72,384]{1,0:T(8,128)S(1)}, u32[]{:S(2)}, u32[]{:S(2)}) collective-permute-start(f32[72,384]{1,0:T(8,128)S(1)} %get-tuple-element.92), channel_id=1, source_target_pairs={{0,15},{1,2},{2,1},{3,4},{4,3},{5,6},{6,5},{7,8},{8,7},{9,10},{10,... | collective-permute-start | bytes 331784 | tf_op jit(solution)/shard_map/ppermute | solution.py:410

commit v3 on v2

--- a/solution.py
+++ b/solution.py
@@ -1,3 +1,4 @@
+import functools
 import math
 
 import jax
@@ -7,13 +8,11 @@
 from jax.experimental.pallas import tpu as pltpu
 from jax.sharding import PartitionSpec as P
 
-STEPS = 2
 DT = 0.1
 LANES = 128
 ROWS = 8
 F32 = jnp.float32
 BF16 = jnp.bfloat16
-TOPMOST = lax.Precision.HIGHEST
 
 
 def halves(value):
@@ -144,7 +143,7 @@
     far[2 * members :, :] = block
 
 
-def prepare_kernel(place, state, coef, wet, conn, eh, el, nh, nl, geh, gel, gnh, gnl, totals, partial):
+def prepare_kernel(place, coef, wet, conn, eh, el, nh, nl, geh, gel, gnh, gnl, totals):
     slots, nodes = conn.shape
     ghosts = geh.shape[1]
     turned = (1 - (place[0] & 1)) * (ghosts // 2)
@@ -163,12 +162,6 @@
         weights = merged(targets, weights)
         build_operator(targets, weights, (eh, el, nh, nl), 0, nodes, column // LANES)
         build_operator(targets, weights, (geh, gel, gnh, gnl), nodes, ghosts, column // LANES)
-    partial[...] = (
-        product(stacked(state[1]), eh, el)
-        + product(stacked(state[2]), nh, nl)
-        - state[1] * totals[0:1, :]
-        - state[2] * totals[1:2, :]
-    )
 
 
 def ghost_flow(near, far, part, members):
@@ -176,7 +169,7 @@
     return jnp.concatenate([near[rows, :], far[rows, :]], axis=1)
 
 
-def level_kernel(place, held, partial, depth, near, far, geh, gel, gnh, gnl, lists, new_level, to_near, to_far):
+def stepped_level(held, partial, depth, near, far, geh, gel, gnh, gnl):
     level = held.at[0] if len(held.shape) == 3 else held
     members = level.shape[0]
     divergence = (
@@ -184,8 +177,33 @@
         + product(stacked(ghost_flow(near, far, 0, members)), geh, gel)
         + product(stacked(ghost_flow(near, far, 1, members)), gnh, gnl)
     )
-    new_level[...] = level[...] - DT * depth[...] * divergence
+    return level[...] - DT * depth[...] * divergence
+
+
+def level_kernel(place, held, partial, depth, near, far, geh, gel, gnh, gnl, lists, new_level, to_near, to_far):
+    new_level[...] = stepped_level(held, partial, depth, near, far, geh, gel, gnh, gnl)
     pick_lanes(new_level, chosen_lists(place, lists), [(to_near, 0, 0), (to_far, 0, 0)])
+
+
+def thirds(value):
+    high, rest = halves(value)
+    middle = rest
+    low = (value - high.astype(F32) - middle.astype(F32)).astype(BF16)
+    return high, middle, low
+
+
+def row_products(left, right):
+    rows = left.shape[0]
+    ours, theirs = thirds(left), thirds(right)
+    total = 0.0
+    for skip, part in enumerate(theirs):
+        block = jnp.concatenate(ours[: 3 - skip], axis=0)
+        found = lax.dot_general(block, part, (((1,), (1,)), ((), ())), preferred_element_type=F32)
+        sums = [found[at * rows : (at + 1) * rows] for at in range(3 - skip)]
+        while len(sums) > 1:
+            sums[-2:] = [sums[-2] + sums[-1]]
+        total = sums[0] + total
+    return total
 
 
 def list_sums(seen, value, weight):
@@ -193,21 +211,28 @@
     anomalies = seen - obs_mean
     pull = jnp.broadcast_to(weight * (value - obs_mean), (ROWS, seen.shape[1]))
     left = jnp.concatenate([anomalies * weight, pull], axis=0)
-    return lax.dot_general(left, anomalies, (((1,), (1,)), ((), ())), precision=TOPMOST, preferred_element_type=F32)
+    return row_products(left, anomalies)
+
+
+def neighbour_payload(which, place, level, lists, high, low, tables, ref):
+    members, width = level.shape[0], lists.shape[1]
+    tiles = high.shape[0] // 2
+    pick_lanes(level, [chosen_lists(place, lists)[which]], [(ref, 0, 0)])
+    seen = product(stacked(level[...]), high, low, which * tiles, tiles)
+    sums = list_sums(seen, tables[2 * which : 2 * which + 1, :], tables[2 * which + 1 : 2 * which + 2, :])
+    ref[members:, :width] = jnp.zeros((ROWS, width), F32)
+    ref[:, width:] = jnp.concatenate([sums, jnp.zeros((members + ROWS, LANES - members), F32)], axis=1)
 
 
 def last_level_kernel(
-    place, level, partial, depth, near, far, geh, gel, gnh, gnl, lists, high, low, tables, new_level, to_near, to_far
+    place, held, partial, depth, near, far, geh, gel, gnh, gnl, lists, high, low, tables, new_level, to_far
 ):
-    members, width = new_level.shape[0], lists.shape[1]
-    level_kernel(place, level, partial, depth, near, far, geh, gel, gnh, gnl, lists, new_level, to_near, to_far)
-    tiles = high.shape[0] // 3
-    stack = stacked(new_level[...])
-    for which, ref in enumerate((to_near, to_far)):
-        seen = product(stack, high, low, which * tiles, tiles)
-        sums = list_sums(seen, tables[2 * which : 2 * which + 1, :], tables[2 * which + 1 : 2 * which + 2, :])
-        ref[members:, :width] = jnp.zeros((ROWS, width), F32)
-        ref[:, width:] = jnp.concatenate([sums, jnp.zeros((members + ROWS, LANES - members), F32)], axis=1)
+    new_level[...] = stepped_level(held, partial, depth, near, far, geh, gel, gnh, gnl)
+    neighbour_payload(1, place, new_level, lists, high, low, tables, to_far)
+
+
+def near_sums_kernel(place, level, lists, high, low, tables, to_near):
+    neighbour_payload(0, place, level, lists, high, low, tables, to_near)
 
 
 def slope_kernel(level, eh, el, nh, nl, totals, east, north):
@@ -217,8 +242,8 @@
 
 
 def sampling_kernel(
-    place, length, near, far, ids, weight, obs_nodes, obs_weight, obs_value, obs_error, high, low, tables,
-    numbers, strengths, scratch, found,
+    place, length, near, far, ids, weight, obs_nodes, obs_weight, obs_value, obs_error, high, low, tables, found,
+    numbers, strengths, scratch,
 ):
     entries, width = ids.shape[1], near.shape[1]
     corners, obs_count = obs_nodes.shape
@@ -250,17 +275,26 @@
         [(found, 0, (owner * tiles + tile) * LANES) for owner, tile in places],
     )
     for owner, tile in places:
-        at = owner * tiles + tile
+        at = slice((owner * tiles + tile) * LANES, (owner * tiles + tile + 1) * LANES)
         own = kept[owner, tile][0]
-        here = found[:, at * LANES : (at + 1) * LANES]
+        cut = slice(tile * LANES, (tile + 1) * LANES)
+        found[corners : 2 * corners, at] = jnp.where(own, found[corners : 2 * corners, at], 0.0)
+        force = found[2 * corners + 1 : 2 * corners + 2, at] * strengths[owner : owner + 1, cut]
+        tables[2 * owner : 2 * owner + 1, cut] = found[2 * corners : 2 * corners + 1, at]
+        tables[2 * owner + 1 : 2 * owner + 2, cut] = jnp.where(own, force, 0.0)
+    corner_operator(found, 2 * tiles, corners, high, low)
+
+
+def corner_operator(found, first, corners, high, low):
+    for tile in range(high.shape[0]):
+        here = found[:, (first + tile) * LANES : (first + tile + 1) * LANES]
         targets = [here[c : c + 1, :].astype(jnp.int32) for c in range(corners)]
-        shares = [jnp.where(own, here[corners + c : corners + c + 1, :], 0.0) for c in range(corners)]
-        shares = merged(targets, [shares])
-        build_operator(targets, shares, (high, low), 0, high.shape[1], at)
-        cut = slice(tile * LANES, (tile + 1) * LANES)
-        force = here[2 * corners + 1 : 2 * corners + 2, :] * strengths[owner : owner + 1, cut]
-        tables[2 * owner : 2 * owner + 1, cut] = here[2 * corners : 2 * corners + 1, :]
-        tables[2 * owner + 1 : 2 * owner + 2, cut] = jnp.where(own, force, 0.0)
+        shares = [here[corners + c : corners + c + 1, :] for c in range(corners)]
+        build_operator(targets, merged(targets, [shares]), (high, low), 0, high.shape[1], tile)
+
+
+def others_kernel(corners, found, high, low):
+    corner_operator(found, 0, corners, high, low)
 
 
 def flow_kernel(place, flow, east, north, near, far, geh, gel, gnh, gnl, lists, new_flow, to_near, to_far):
@@ -275,19 +309,18 @@
 
 
 def divergence_kernel(flow, eh, el, nh, nl, totals, partial):
+    first = flow.shape[0] - 2
+    east, north = flow[first], flow[first + 1]
     partial[...] = (
-        product(stacked(flow[0]), eh, el)
-        + product(stacked(flow[1]), nh, nl)
-        - flow[0] * totals[0:1, :]
-        - flow[1] * totals[1:2, :]
-    )
-
-
-def last_slope_kernel(level, eh, el, nh, nl, totals, high, low, tables, east, north, sums):
-    slope_kernel(level, eh, el, nh, nl, totals, east, north)
-    tiles = high.shape[0] // 3
-    seen = product(stacked(level[...]), high, low, 2 * tiles, tiles)
-    sums[...] = list_sums(seen, tables[4:5, :], tables[5:6, :])
+        product(stacked(east), eh, el)
+        + product(stacked(north), nh, nl)
+        - east * totals[0:1, :]
+        - north * totals[1:2, :]
+    )
+
+
+def own_sums_kernel(level, high, low, tables, sums):
+    sums[...] = list_sums(product(stacked(level[...]), high, low), tables[4:5, :], tables[5:6, :])
 
 
 def pair_inverse(a, b, c):
@@ -300,7 +333,7 @@
     return first * lax.rsqrt(a), (second - m * first) * lax.rsqrt(c - m * b)
 
 
-def inverse_factor(gram):
+def inverse_factor(gram, beside):
     size = gram.shape[0]
     wide = (ROWS, 2 * size)
     row = lax.broadcasted_iota(jnp.int32, (size, size), 0)
@@ -351,32 +384,56 @@
                 if place == home:
                     change = jnp.where(inner >= spot + 4, change, 0.0)
                 blocks[place] = blocks[place] - change
+            beside()
         done.append(result)
     return jnp.concatenate(done, axis=0)[:, size:]
 
 
-def analysis_kernel(flow, level, east, north, sums, near, far, geh, gel, gnh, gnl, out, fields):
-    members = level.shape[0]
+def analysis_kernel(
+    flow, level, east, north, sums, near, far, geh, gel, gnh, gnl, out, result, moved, averages, sent
+):
+    members, nodes = level.shape
     width = near.shape[1] - LANES
     total = sums[...] + near[:, width : width + members] + far[:, width : width + members]
     row = lax.broadcasted_iota(jnp.int32, (members, members), 0)
     col = lax.broadcasted_iota(jnp.int32, (members, members), 1)
     gram = total[:members] + jnp.where(row == col, members - 1.0, 0.0)
     rhs = total[members : members + 1]
-    inverse = inverse_factor(gram)
     stack = stacked(jnp.concatenate([near[:members, :width], far[:members, :width]], axis=1))
-    fields[0] = level[...]
-    fields[1] = flow[0] - DT * (east[...] + product(stack, geh, gel))
-    fields[2] = flow[1] - DT * (north[...] + product(stack, gnh, gnl))
+    operators = ((geh, gel), (gnh, gnl))
+
+    def piece(part, tile):
+        cut = slice(tile * LANES, (tile + 2) * LANES)
+        if part == 0:
+            field = level[:, cut]
+        else:
+            slope = (east, north)[part - 1][:, cut] + product(stack, *operators[part - 1], tile, 2)
+            field = flow[part - 1, :, cut] - DT * slope
+        average = jnp.mean(field, axis=0, keepdims=True)
+        moved[part, :, cut] = stacked(field - average)
+        averages[part : part + 1, cut] = average
+
+    pieces = [(part, tile) for part in (1, 2, 0) for tile in range(0, nodes // LANES, 2)]
+
+    def beside():
+        if pieces:
+            piece(*pieces.pop(0))
+
+    inverse = inverse_factor(gram, beside)
+    while pieces:
+        beside()
     halfway = jnp.sum(inverse * rhs, axis=1, keepdims=True)
     mean_w = jnp.sum(inverse * halfway, axis=0, keepdims=True)
-    blend = stacked(math.sqrt(members - 1.0) * inverse + mean_w)
+    blend = math.sqrt(members - 1.0) * inverse + mean_w
+    blend = stacked(jnp.concatenate([blend, blend], axis=1))
+    copies = []
     for part in range(3):
-        field = fields[part]
-        average = jnp.mean(field, axis=0, keepdims=True)
-        high, low = halves(field - average)
-        moved = jnp.dot(blend, high, preferred_element_type=F32) + jnp.dot(blend, low, preferred_element_type=F32)
-        out[part] = average + moved[:members] + moved[members:]
+        change = jnp.dot(blend, moved[part], preferred_element_type=F32)
+        result[part] = averages[part : part + 1, :] + (change[:members] + change[members:])
+        copies.append(pltpu.make_async_copy(result.at[part], out.at[part], sent.at[part]))
+        copies[-1].start()
+    for copy in copies:
+        copy.wait()
 
 
 def call(kernel, outs, args, scalars=0, scratch=(), flops=0, final=False, limit=16, raw=False):
@@ -391,7 +448,7 @@
         kernel,
         out_shape=outs,
         in_specs=in_specs,
-        out_specs=[vmem] * len(outs),
+        out_specs=[pl.BlockSpec(memory_space=pltpu.HBM) if final else vmem] * len(outs),
         scratch_shapes=scratch,
         compiler_params=pltpu.CompilerParams(vmem_limit_bytes=limit << 20),
         cost_estimate=pl.CostEstimate(flops=flops, bytes_accessed=held, transcendentals=0),
@@ -402,14 +459,15 @@
     return jax.ShapeDtypeStruct(dims, dtype)
 
 
-def exchange(to_near, to_far):
+def to_partner(value):
+    pairs = [(i, i ^ 1) for i in range(lax.axis_size("mesh"))]
+    return lax.ppermute(value, "mesh", pairs)
+
+
+def to_other(value):
     count = lax.axis_size("mesh")
-    pairs = [(i, i ^ 1) for i in range(count)]
-    others = [(i, (((i + 1) % count) ^ 1) - 1) for i in range(count)]
-    others = [(source, target % count) for source, target in others]
-    from_far = lax.ppermute(to_far, "mesh", others)
-    from_near = lax.ppermute(to_near, "mesh", pairs)
-    return from_near, from_far
+    others = [(i, ((i + 1) ^ 1) - 1) for i in range(1, count - 1)]
+    return lax.ppermute(value, "mesh", others)
 
 
 def local(
@@ -447,66 +505,75 @@
         scratch=[pltpu.SemaphoreType.DMA((len(brought) + 2,))],
         raw=True,
     )
-    sent = [near, far]
     state, send_list, loc_ids, loc_weight, depth, coef, wet_faces, conn = brought[:8]
     obs_nodes, obs_weight, obs_value, obs_error = brought[8:]
-    from_near, from_far = exchange(*sent)
+    corners = obs_nodes.shape[0]
+    from_far = to_other(far)
+    from_near = to_partner(near)
     big = [shape(tiles, nodes, LANES, dtype=BF16)] * 4
     small = [shape(tiles, ghosts, LANES, dtype=BF16)] * 4
     made = call(
-        prepare_kernel,
-        big + small + [shape(2, nodes), shape(members, nodes)],
-        [place, state, coef, wet_faces, conn],
+        prepare_kernel, big + small + [shape(2, nodes)], [place, coef, wet_faces, conn], scalars=1, flops=2 * work
+    )
+    operators, ghost_operators, totals = made[:4], made[4:8], made[8]
+    field, payload = shape(members, nodes), shape(members, width)
+    (partial,) = call(divergence_kernel, [field], [state, *operators, totals], flops=work)
+    early = from_near, from_far
+
+    args = [place, state, partial, depth, from_near, from_far, *ghost_operators, send_list]
+    level, near, far = call(level_kernel, [field, payload, payload], args, scalars=1, flops=work)
+    from_far = to_other(far)
+    from_near = to_partner(near)
+    east, north = call(slope_kernel, [field] * 2, [level, *operators, totals], flops=work)
+    entry_tiles = entries // LANES
+    own_high, own_low, tables, found = call(
+        sampling_kernel,
+        [shape(entry_tiles, nodes, LANES, dtype=BF16)] * 2 + [shape(ROWS, entries), shape(ROWS, 3 * entries)],
+        [place, loc_len, *early, loc_ids, loc_weight, obs_nodes, obs_weight, obs_value, obs_error],
+        scalars=2,
+        scratch=[
+            pltpu.VMEM((ROWS, entries), jnp.int32),
+            pltpu.VMEM((ROWS, entries), F32),
+            pltpu.VMEM((ROWS, obs_nodes.shape[1]), F32),
+        ],
+        flops=work,
+    )
+
+    flow, near, far = call(
+        flow_kernel,
+        [shape(2, members, nodes)] + [shape(2 * members, width)] * 2,
+        [place, state, east, north, from_near, from_far, *ghost_operators, send_list],
         scalars=1,
-        flops=4 * work,
-    )
-    operators, ghost_operators, totals, partial = made[:4], made[4:8], made[8], made[9]
-    level = flow = state
-    early = from_near, from_far
-    for step in range(STEPS):
-        last = step == STEPS - 1
-        args = [place, level, partial, depth, from_near, from_far, *ghost_operators, send_list]
-        kernel, extra, payload = level_kernel, [], shape(members, width)
-        if last:
-            kernel, extra, payload = last_level_kernel, list(sampling), shape(members + ROWS, width + LANES)
-        level, *sent = call(kernel, [shape(members, nodes), payload, payload], args + extra, scalars=1, flops=work)
-        from_near, from_far = exchange(*sent)
-        slopes = [shape(members, nodes)] * 2
-        args = [level, *operators, totals]
-        if last:
-            east, north, sums = call(
-                last_slope_kernel, slopes + [shape(members + ROWS, members)], args + list(sampling), flops=2 * work
-            )
-            break
-        east, north = call(slope_kernel, slopes, args, flops=2 * work)
-        flow, *sent = call(
-            flow_kernel,
-            [shape(2, members, nodes)] + [shape(2 * members, width)] * 2,
-            [place, flow, east, north, from_near, from_far, *ghost_operators, send_list],
-            scalars=1,
-            flops=work,
-        )
-        early, sent[0] = lax.optimization_barrier((early, sent[0]))
-        from_near, from_far = exchange(*sent)
-        (partial,) = call(divergence_kernel, [shape(members, nodes)], [flow, *operators, totals], flops=2 * work)
-        sampling = call(
-            sampling_kernel,
-            [shape(3 * entries // LANES, nodes, LANES, dtype=BF16)] * 2 + [shape(ROWS, entries)],
-            [place, loc_len, *early, loc_ids, loc_weight, obs_nodes, obs_weight, obs_value, obs_error],
-            scalars=2,
-            scratch=[
-                pltpu.VMEM((ROWS, entries), jnp.int32),
-                pltpu.VMEM((ROWS, entries), F32),
-                pltpu.VMEM((ROWS, obs_nodes.shape[1]), F32),
-                pltpu.VMEM((ROWS, 3 * entries), F32),
-            ],
-            flops=work,
-        )
+        flops=work,
+    )
+    from_far = to_other(far)
+    from_near = to_partner(near)
+    high, low = call(
+        functools.partial(others_kernel, corners),
+        [shape(2 * entry_tiles, nodes, LANES, dtype=BF16)] * 2,
+        [found],
+        flops=work,
+    )
+    (partial,) = call(divergence_kernel, [field], [flow, *operators, totals], flops=work)
+
+    payload = shape(members + ROWS, width + LANES)
+    args = [place, level, partial, depth, from_near, from_far, *ghost_operators, send_list, high, low, tables]
+    level, far = call(last_level_kernel, [field, payload], args, scalars=1, flops=work)
+    from_far = to_other(far)
+    (near,) = call(near_sums_kernel, [payload], [place, level, send_list, high, low, tables], scalars=1, flops=work)
+    from_near = to_partner(near)
+    east, north = call(slope_kernel, [field] * 2, [level, *operators, totals], flops=work)
+    (sums,) = call(own_sums_kernel, [shape(members + ROWS, members)], [level, own_high, own_low, tables], flops=work)
     (out,) = call(
         analysis_kernel,
         [shape(3, members, nodes)],
         [flow, level, east, north, sums, from_near, from_far, *ghost_operators],
-        scratch=[pltpu.VMEM((3, members, nodes), F32)],
+        scratch=[
+            pltpu.VMEM((3, members, nodes), F32),
+            pltpu.VMEM((3, 2 * members, nodes), BF16),
+            pltpu.VMEM((ROWS, nodes), F32),
+            pltpu.SemaphoreType.DMA((3,)),
+        ],
         flops=work,
         final=True,
     )

time: 46.7 us -> 45.5 us (0.974)
  the two profiles are of different devices: /device:TPU:0 before, /device:TPU:9 now
where the time goes in v3:
time: 45.5 us; the launch traced here: 45.3 us
  Pallas kernels  25.3 us (56%)
  starting transfers between devices  14 us (31%)
  waiting for transfers between devices  5.01 us (11%)
  between operations  0.98 us (2%)
    pallas_call x14, Pallas kernels, call(): pl.pallas_call(kernel, out_shape=outs, in_specs=in_specs, out_specs=[pl.B...  25.3 us
    ppermute x4, starting transfers between devices, to_other(): return lax.ppermute(value, 'mesh', others)  12.3 us
    ppermute x4, waiting for transfers between devices, to_other(): return lax.ppermute(value, 'mesh', others)  5 us
    ppermute x4, starting transfers between devices, to_partner(): return lax.ppermute(value, 'mesh', pairs)  1.75 us
  transfers between devices with their start and end apart: 8, of which 3 were waited for; matrix products, arithmetic and copies ran while one was open for 0% of the time, Pallas kernels for 28%

profile of v3, /device:TPU:9, one launch (start us, length us, event | category | flops | bytes accessed | tf_op | source)
XLA Modules:
  0.0 45.3 jit_solution(5999027345564937724)
XLA Ops:
  0.7 2.2 %shard_map.127 = (f32[136,256]{1,0:T(8,128)S(1)}, f32[136,256]{1,0:T(8,128)S(1)}, f32[3,64,1024]{2,1,0:T(8,128)S(1)}, s32[2,256]{1,0:T(2,128)S(1)}, s32[1,512]{1...) custom-call(s32[1]{0:T(128)} %bitcast.place, ...), custom_call_target="tpu_custom_call" | custom-call | bytes 2134024 | tf_op jit(solution)/shard_map/pallas_call | solution.py:447
  2.9 0.7 %collective-permute-start = (f32[136,256]{1,0:T(8,128)S(1)}, f32[136,256]{1,0:T(8,128)S(1)}, u32[]{:S(2)}, u32[]{:S(2)}) collective-permute-start(f32[136,256]{1,0:T(8,128)S(1)} %get-tuple-element.56), channel_id=1, source_target_pairs={{0,1},{1,0},{2,3},{3,2},{4,5},{5,4},{6,7},{7,6},{8,9},{9,8},{10,11... | collective-permute-start | bytes 417800 | tf_op jit(solution)/shard_map/ppermute | solution.py:464
  3.6 3.0 %collective-permute-start.1 = (f32[136,256]{1,0:T(8,128)S(1)}, f32[136,256]{1,0:T(8,128)S(1)}, u32[]{:S(2)}, u32[]{:S(2)}) collective-permute-start(f32[136,256]{1,0:T(8,128)S(1)} %get-tuple-element.57), channel_id=1, source_target_pairs={{1,2},{2,1},{3,4},{4,3},{5,6},{6,5},{7,8},{8,7},{9,10},{10,9},{11,... | collective-permute-start | bytes 417800 | tf_op jit(solution)/shard_map/ppermute | solution.py:470
  6.7 4.6 %shard_map.128 = (bf16[8,1024,128]{2,1,0:T(8,128)(2,1)S(1)}, bf16[8,1024,128]{2,1,0:T(8,128)(2,1)S(1)}, bf16[8,1024,128]{2,1,0:T(8,128)(2,1)S(1)}, bf16[8,1024,1...) custom-call(s32[1]{0:T(128)} %bitcast.place, ...), custom_call_target="tpu_custom_call" | custom-call | flops 1073741824 | bytes 12689412 | tf_op jit(solution)/shard_map/pallas_call | solution.py:447
  11.3 1.3 %shard_map.129.partial = f32[64,1024]{1,0:T(8,128)S(1)} custom-call(f32[3,64,1024]{2,1,0:T(8,128)S(1)} %get-tuple-element.46.flow.held, bf16[8,1024,128]{2,1,0:T(8,128)(2,1)S(1)} %get-tuple-element.50.eh, bf16[8,1024,128]{2,1,0:T(8,128)(2,1)S(1)} %get-tuple-element.51.el, bf16[8,1024,128]{2,1,0:T(8,128)(2,1)S(1)} %get-tuple-element.52.nh, ...), custom_call_target="tpu_custom_call" | custom-call | flops 536870912 | bytes 9445376 | tf_op jit(solution)/shard_map/pallas_call | solution.py:447
  12.6 1.3 %shard_map.130 = (f32[64,1024]{1,0:T(8,128)S(1)}, f32[64,256]{1,0:T(8,128)S(1)}, f32[64,256]{1,0:T(8,128)S(1)}) custom-call(s32[1]{0:T(128)} %bitcast.place, f32[3,64,1024]{2,1,0:T(8,128)S(1)} %get-tuple-element.46.flow.held, f32[64,1024]{1,0:T(8,128)S(1)} %shard_map.129.partial, f32[1,1024]{1,0:T(1,128)S(1)} %get-tuple-element.55.depth, ...), custom_call_target="tpu_custom_call" | custom-call | flops 536870912 | bytes 5920772 | tf_op jit(solution)/shard_map/pallas_call | solution.py:447
  13.9 0.4 collective-permute-start.2
  14.3 3.2 %collective-permute-start.3 = (f32[64,256]{1,0:T(8,128)S(1)}, f32[64,256]{1,0:T(8,128)S(1)}, u32[]{:S(2)}, u32[]{:S(2)}) collective-permute-start(f32[64,256]{1,0:T(8,128)S(1)} %get-tuple-element.67), channel_id=1, source_target_pairs={{1,2},{2,1},{3,4},{4,3},{5,6},{6,5},{7,8},{8,7},{9,10},{10,9},{11,... | collective-permute-start | bytes 196616 | tf_op jit(solution)/shard_map/ppermute | solution.py:470
  17.5 1.3 %shard_map.131 = (f32[64,1024]{1,0:T(8,128)S(1)}, f32[64,1024]{1,0:T(8,128)S(1)}) custom-call(f32[64,1024]{1,0:T(8,128)S(1)} %get-tuple-element.63.level.held, bf16[8,1024,128]{2,1,0:T(8,128)(2,1)S(1)} %get-tuple-element.50.eh, bf16[8,1024,128]{2,1,0:T(8,128)(2,1)S(1)} %get-tuple-element.51.el, bf16[8,1024,128]{2,1,0:T(8,128)(2,1)S(1)} %get-tuple-element.52.nh, ...), custom_call_target="tpu_custom_call" | custom-call | flops 536870912 | bytes 9183232 | tf_op jit(solution)/shard_map/pallas_call | solution.py:447
  18.8 1.8 %collective-permute-done.3.far = f32[64,256]{1,0:T(8,128)S(1)} collective-permute-done((f32[64,256]{1,0:T(8,128)S(1)}, f32[64,256]{1,0:T(8,128)S(1)}, u32[]{:S(2)}, u32[]{:S(2)}) %collective-permute-start.3) | collective-permute-done | bytes 65568 | tf_op jit(solution)/shard_map/ppermute | solution.py:470
  20.6 1.8 %shard_map.132 = (f32[2,64,1024]{2,1,0:T(8,128)S(1)}, f32[128,256]{1,0:T(8,128)S(1)}, f32[128,256]{1,0:T(8,128)S(1)}) custom-call(s32[1]{0:T(128)} %bitcast.place, f32[3,64,1024]{2,1,0:T(8,128)S(1)} %get-tuple-element.46.flow.held, f32[64,1024]{1,0:T(8,128)S(1)} %get-tuple-element.64.east, f32[64,1024]{1,0:T(8,128)S(1)} %get-tuple-element.65.north, ...), custom_call_target="tpu_custom_call" | custom-call | flops 536870912 | bytes 6424580 | tf_op jit(solution)/shard_map/pallas_call | solution.py:447
  22.4 0.5 %collective-permute-start.4 = (f32[128,256]{1,0:T(8,128)S(1)}, f32[128,256]{1,0:T(8,128)S(1)}, u32[]{:S(2)}, u32[]{:S(2)}) collective-permute-start(f32[128,256]{1,0:T(8,128)S(1)} %get-tuple-element.69), channel_id=1, source_target_pairs={{0,1},{1,0},{2,3},{3,2},{4,5},{5,4},{6,7},{7,6},{8,9},{9,8},{10,11... | collective-permute-start | bytes 393224 | tf_op jit(solution)/shard_map/ppermute | solution.py:464
  22.9 2.9 %collective-permute-start.5 = (f32[128,256]{1,0:T(8,128)S(1)}, f32[128,256]{1,0:T(8,128)S(1)}, u32[]{:S(2)}, u32[]{:S(2)}) collective-permute-start(f32[128,256]{1,0:T(8,128)S(1)} %get-tuple-element.70), channel_id=1, source_target_pairs={{1,2},{2,1},{3,4},{4,3},{5,6},{6,5},{7,8},{8,7},{9,10},{10,9},{11,... | collective-permute-start | bytes 393224 | tf_op jit(solution)/shard_map/ppermute | solution.py:470
  25.8 0.9 %shard_map.134 = (bf16[4,1024,128]{2,1,0:T(8,128)(2,1)S(1)}, bf16[4,1024,128]{2,1,0:T(8,128)(2,1)S(1)}, f32[8,512]{1,0:T(8,128)S(1)}, f32[8,1536]{1,0:T(8,128)S(1)}) custom-call(s32[1]{0:T(128)} %bitcast.place, s32[1]{0:T(128)S(6)} %copy.14.length, f32[136,256]{1,0:T(8,128)S(1)} %collective-permute-done.near, f32[136,256]{1,0:T(8,128)S(1)} %collective-permute-done.1.far, ...), custom_call_target="tpu_custom_call" | custom-call | flops 536870912 | bytes 2478088 | tf_op jit(solution)/shard_map/pallas_call | solution.py:447
  26.8 1.4 %shard_map.135 = (bf16[8,1024,128]{2,1,0:T(8,128)(2,1)S(1)}, bf16[8,1024,128]{2,1,0:T(8,128)(2,1)S(1)}) custom-call(f32[8,1536]{1,0:T(8,128)S(1)} %get-tuple-element.77.found), custom_call_target="tpu_custom_call" | custom-call | flops 536870912 | bytes 4243456 | tf_op jit(solution)/shard_map/pallas_call | solution.py:447
  28.2 1.3 %shard_map.133.partial = f32[64,1024]{1,0:T(8,128)S(1)} custom-call(f32[2,64,1024]{2,1,0:T(8,128)S(1)} %get-tuple-element.68.flow, bf16[8,1024,128]{2,1,0:T(8,128)(2,1)S(1)} %get-tuple-element.50.eh, bf16[8,1024,128]{2,1,0:T(8,128)(2,1)S(1)} %get-tuple-element.51.el, bf16[8,1024,128]{2,1,0:T(8,128)(2,1)S(1)} %get-tuple-element.52.nh, ...), custom_call_target="tpu_custom_call" | custom-call | flops 536870912 | bytes 9183232 | tf_op jit(solution)/shard_map/pallas_call | solution.py:447
  29.5 1.1 %collective-permute-done.5.far = f32[128,256]{1,0:T(8,128)S(1)} collective-permute-done((f32[128,256]{1,0:T(8,128)S(1)}, f32[128,256]{1,0:T(8,128)S(1)}, u32[]{:S(2)}, u32[]{:S(2)}) %collective-permute-start.5) | collective-permute-done | bytes 131104 | tf_op jit(solution)/shard_map/ppermute | solution.py:470
  30.6 1.7 %shard_map.136 = (f32[64,1024]{1,0:T(8,128)S(1)}, f32[72,384]{1,0:T(8,128)S(1)}) custom-call(s32[1]{0:T(128)} %bitcast.place, f32[64,1024]{1,0:T(8,128)S(1)} %get-tuple-element.63.level.held, f32[64,1024]{1,0:T(8,128)S(1)} %shard_map.133.partial, f32[1,1024]{1,0:T(1,128)S(1)} %get-tuple-element.55.depth, f32[128,256]{1,0:T(8,128)S(1)} %collective-permute-done.4.near, ...), custom_call_target="tpu_custom_call" | custom-call | flops 536870912 | bytes 9570308 | tf_op jit(solution)/shard_map/pallas_call | solution.py:447
  32.3 1.0 %shard_map.139 = f32[72,384]{1,0:T(8,128)S(1)} custom-call(s32[1]{0:T(128)} %bitcast.place, f32[64,1024]{1,0:T(8,128)S(1)} %get-tuple-element.81.level, s32[2,256]{1,0:T(2,128)S(1)} %get-tuple-element.62.lists, bf16[8,1024,128]{2,1,0:T(8,128)(2,1)S(1)} %get-tuple-element.78.high, bf16[8,1024,128]{2,1,0:T(8,128)(2,1)S(1)} %get-tuple-element.79.low, ...), custom_call_target="tpu_custom_call" | custom-call | flops 536870912 | bytes 4585476 | tf_op jit(solution)/shard_map/pallas_call | solution.py:447
  33.4 3.1 %collective-permute-start.7 = (f32[72,384]{1,0:T(8,128)S(1)}, f32[72,384]{1,0:T(8,128)S(1)}, u32[]{:S(2)}, u32[]{:S(2)}) collective-permute-start(f32[72,384]{1,0:T(8,128)S(1)} %get-tuple-element.86), channel_id=1, source_target_pairs={{1,2},{2,1},{3,4},{4,3},{5,6},{6,5},{7,8},{8,7},{9,10},{10,9},{11,... | collective-permute-start | bytes 331784 | tf_op jit(solution)/shard_map/ppermute | solution.py:470
  36.6 1.3 %shard_map.137 = (f32[64,1024]{1,0:T(8,128)S(1)}, f32[64,1024]{1,0:T(8,128)S(1)}) custom-call(f32[64,1024]{1,0:T(8,128)S(1)} %get-tuple-element.81.level, bf16[8,1024,128]{2,1,0:T(8,128)(2,1)S(1)} %get-tuple-element.50.eh, bf16[8,1024,128]{2,1,0:T(8,128)(2,1)S(1)} %get-tuple-element.51.el, bf16[8,1024,128]{2,1,0:T(8,128)(2,1)S(1)} %get-tuple-element.52.nh, ...), custom_call_target="tpu_custom_call" | custom-call | flops 536870912 | bytes 9183232 | tf_op jit(solution)/shard_map/pallas_call | solution.py:447
  37.8 0.7 %shard_map.138.sums = f32[72,64]{1,0:T(8,128)S(1)} custom-call(f32[64,1024]{1,0:T(8,128)S(1)} %get-tuple-element.81.level, bf16[4,1024,128]{2,1,0:T(8,128)(2,1)S(1)} %get-tuple-element.84.high, bf16[4,1024,128]{2,1,0:T(8,128)(2,1)S(1)} %get-tuple-element.85.low, f32[8,512]{1,0:T(8,128)S(1)} %get-tuple-element.80.tables), custom_call_target="tpu_custom_call" | custom-call | flops 536870912 | bytes 2394112 | tf_op jit(solution)/shard_map/pallas_call | solution.py:447
  38.6 2.1 %collective-permute-done.7.far = f32[72,384]{1,0:T(8,128)S(1)} collective-permute-done((f32[72,384]{1,0:T(8,128)S(1)}, f32[72,384]{1,0:T(8,128)S(1)}, u32[]{:S(2)}, u32[]{:S(2)}) %collective-permute-start.7) | collective-permute-done | bytes 110624 | tf_op jit(solution)/shard_map/ppermute | solution.py:470
  40.7 4.5 %shard_map.140 = f32[3,64,1024]{2,1,0:T(8,128)} custom-call(f32[2,64,1024]{2,1,0:T(8,128)S(1)} %get-tuple-element.68.flow, f32[64,1024]{1,0:T(8,128)S(1)} %get-tuple-element.81.level, f32[64,1024]{1,0:T(8,128)S(1)} %get-tuple-element.82.east, f32[64,1024]{1,0:T(8,128)S(1)} %get-tuple-element.83.north, f32[72,64]{1,0:T(8,128)S(1)} %shard_map.138.sums, ...), custom_call_target="tpu_custom_call" | custom-call | flops 536870912 | bytes 6531072 | tf_op jit(solution)/shard_map/pallas_call | solution.py:447
  (6 shorter events, 0.1 us)
Async XLA Ops:
  2.9 9.7 %collective-permute-start = (f32[136,256]{1,0:T(8,128)S(1)}, f32[136,256]{1,0:T(8,128)S(1)}, u32[]{:S(2)}, u32[]{:S(2)}) collective-permute-start(f32[136,256]{1,0:T(8,128)S(1)} %get-tuple-element.56), channel_id=1, source_target_pairs={{0,1},{1,0},{2,3},{3,2},{4,5},{5,4},{6,7},{7,6},{8,9},{9,8},{10,11... | collective-permute-start | bytes 417800 | tf_op jit(solution)/shard_map/ppermute | solution.py:464
  3.6 9.0 %collective-permute-start.1 = (f32[136,256]{1,0:T(8,128)S(1)}, f32[136,256]{1,0:T(8,128)S(1)}, u32[]{:S(2)}, u32[]{:S(2)}) collective-permute-start(f32[136,256]{1,0:T(8,128)S(1)} %get-tuple-element.57), channel_id=1, source_target_pairs={{1,2},{2,1},{3,4},{4,3},{5,6},{6,5},{7,8},{8,7},{9,10},{10,9},{11,... | collective-permute-start | bytes 417800 | tf_op jit(solution)/shard_map/ppermute | solution.py:470
  13.9 4.9 %collective-permute-start.2 = (f32[64,256]{1,0:T(8,128)S(1)}, f32[64,256]{1,0:T(8,128)S(1)}, u32[]{:S(2)}, u32[]{:S(2)}) collective-permute-start(f32[64,256]{1,0:T(8,128)S(1)} %get-tuple-element.66), channel_id=1, source_target_pairs={{0,1},{1,0},{2,3},{3,2},{4,5},{5,4},{6,7},{7,6},{8,9},{9,8},{10,11... | collective-permute-start | bytes 196616 | tf_op jit(solution)/shard_map/ppermute | solution.py:464
  14.3 6.3 %collective-permute-start.3 = (f32[64,256]{1,0:T(8,128)S(1)}, f32[64,256]{1,0:T(8,128)S(1)}, u32[]{:S(2)}, u32[]{:S(2)}) collective-permute-start(f32[64,256]{1,0:T(8,128)S(1)} %get-tuple-element.67), channel_id=1, source_target_pairs={{1,2},{2,1},{3,4},{4,3},{5,6},{6,5},{7,8},{8,7},{9,10},{10,9},{11,... | collective-permute-start | bytes 196616 | tf_op jit(solution)/shard_map/ppermute | solution.py:470
  22.4 7.1 %collective-permute-start.4 = (f32[128,256]{1,0:T(8,128)S(1)}, f32[128,256]{1,0:T(8,128)S(1)}, u32[]{:S(2)}, u32[]{:S(2)}) collective-permute-start(f32[128,256]{1,0:T(8,128)S(1)} %get-tuple-element.69), channel_id=1, source_target_pairs={{0,1},{1,0},{2,3},{3,2},{4,5},{5,4},{6,7},{7,6},{8,9},{9,8},{10,11... | collective-permute-start | bytes 393224 | tf_op jit(solution)/shard_map/ppermute | solution.py:464
  22.9 7.7 %collective-permute-start.5 = (f32[128,256]{1,0:T(8,128)S(1)}, f32[128,256]{1,0:T(8,128)S(1)}, u32[]{:S(2)}, u32[]{:S(2)}) collective-permute-start(f32[128,256]{1,0:T(8,128)S(1)} %get-tuple-element.70), channel_id=1, source_target_pairs={{1,2},{2,1},{3,4},{4,3},{5,6},{6,5},{7,8},{8,7},{9,10},{10,9},{11,... | collective-permute-start | bytes 393224 | tf_op jit(solution)/shard_map/ppermute | solution.py:470
  33.4 5.3 %collective-permute-start.6 = (f32[72,384]{1,0:T(8,128)S(1)}, f32[72,384]{1,0:T(8,128)S(1)}, u32[]{:S(2)}, u32[]{:S(2)}) collective-permute-start(f32[72,384]{1,0:T(8,128)S(1)} %shard_map.139), channel_id=1, source_target_pairs={{0,1},{1,0},{2,3},{3,2},{4,5},{5,4},{6,7},{7,6},{8,9},{9,8},{10,11... | collective-permute-start | bytes 331784 | tf_op jit(solution)/shard_map/ppermute | solution.py:464
  33.4 7.3 %collective-permute-start.7 = (f32[72,384]{1,0:T(8,128)S(1)}, f32[72,384]{1,0:T(8,128)S(1)}, u32[]{:S(2)}, u32[]{:S(2)}) collective-permute-start(f32[72,384]{1,0:T(8,128)S(1)} %get-tuple-element.86), channel_id=1, source_target_pairs={{1,2},{2,1},{3,4},{4,3},{5,6},{6,5},{7,8},{8,7},{9,10},{10,9},{11,... | collective-permute-start | bytes 331784 | tf_op jit(solution)/shard_map/ppermute | solution.py:470

commit v4 on v3

--- a/solution.py
+++ b/solution.py
@@ -57,7 +57,7 @@
             ref[pl.ds(row0 + first, ROWS), col0 + start : col0 + start + LANES] = total
         return carry
 
-    lax.fori_loop(0, rows // ROWS, group, 0, unroll=4)
+    lax.fori_loop(0, rows // ROWS, group, 0, unroll=True)
 
 
 def merged(targets, weights):
@@ -102,7 +102,7 @@
         return rows + jnp.int16(tall)
 
     start = lax.broadcasted_iota(jnp.int32, (tall, LANES), 0).astype(jnp.int16)
-    lax.fori_loop(0, extent // tall, block, start, unroll=8)
+    lax.fori_loop(0, extent // tall, block, start, unroll=8 if count > 3 else 32)
 
 
 def chosen_lists(place, lists):
@@ -180,9 +180,18 @@
     return level[...] - DT * depth[...] * divergence
 
 
-def level_kernel(place, held, partial, depth, near, far, geh, gel, gnh, gnl, lists, new_level, to_near, to_far):
+def level_kernel(place, held, partial, depth, near, far, geh, gel, gnh, gnl, lists, new_level, to_far):
     new_level[...] = stepped_level(held, partial, depth, near, far, geh, gel, gnh, gnl)
-    pick_lanes(new_level, chosen_lists(place, lists), [(to_near, 0, 0), (to_far, 0, 0)])
+    pick_lanes(new_level, chosen_lists(place, lists)[1:], [(to_far, 0, 0)])
+
+
+def near_picks_kernel(place, field, lists, to_near):
+    chosen = chosen_lists(place, lists)[:1]
+    if len(field.shape) == 2:
+        pick_lanes(field, chosen, [(to_near, 0, 0)])
+    else:
+        for part in range(field.shape[0]):
+            pick_lanes(field.at[part], chosen, [(to_near, part * field.shape[1], 0)])
 
 
 def thirds(value):
@@ -297,15 +306,15 @@
     corner_operator(found, 0, corners, high, low)
 
 
-def flow_kernel(place, flow, east, north, near, far, geh, gel, gnh, gnl, lists, new_flow, to_near, to_far):
+def flow_kernel(place, flow, east, north, near, far, geh, gel, gnh, gnl, lists, new_flow, to_far):
     members = east.shape[0]
     stack = stacked(jnp.concatenate([near[...], far[...]], axis=1))
-    chosen = chosen_lists(place, lists)
+    chosen = chosen_lists(place, lists)[1:]
     first = flow.shape[0] - 2
     new_flow[0] = flow[first] - DT * (east[...] + product(stack, geh, gel))
     new_flow[1] = flow[first + 1] - DT * (north[...] + product(stack, gnh, gnl))
     for part in range(2):
-        pick_lanes(new_flow.at[part], chosen, [(to_near, part * members, 0), (to_far, part * members, 0)])
+        pick_lanes(new_flow.at[part], chosen, [(to_far, part * members, 0)])
 
 
 def divergence_kernel(flow, eh, el, nh, nl, totals, partial):
@@ -345,47 +354,43 @@
     def spread(value):
         return jnp.broadcast_to(value, wide)
 
+    def columns_of(block, pivot):
+        return [spread(block[:, pivot + i : pivot + i + 1]) for i in range(ROWS)]
+
     done = []
     for home in range(len(blocks)):
+        pivot = home * ROWS
+        lines = [spread(blocks[home][i : i + 1, :]) for i in range(ROWS)]
+        columns = columns_of(blocks[home], pivot)
+        entry = {(i, j): spread(columns[j][i : i + 1, :]) for i in range(ROWS) for j in range(i + 1)}
+        inverses, factors = {}, {}
         result = jnp.zeros(wide, F32)
-        for spot in range(0, ROWS, 4):
-            pivot = home * ROWS + spot
-            lines = [spread(blocks[home][spot + i : spot + i + 1, :]) for i in range(4)]
-            columns = [spread(blocks[home][:, pivot + i : pivot + i + 1]) for i in range(4)]
-
-            def entry(i, j):
-                return spread(columns[j][spot + i : spot + i + 1, :])
-
-            head = entry(0, 0), entry(1, 0), entry(1, 1)
-            p = pair_inverse(*head)
-            b = [[entry(2 + i, j) for j in range(2)] for i in range(2)]
-            t = [[b[i][0] * p[0] + b[i][1] * p[1], b[i][0] * p[1] + b[i][1] * p[2]] for i in range(2)]
-            tail = (
-                entry(2, 2) - (t[0][0] * b[0][0] + t[0][1] * b[0][1]),
-                entry(3, 2) - (t[1][0] * b[0][0] + t[1][1] * b[0][1]),
-                entry(3, 3) - (t[1][0] * b[1][0] + t[1][1] * b[1][1]),
-            )
-            rest = [lines[2 + i] - (t[i][0] * lines[0] + t[i][1] * lines[1]) for i in range(2)]
-            q = pair_inverse(*tail)
-            z2 = q[0] * rest[0] + q[1] * rest[1]
-            z3 = q[1] * rest[0] + q[2] * rest[1]
-            z0 = (p[0] * lines[0] + p[1] * lines[1]) - (t[0][0] * z2 + t[1][0] * z3)
-            z1 = (p[1] * lines[0] + p[2] * lines[1]) - (t[0][1] * z2 + t[1][1] * z3)
-            final = pair_rows(*head, lines[0], lines[1]) + pair_rows(*tail, rest[0], rest[1])
-            for i, value in enumerate(final):
-                result = jnp.where(inner == spot + i, value, result)
-            for place in range(home, len(blocks)):
-                factors = columns
-                if place > home:
-                    factors = [spread(blocks[place][:, pivot + i : pivot + i + 1]) for i in range(4)]
-                elif spot + 4 == ROWS:
-                    continue
-                change = (factors[2] * z2 + factors[3] * z3) + (factors[0] * z0 + factors[1] * z1)
-                if place == home:
-                    change = jnp.where(inner >= spot + 4, change, 0.0)
-                blocks[place] = blocks[place] - change
-            beside()
+        for k in range(0, ROWS, 2):
+            head = entry[k, k], entry[k + 1, k], entry[k + 1, k + 1]
+            p = inverses[k] = pair_inverse(*head)
+            for i, value in enumerate(pair_rows(*head, lines[k], lines[k + 1])):
+                result = jnp.where(inner == k + i, value, result)
+            for r in range(k + 2, ROWS):
+                u, v = entry[r, k], entry[r, k + 1]
+                t = factors[r, k] = u * p[0] + v * p[1], u * p[1] + v * p[2]
+                for c in range(k + 2, r + 1):
+                    entry[r, c] = entry[r, c] - (t[0] * entry[c, k] + t[1] * entry[c, k + 1])
+                lines[r] = lines[r] - (t[0] * lines[k] + t[1] * lines[k + 1])
         done.append(result)
+        z = [None] * ROWS
+        for k in range(ROWS - 2, -1, -2):
+            p = inverses[k]
+            z[k] = p[0] * lines[k] + p[1] * lines[k + 1]
+            z[k + 1] = p[1] * lines[k] + p[2] * lines[k + 1]
+            for r in range(k + 2, ROWS):
+                z[k] = z[k] - factors[r, k][0] * z[r]
+                z[k + 1] = z[k + 1] - factors[r, k][1] * z[r]
+        for place in range(home + 1, len(blocks)):
+            terms = [f * z[i] for i, f in enumerate(columns_of(blocks[place], pivot))]
+            while len(terms) > 1:
+                terms = [terms[i] + terms[i + 1] for i in range(0, len(terms), 2)]
+            blocks[place] = blocks[place] - terms[0]
+        beside()
     return jnp.concatenate(done, axis=0)[:, size:]
 
 
@@ -416,8 +421,9 @@
     pieces = [(part, tile) for part in (1, 2, 0) for tile in range(0, nodes // LANES, 2)]
 
     def beside():
-        if pieces:
-            piece(*pieces.pop(0))
+        for _ in range(2):
+            if pieces:
+                piece(*pieces.pop(0))
 
     inverse = inverse_factor(gram, beside)
     while pieces:
@@ -521,8 +527,9 @@
     early = from_near, from_far
 
     args = [place, state, partial, depth, from_near, from_far, *ghost_operators, send_list]
-    level, near, far = call(level_kernel, [field, payload, payload], args, scalars=1, flops=work)
+    level, far = call(level_kernel, [field, payload], args, scalars=1, flops=work)
     from_far = to_other(far)
+    (near,) = call(near_picks_kernel, [payload], [place, level, send_list], scalars=1)
     from_near = to_partner(near)
     east, north = call(slope_kernel, [field] * 2, [level, *operators, totals], flops=work)
     entry_tiles = entries // LANES
@@ -539,14 +546,15 @@
         flops=work,
     )
 
-    flow, near, far = call(
+    flow, far = call(
         flow_kernel,
-        [shape(2, members, nodes)] + [shape(2 * members, width)] * 2,
+        [shape(2, members, nodes), shape(2 * members, width)],
         [place, state, east, north, from_near, from_far, *ghost_operators, send_list],
         scalars=1,
         flops=work,
     )
     from_far = to_other(far)
+    (near,) = call(near_picks_kernel, [shape(2 * members, width)], [place, flow, send_list], scalars=1)
     from_near = to_partner(near)
     high, low = call(
         functools.partial(others_kernel, corners),

time: 45.5 us -> 43.4 us (0.954)
  the two profiles are of different devices: /device:TPU:9 before, /device:TPU:19 now
where the time goes in v4:
time: 43.4 us; the launch traced here: 43.2 us
  Pallas kernels  22.8 us (53%)
  starting transfers between devices  14 us (32%)
  waiting for transfers between devices  5.36 us (12%)
  between operations  0.99 us (2%)
    pallas_call x16, Pallas kernels, call(): pl.pallas_call(kernel, out_shape=outs, in_specs=in_specs, out_specs=[pl.B...  22.8 us
    ppermute x4, starting transfers between devices, to_other(): return lax.ppermute(value, 'mesh', others)  12.3 us
    ppermute x4, waiting for transfers between devices, to_other(): return lax.ppermute(value, 'mesh', others)  5.35 us
    ppermute x4, starting transfers between devices, to_partner(): return lax.ppermute(value, 'mesh', pairs)  1.75 us
  transfers between devices with their start and end apart: 8, of which 3 were waited for; matrix products, arithmetic and copies ran while one was open for 0% of the time, Pallas kernels for 29%

profile of v4, /device:TPU:19, one launch (start us, length us, event | category | flops | bytes accessed | tf_op | source)
XLA Modules:
  0.0 43.2 jit_solution(7900481706978878318)
XLA Ops:
  0.7 2.0 %shard_map.127 = (f32[136,256]{1,0:T(8,128)S(1)}, f32[136,256]{1,0:T(8,128)S(1)}, f32[3,64,1024]{2,1,0:T(8,128)S(1)}, s32[2,256]{1,0:T(2,128)S(1)}, s32[1,512]{1...) custom-call(s32[1]{0:T(128)} %bitcast.place, ...), custom_call_target="tpu_custom_call" | custom-call | bytes 2134024 | tf_op jit(solution)/shard_map/pallas_call | solution.py:453
  2.7 0.7 %collective-permute-start = (f32[136,256]{1,0:T(8,128)S(1)}, f32[136,256]{1,0:T(8,128)S(1)}, u32[]{:S(2)}, u32[]{:S(2)}) collective-permute-start(f32[136,256]{1,0:T(8,128)S(1)} %get-tuple-element.54), channel_id=1, source_target_pairs={{0,1},{1,0},{2,3},{3,2},{4,5},{5,4},{6,7},{7,6},{8,9},{9,8},{10,11... | collective-permute-start | bytes 417800 | tf_op jit(solution)/shard_map/ppermute | solution.py:470
  3.4 3.0 %collective-permute-start.1 = (f32[136,256]{1,0:T(8,128)S(1)}, f32[136,256]{1,0:T(8,128)S(1)}, u32[]{:S(2)}, u32[]{:S(2)}) collective-permute-start(f32[136,256]{1,0:T(8,128)S(1)} %get-tuple-element.55), channel_id=1, source_target_pairs={{1,2},{2,1},{3,4},{4,3},{5,6},{6,5},{7,8},{8,7},{9,10},{10,9},{11,... | collective-permute-start | bytes 417800 | tf_op jit(solution)/shard_map/ppermute | solution.py:476
  6.5 4.6 %shard_map.128 = (bf16[8,1024,128]{2,1,0:T(8,128)(2,1)S(1)}, bf16[8,1024,128]{2,1,0:T(8,128)(2,1)S(1)}, bf16[8,1024,128]{2,1,0:T(8,128)(2,1)S(1)}, bf16[8,1024,1...) custom-call(s32[1]{0:T(128)} %bitcast.place, ...), custom_call_target="tpu_custom_call" | custom-call | flops 1073741824 | bytes 12689412 | tf_op jit(solution)/shard_map/pallas_call | solution.py:453
  11.1 1.3 %shard_map.129.partial = f32[64,1024]{1,0:T(8,128)S(1)} custom-call(f32[3,64,1024]{2,1,0:T(8,128)S(1)} %get-tuple-element.44.flow.held, bf16[8,1024,128]{2,1,0:T(8,128)(2,1)S(1)} %get-tuple-element.48.eh, bf16[8,1024,128]{2,1,0:T(8,128)(2,1)S(1)} %get-tuple-element.49.el, bf16[8,1024,128]{2,1,0:T(8,128)(2,1)S(1)} %get-tuple-element.50.nh, ...), custom_call_target="tpu_custom_call" | custom-call | flops 536870912 | bytes 9445376 | tf_op jit(solution)/shard_map/pallas_call | solution.py:453
  12.4 0.9 %shard_map.130 = (f32[64,1024]{1,0:T(8,128)S(1)}, f32[64,256]{1,0:T(8,128)S(1)}) custom-call(s32[1]{0:T(128)} %bitcast.place, f32[3,64,1024]{2,1,0:T(8,128)S(1)} %get-tuple-element.44.flow.held, f32[64,1024]{1,0:T(8,128)S(1)} %shard_map.129.partial, f32[1,1024]{1,0:T(1,128)S(1)} %get-tuple-element.53.depth, f32[136,256]{1,0:T(8,128)S(1)} %collective-permute-done.near, ...), custom_call_target="tpu_custom_call" | custom-call | flops 536870912 | bytes 5855236 | tf_op jit(solution)/shard_map/pallas_call | solution.py:453
  14.0 3.2 %collective-permute-start.3 = (f32[64,256]{1,0:T(8,128)S(1)}, f32[64,256]{1,0:T(8,128)S(1)}, u32[]{:S(2)}, u32[]{:S(2)}) collective-permute-start(f32[64,256]{1,0:T(8,128)S(1)} %get-tuple-element.64), channel_id=1, source_target_pairs={{1,2},{2,1},{3,4},{4,3},{5,6},{6,5},{7,8},{8,7},{9,10},{10,9},{11,... | collective-permute-start | bytes 196616 | tf_op jit(solution)/shard_map/ppermute | solution.py:476
  17.2 1.3 %shard_map.131 = (f32[64,1024]{1,0:T(8,128)S(1)}, f32[64,1024]{1,0:T(8,128)S(1)}) custom-call(f32[64,1024]{1,0:T(8,128)S(1)} %get-tuple-element.61.level.field.held, bf16[8,1024,128]{2,1,0:T(8,128)(2,1)S(1)} %get-tuple-element.48.eh, bf16[8,1024,128]{2,1,0:T(8,128)(2,1)S(1)} %get-tuple-element.49.el, bf16[8,1024,128]{2,1,0:T(8,128)(2,1)S(1)} %get-tuple-element.50.nh, ...), custom_call_target="tpu_custom_call" | custom-call | flops 536870912 | bytes 9183232 | tf_op jit(solution)/shard_map/pallas_call | solution.py:453
  18.5 1.8 %collective-permute-done.3.far = f32[64,256]{1,0:T(8,128)S(1)} collective-permute-done((f32[64,256]{1,0:T(8,128)S(1)}, f32[64,256]{1,0:T(8,128)S(1)}, u32[]{:S(2)}, u32[]{:S(2)}) %collective-permute-start.3) | collective-permute-done | bytes 65568 | tf_op jit(solution)/shard_map/ppermute | solution.py:476
  20.3 0.9 %shard_map.133 = (f32[2,64,1024]{2,1,0:T(8,128)S(1)}, f32[128,256]{1,0:T(8,128)S(1)}) custom-call(s32[1]{0:T(128)} %bitcast.place, f32[3,64,1024]{2,1,0:T(8,128)S(1)} %get-tuple-element.44.flow.held, f32[64,1024]{1,0:T(8,128)S(1)} %get-tuple-element.62.east, f32[64,1024]{1,0:T(8,128)S(1)} %get-tuple-element.63.north, ...), custom_call_target="tpu_custom_call" | custom-call | flops 536870912 | bytes 6293508 | tf_op jit(solution)/shard_map/pallas_call | solution.py:453
  21.3 0.4 %shard_map.135 = f32[128,256]{1,0:T(8,128)S(1)} custom-call(s32[1]{0:T(128)} %bitcast.place, f32[2,64,1024]{2,1,0:T(8,128)S(1)} %get-tuple-element.65.flow.field, s32[2,256]{1,0:T(2,128)S(1)} %get-tuple-element.60.lists), custom_call_target="tpu_custom_call" | custom-call | bytes 657412 | tf_op jit(solution)/shard_map/pallas_call | solution.py:453
  21.7 0.5 %collective-permute-start.4 = (f32[128,256]{1,0:T(8,128)S(1)}, f32[128,256]{1,0:T(8,128)S(1)}, u32[]{:S(2)}, u32[]{:S(2)}) collective-permute-start(f32[128,256]{1,0:T(8,128)S(1)} %shard_map.135), channel_id=1, source_target_pairs={{0,1},{1,0},{2,3},{3,2},{4,5},{5,4},{6,7},{7,6},{8,9},{9,8},{10,11... | collective-permute-start | bytes 393224 | tf_op jit(solution)/shard_map/ppermute | solution.py:470
  22.2 2.9 %collective-permute-start.5 = (f32[128,256]{1,0:T(8,128)S(1)}, f32[128,256]{1,0:T(8,128)S(1)}, u32[]{:S(2)}, u32[]{:S(2)}) collective-permute-start(f32[128,256]{1,0:T(8,128)S(1)} %get-tuple-element.66), channel_id=1, source_target_pairs={{1,2},{2,1},{3,4},{4,3},{5,6},{6,5},{7,8},{8,7},{9,10},{10,9},{11,... | collective-permute-start | bytes 393224 | tf_op jit(solution)/shard_map/ppermute | solution.py:476
  25.2 0.8 %shard_map.136 = (bf16[4,1024,128]{2,1,0:T(8,128)(2,1)S(1)}, bf16[4,1024,128]{2,1,0:T(8,128)(2,1)S(1)}, f32[8,512]{1,0:T(8,128)S(1)}, f32[8,1536]{1,0:T(8,128)S(1)}) custom-call(s32[1]{0:T(128)} %bitcast.place, s32[1]{0:T(128)S(6)} %copy.14.length, f32[136,256]{1,0:T(8,128)S(1)} %collective-permute-done.near, f32[136,256]{1,0:T(8,128)S(1)} %collective-permute-done.1.far, ...), custom_call_target="tpu_custom_call" | custom-call | flops 536870912 | bytes 2478088 | tf_op jit(solution)/shard_map/pallas_call | solution.py:453
  26.0 1.1 %shard_map.137 = (bf16[8,1024,128]{2,1,0:T(8,128)(2,1)S(1)}, bf16[8,1024,128]{2,1,0:T(8,128)(2,1)S(1)}) custom-call(f32[8,1536]{1,0:T(8,128)S(1)} %get-tuple-element.73.found), custom_call_target="tpu_custom_call" | custom-call | flops 536870912 | bytes 4243456 | tf_op jit(solution)/shard_map/pallas_call | solution.py:453
  27.1 1.3 %shard_map.134.partial = f32[64,1024]{1,0:T(8,128)S(1)} custom-call(f32[2,64,1024]{2,1,0:T(8,128)S(1)} %get-tuple-element.65.flow.field, bf16[8,1024,128]{2,1,0:T(8,128)(2,1)S(1)} %get-tuple-element.48.eh, bf16[8,1024,128]{2,1,0:T(8,128)(2,1)S(1)} %get-tuple-element.49.el, bf16[8,1024,128]{2,1,0:T(8,128)(2,1)S(1)} %get-tuple-element.50.nh, ...), custom_call_target="tpu_custom_call" | custom-call | flops 536870912 | bytes 9183232 | tf_op jit(solution)/shard_map/pallas_call | solution.py:453
  28.4 1.5 %collective-permute-done.5.far = f32[128,256]{1,0:T(8,128)S(1)} collective-permute-done((f32[128,256]{1,0:T(8,128)S(1)}, f32[128,256]{1,0:T(8,128)S(1)}, u32[]{:S(2)}, u32[]{:S(2)}) %collective-permute-start.5) | collective-permute-done | bytes 131104 | tf_op jit(solution)/shard_map/ppermute | solution.py:476
  29.9 1.4 %shard_map.138 = (f32[64,1024]{1,0:T(8,128)S(1)}, f32[72,384]{1,0:T(8,128)S(1)}) custom-call(s32[1]{0:T(128)} %bitcast.place, f32[64,1024]{1,0:T(8,128)S(1)} %get-tuple-element.61.level.field.held, f32[64,1024]{1,0:T(8,128)S(1)} %shard_map.134.partial, f32[1,1024]{1,0:T(1,128)S(1)} %get-tuple-element.53.depth, f32[128,256]{1,0:T(8,128)S(1)} %collective-permute-done.4.near, ...), custom_call_target="tpu_custom_call" | custom-call | flops 536870912 | bytes 9570308 | tf_op jit(solution)/shard_map/pallas_call | solution.py:453
  31.3 0.7 %shard_map.141 = f32[72,384]{1,0:T(8,128)S(1)} custom-call(s32[1]{0:T(128)} %bitcast.place, f32[64,1024]{1,0:T(8,128)S(1)} %get-tuple-element.77.level, s32[2,256]{1,0:T(2,128)S(1)} %get-tuple-element.60.lists, bf16[8,1024,128]{2,1,0:T(8,128)(2,1)S(1)} %get-tuple-element.74.high, bf16[8,1024,128]{2,1,0:T(8,128)(2,1)S(1)} %get-tuple-element.75.low, ...), custom_call_target="tpu_custom_call" | custom-call | flops 536870912 | bytes 4585476 | tf_op jit(solution)/shard_map/pallas_call | solution.py:453
  32.1 3.1 %collective-permute-start.7 = (f32[72,384]{1,0:T(8,128)S(1)}, f32[72,384]{1,0:T(8,128)S(1)}, u32[]{:S(2)}, u32[]{:S(2)}) collective-permute-start(f32[72,384]{1,0:T(8,128)S(1)} %get-tuple-element.82), channel_id=1, source_target_pairs={{1,2},{2,1},{3,4},{4,3},{5,6},{6,5},{7,8},{8,7},{9,10},{10,9},{11,... | collective-permute-start | bytes 331784 | tf_op jit(solution)/shard_map/ppermute | solution.py:476
  35.2 1.3 %shard_map.139 = (f32[64,1024]{1,0:T(8,128)S(1)}, f32[64,1024]{1,0:T(8,128)S(1)}) custom-call(f32[64,1024]{1,0:T(8,128)S(1)} %get-tuple-element.77.level, bf16[8,1024,128]{2,1,0:T(8,128)(2,1)S(1)} %get-tuple-element.48.eh, bf16[8,1024,128]{2,1,0:T(8,128)(2,1)S(1)} %get-tuple-element.49.el, bf16[8,1024,128]{2,1,0:T(8,128)(2,1)S(1)} %get-tuple-element.50.nh, ...), custom_call_target="tpu_custom_call" | custom-call | flops 536870912 | bytes 9183232 | tf_op jit(solution)/shard_map/pallas_call | solution.py:453
  36.5 0.7 %shard_map.140.sums = f32[72,64]{1,0:T(8,128)S(1)} custom-call(f32[64,1024]{1,0:T(8,128)S(1)} %get-tuple-element.77.level, bf16[4,1024,128]{2,1,0:T(8,128)(2,1)S(1)} %get-tuple-element.80.high, bf16[4,1024,128]{2,1,0:T(8,128)(2,1)S(1)} %get-tuple-element.81.low, f32[8,512]{1,0:T(8,128)S(1)} %get-tuple-element.76.tables), custom_call_target="tpu_custom_call" | custom-call | flops 536870912 | bytes 2394112 | tf_op jit(solution)/shard_map/pallas_call | solution.py:453
  37.3 2.1 %collective-permute-done.7.far = f32[72,384]{1,0:T(8,128)S(1)} collective-permute-done((f32[72,384]{1,0:T(8,128)S(1)}, f32[72,384]{1,0:T(8,128)S(1)}, u32[]{:S(2)}, u32[]{:S(2)}) %collective-permute-start.7) | collective-permute-done | bytes 110624 | tf_op jit(solution)/shard_map/ppermute | solution.py:476
  39.3 3.7 %shard_map.142 = f32[3,64,1024]{2,1,0:T(8,128)} custom-call(f32[2,64,1024]{2,1,0:T(8,128)S(1)} %get-tuple-element.65.flow.field, f32[64,1024]{1,0:T(8,128)S(1)} %get-tuple-element.77.level, f32[64,1024]{1,0:T(8,128)S(1)} %get-tuple-element.78.east, f32[64,1024]{1,0:T(8,128)S(1)} %get-tuple-element.79.north, f32[72,64]{1,0:T(8,128)S(1)} %shard_map.140.sums, ...), custom_call_target="tpu_custom_call" | custom-call | flops 536870912 | bytes 6531072 | tf_op jit(solution)/shard_map/pallas_call | solution.py:453
  (8 shorter events, 0.8 us)
Async XLA Ops:
  2.7 9.7 %collective-permute-start = (f32[136,256]{1,0:T(8,128)S(1)}, f32[136,256]{1,0:T(8,128)S(1)}, u32[]{:S(2)}, u32[]{:S(2)}) collective-permute-start(f32[136,256]{1,0:T(8,128)S(1)} %get-tuple-element.54), channel_id=1, source_target_pairs={{0,1},{1,0},{2,3},{3,2},{4,5},{5,4},{6,7},{7,6},{8,9},{9,8},{10,11... | collective-permute-start | bytes 417800 | tf_op jit(solution)/shard_map/ppermute | solution.py:470
  3.4 9.0 %collective-permute-start.1 = (f32[136,256]{1,0:T(8,128)S(1)}, f32[136,256]{1,0:T(8,128)S(1)}, u32[]{:S(2)}, u32[]{:S(2)}) collective-permute-start(f32[136,256]{1,0:T(8,128)S(1)} %get-tuple-element.55), channel_id=1, source_target_pairs={{1,2},{2,1},{3,4},{4,3},{5,6},{6,5},{7,8},{8,7},{9,10},{10,9},{11,... | collective-permute-start | bytes 417800 | tf_op jit(solution)/shard_map/ppermute | solution.py:476
  13.6 4.9 %collective-permute-start.2 = (f32[64,256]{1,0:T(8,128)S(1)}, f32[64,256]{1,0:T(8,128)S(1)}, u32[]{:S(2)}, u32[]{:S(2)}) collective-permute-start(f32[64,256]{1,0:T(8,128)S(1)} %shard_map.132), channel_id=1, source_target_pairs={{0,1},{1,0},{2,3},{3,2},{4,5},{5,4},{6,7},{7,6},{8,9},{9,8},{10,11... | collective-permute-start | bytes 196616 | tf_op jit(solution)/shard_map/ppermute | solution.py:470
  14.0 6.3 %collective-permute-start.3 = (f32[64,256]{1,0:T(8,128)S(1)}, f32[64,256]{1,0:T(8,128)S(1)}, u32[]{:S(2)}, u32[]{:S(2)}) collective-permute-start(f32[64,256]{1,0:T(8,128)S(1)} %get-tuple-element.64), channel_id=1, source_target_pairs={{1,2},{2,1},{3,4},{4,3},{5,6},{6,5},{7,8},{8,7},{9,10},{10,9},{11,... | collective-permute-start | bytes 196616 | tf_op jit(solution)/shard_map/ppermute | solution.py:476
  21.7 6.7 %collective-permute-start.4 = (f32[128,256]{1,0:T(8,128)S(1)}, f32[128,256]{1,0:T(8,128)S(1)}, u32[]{:S(2)}, u32[]{:S(2)}) collective-permute-start(f32[128,256]{1,0:T(8,128)S(1)} %shard_map.135), channel_id=1, source_target_pairs={{0,1},{1,0},{2,3},{3,2},{4,5},{5,4},{6,7},{7,6},{8,9},{9,8},{10,11... | collective-permute-start | bytes 393224 | tf_op jit(solution)/shard_map/ppermute | solution.py:470
  22.2 7.7 %collective-permute-start.5 = (f32[128,256]{1,0:T(8,128)S(1)}, f32[128,256]{1,0:T(8,128)S(1)}, u32[]{:S(2)}, u32[]{:S(2)}) collective-permute-start(f32[128,256]{1,0:T(8,128)S(1)} %get-tuple-element.66), channel_id=1, source_target_pairs={{1,2},{2,1},{3,4},{4,3},{5,6},{6,5},{7,8},{8,7},{9,10},{10,9},{11,... | collective-permute-start | bytes 393224 | tf_op jit(solution)/shard_map/ppermute | solution.py:476
  32.0 5.3 %collective-permute-start.6 = (f32[72,384]{1,0:T(8,128)S(1)}, f32[72,384]{1,0:T(8,128)S(1)}, u32[]{:S(2)}, u32[]{:S(2)}) collective-permute-start(f32[72,384]{1,0:T(8,128)S(1)} %shard_map.141), channel_id=1, source_target_pairs={{0,1},{1,0},{2,3},{3,2},{4,5},{5,4},{6,7},{7,6},{8,9},{9,8},{10,11... | collective-permute-start | bytes 331784 | tf_op jit(solution)/shard_map/ppermute | solution.py:470
  32.1 7.3 %collective-permute-start.7 = (f32[72,384]{1,0:T(8,128)S(1)}, f32[72,384]{1,0:T(8,128)S(1)}, u32[]{:S(2)}, u32[]{:S(2)}) collective-permute-start(f32[72,384]{1,0:T(8,128)S(1)} %get-tuple-element.82), channel_id=1, source_target_pairs={{1,2},{2,1},{3,4},{4,3},{5,6},{6,5},{7,8},{8,7},{9,10},{10,9},{11,... | collective-permute-start | bytes 331784 | tf_op jit(solution)/shard_map/ppermute | solution.py:476

commit v5 on v4

--- a/solution.py
+++ b/solution.py
@@ -73,7 +73,7 @@
     return weights
 
 
-def build_operator(targets, weights, outputs, begin, extent, tile):
+def build_operator(targets, weights, outputs, begin, extent, tile, unroll):
     count = len(targets)
     tall = 2 * ROWS
     wanted = [jnp.broadcast_to(t - begin, (tall, LANES)).astype(jnp.int16) for t in targets]
@@ -102,7 +102,7 @@
         return rows + jnp.int16(tall)
 
     start = lax.broadcasted_iota(jnp.int32, (tall, LANES), 0).astype(jnp.int16)
-    lax.fori_loop(0, extent // tall, block, start, unroll=8 if count > 3 else 32)
+    lax.fori_loop(0, extent // tall, block, start, unroll=unroll)
 
 
 def chosen_lists(place, lists):
@@ -143,12 +143,15 @@
     far[2 * members :, :] = block
 
 
-def prepare_kernel(place, coef, wet, conn, eh, el, nh, nl, geh, gel, gnh, gnl, totals):
+def prepare_kernel(
+    place, state, coef, wet, conn, eh, el, nh, nl, geh, gel, gnh, gnl, totals, partial, stacks, targets_at, weights_at
+):
     slots, nodes = conn.shape
     ghosts = geh.shape[1]
     turned = (1 - (place[0] & 1)) * (ghosts // 2)
-    for column in range(0, nodes, LANES):
-        cut = slice(column, column + LANES)
+    count = nodes // LANES
+    for tile in range(count):
+        cut = slice(tile * LANES, (tile + 1) * LANES)
         targets = []
         for s in range(slots):
             raw = conn[s : s + 1, cut]
@@ -160,8 +163,22 @@
         for d in range(2):
             totals[d : d + 1, cut] = sum(weights[d][1:], weights[d][0])
         weights = merged(targets, weights)
-        build_operator(targets, weights, (eh, el, nh, nl), 0, nodes, column // LANES)
-        build_operator(targets, weights, (geh, gel, gnh, gnl), nodes, ghosts, column // LANES)
+        for s in range(slots):
+            targets_at[s : s + 1, cut] = targets[s]
+            for d in range(2):
+                weights_at[d, s : s + 1, cut] = weights[d][s]
+        build_operator(targets, weights, (eh, el, nh, nl), 0, nodes, tile, 8)
+    for d in range(2):
+        stacks[d] = stacked(state[1 + d])
+    for tile in range(count):
+        pair, d = divmod(tile, 2)
+        span = slice(2 * pair * LANES, 2 * (pair + 1) * LANES)
+        found = product(stacks[d], *((eh, el), (nh, nl))[d], 2 * pair, 2) - state[1 + d, :, span] * totals[d : d + 1, span]
+        cut = slice(tile * LANES, (tile + 1) * LANES)
+        targets = [targets_at[s : s + 1, cut] for s in range(slots)]
+        weights = [[weights_at[g, s : s + 1, cut] for s in range(slots)] for g in range(2)]
+        build_operator(targets, weights, (geh, gel, gnh, gnl), nodes, ghosts, tile, True)
+        partial[:, span] = found if d == 0 else partial[:, span] + found
 
 
 def ghost_flow(near, far, part, members):
@@ -299,7 +316,7 @@
         here = found[:, (first + tile) * LANES : (first + tile + 1) * LANES]
         targets = [here[c : c + 1, :].astype(jnp.int32) for c in range(corners)]
         shares = [here[corners + c : corners + c + 1, :] for c in range(corners)]
-        build_operator(targets, merged(targets, [shares]), (high, low), 0, high.shape[1], tile)
+        build_operator(targets, merged(targets, [shares]), (high, low), 0, high.shape[1], tile, 32)
 
 
 def others_kernel(corners, found, high, low):
@@ -519,11 +536,19 @@
     big = [shape(tiles, nodes, LANES, dtype=BF16)] * 4
     small = [shape(tiles, ghosts, LANES, dtype=BF16)] * 4
     made = call(
-        prepare_kernel, big + small + [shape(2, nodes)], [place, coef, wet_faces, conn], scalars=1, flops=2 * work
-    )
-    operators, ghost_operators, totals = made[:4], made[4:8], made[8]
+        prepare_kernel,
+        big + small + [shape(2, nodes), shape(members, nodes)],
+        [place, state, coef, wet_faces, conn],
+        scalars=1,
+        scratch=[
+            pltpu.VMEM((2, 2 * members, nodes), BF16),
+            pltpu.VMEM(conn.shape, jnp.int32),
+            pltpu.VMEM((2,) + conn.shape, F32),
+        ],
+        flops=3 * work,
+    )
+    operators, ghost_operators, totals, partial = made[:4], made[4:8], made[8], made[9]
     field, payload = shape(members, nodes), shape(members, width)
-    (partial,) = call(divergence_kernel, [field], [state, *operators, totals], flops=work)
     early = from_near, from_far
 
     args = [place, state, partial, depth, from_near, from_far, *ghost_operators, send_list]

time: 43.4 us -> 42.7 us (0.984)
  the two profiles are of different devices: /device:TPU:19 before, /device:TPU:25 now
where the time goes in v5:
time: 42.7 us; the launch traced here: 42.5 us
  Pallas kernels  22.2 us (52%)
  starting transfers between devices  11 us (26%)
  waiting for transfers between devices  8.4 us (20%)
  between operations  0.98 us (2%)
    pallas_call x15, Pallas kernels, call(): pl.pallas_call(kernel, out_shape=outs, in_specs=in_specs, out_specs=[pl.B...  22.2 us
    ppermute x4, starting transfers between devices, to_other(): return lax.ppermute(value, 'mesh', others)  9.2 us
    ppermute x4, waiting for transfers between devices, to_other(): return lax.ppermute(value, 'mesh', others)  8.39 us
    ppermute x4, starting transfers between devices, to_partner(): return lax.ppermute(value, 'mesh', pairs)  1.76 us
  transfers between devices with their start and end apart: 8, of which 3 were waited for; matrix products, arithmetic and copies ran while one was open for 0% of the time, Pallas kernels for 28%

profile of v5, /device:TPU:25, one launch (start us, length us, event | category | flops | bytes accessed | tf_op | source)
XLA Modules:
  0.0 42.5 jit_solution(16282637188771747904)
XLA Ops:
  0.7 2.0 %shard_map.127 = (f32[136,256]{1,0:T(8,128)S(1)}, f32[136,256]{1,0:T(8,128)S(1)}, f32[3,64,1024]{2,1,0:T(8,128)S(1)}, s32[2,256]{1,0:T(2,128)S(1)}, s32[1,512]{1...) custom-call(s32[1]{0:T(128)} %bitcast.place, ...), custom_call_target="tpu_custom_call" | custom-call | bytes 2134024 | tf_op jit(solution)/shard_map/pallas_call | solution.py:470
  2.7 0.7 %collective-permute-start = (f32[136,256]{1,0:T(8,128)S(1)}, f32[136,256]{1,0:T(8,128)S(1)}, u32[]{:S(2)}, u32[]{:S(2)}) collective-permute-start(f32[136,256]{1,0:T(8,128)S(1)} %get-tuple-element.51), channel_id=1, source_target_pairs={{0,1},{1,0},{2,3},{3,2},{4,5},{5,4},{6,7},{7,6},{8,9},{9,8},{10,11... | collective-permute-start | bytes 417800 | tf_op jit(solution)/shard_map/ppermute | solution.py:487
  3.4 3.0 %collective-permute-start.1 = (f32[136,256]{1,0:T(8,128)S(1)}, f32[136,256]{1,0:T(8,128)S(1)}, u32[]{:S(2)}, u32[]{:S(2)}) collective-permute-start(f32[136,256]{1,0:T(8,128)S(1)} %get-tuple-element.52), channel_id=1, source_target_pairs={{1,2},{2,1},{3,4},{4,3},{5,6},{6,5},{7,8},{8,7},{9,10},{10,9},{11,... | collective-permute-start | bytes 417800 | tf_op jit(solution)/shard_map/ppermute | solution.py:493
  6.5 5.2 %shard_map.128 = (bf16[8,1024,128]{2,1,0:T(8,128)(2,1)S(1)}, bf16[8,1024,128]{2,1,0:T(8,128)(2,1)S(1)}, bf16[8,1024,128]{2,1,0:T(8,128)(2,1)S(1)}, bf16[8,1024,1...) custom-call(s32[1]{0:T(128)} %bitcast.place, ...), custom_call_target="tpu_custom_call" | custom-call | flops 1610612736 | bytes 13737988 | tf_op jit(solution)/shard_map/pallas_call | solution.py:470
  11.8 0.9 %shard_map.129 = (f32[64,1024]{1,0:T(8,128)S(1)}, f32[64,256]{1,0:T(8,128)S(1)}) custom-call(s32[1]{0:T(128)} %bitcast.place, f32[3,64,1024]{2,1,0:T(8,128)S(1)} %get-tuple-element.45.state.held.flow, f32[64,1024]{1,0:T(8,128)S(1)} %get-tuple-element.49.partial, f32[1,1024]{1,0:T(1,128)S(1)} %get-tuple-element.50.depth, ...), custom_call_target="tpu_custom_call" | custom-call | flops 536870912 | bytes 5855236 | tf_op jit(solution)/shard_map/pallas_call | solution.py:470
  12.9 0.4 %collective-permute-start.2 = (f32[64,256]{1,0:T(8,128)S(1)}, f32[64,256]{1,0:T(8,128)S(1)}, u32[]{:S(2)}, u32[]{:S(2)}) collective-permute-start(f32[64,256]{1,0:T(8,128)S(1)} %shard_map.131), channel_id=1, source_target_pairs={{0,1},{1,0},{2,3},{3,2},{4,5},{5,4},{6,7},{7,6},{8,9},{9,8},{10,11... | collective-permute-start | bytes 196616 | tf_op jit(solution)/shard_map/ppermute | solution.py:487
  13.4 2.1 %collective-permute-start.3 = (f32[64,256]{1,0:T(8,128)S(1)}, f32[64,256]{1,0:T(8,128)S(1)}, u32[]{:S(2)}, u32[]{:S(2)}) collective-permute-start(f32[64,256]{1,0:T(8,128)S(1)} %get-tuple-element.66), channel_id=1, source_target_pairs={{1,2},{2,1},{3,4},{4,3},{5,6},{6,5},{7,8},{8,7},{9,10},{10,9},{11,... | collective-permute-start | bytes 196616 | tf_op jit(solution)/shard_map/ppermute | solution.py:493
  15.5 1.3 %shard_map.130 = (f32[64,1024]{1,0:T(8,128)S(1)}, f32[64,1024]{1,0:T(8,128)S(1)}) custom-call(f32[64,1024]{1,0:T(8,128)S(1)} %get-tuple-element.58.level.field.held, bf16[8,1024,128]{2,1,0:T(8,128)(2,1)S(1)} %get-tuple-element.59.eh, bf16[8,1024,128]{2,1,0:T(8,128)(2,1)S(1)} %get-tuple-element.60.el, bf16[8,1024,128]{2,1,0:T(8,128)(2,1)S(1)} %get-tuple-element.61.nh, ...), custom_call_target="tpu_custom_call" | custom-call | flops 536870912 | bytes 9183232 | tf_op jit(solution)/shard_map/pallas_call | solution.py:470
  16.8 2.8 %collective-permute-done.3.far = f32[64,256]{1,0:T(8,128)S(1)} collective-permute-done((f32[64,256]{1,0:T(8,128)S(1)}, f32[64,256]{1,0:T(8,128)S(1)}, u32[]{:S(2)}, u32[]{:S(2)}) %collective-permute-start.3) | collective-permute-done | bytes 65568 | tf_op jit(solution)/shard_map/ppermute | solution.py:493
  19.7 0.9 %shard_map.132 = (f32[2,64,1024]{2,1,0:T(8,128)S(1)}, f32[128,256]{1,0:T(8,128)S(1)}) custom-call(s32[1]{0:T(128)} %bitcast.place, f32[3,64,1024]{2,1,0:T(8,128)S(1)} %get-tuple-element.45.state.held.flow, f32[64,1024]{1,0:T(8,128)S(1)} %get-tuple-element.64.east, f32[64,1024]{1,0:T(8,128)S(1)} %get-tuple-element.65.north, ...), custom_call_target="tpu_custom_call" | custom-call | flops 536870912 | bytes 6293508 | tf_op jit(solution)/shard_map/pallas_call | solution.py:470
  20.6 0.4 %shard_map.134 = f32[128,256]{1,0:T(8,128)S(1)} custom-call(s32[1]{0:T(128)} %bitcast.place, f32[2,64,1024]{2,1,0:T(8,128)S(1)} %get-tuple-element.67.flow.field, s32[2,256]{1,0:T(2,128)S(1)} %get-tuple-element.57.lists), custom_call_target="tpu_custom_call" | custom-call | bytes 657412 | tf_op jit(solution)/shard_map/pallas_call | solution.py:470
  21.0 0.5 %collective-permute-start.4 = (f32[128,256]{1,0:T(8,128)S(1)}, f32[128,256]{1,0:T(8,128)S(1)}, u32[]{:S(2)}, u32[]{:S(2)}) collective-permute-start(f32[128,256]{1,0:T(8,128)S(1)} %shard_map.134), channel_id=1, source_target_pairs={{0,1},{1,0},{2,3},{3,2},{4,5},{5,4},{6,7},{7,6},{8,9},{9,8},{10,11... | collective-permute-start | bytes 393224 | tf_op jit(solution)/shard_map/ppermute | solution.py:487
  21.5 1.9 %collective-permute-start.5 = (f32[128,256]{1,0:T(8,128)S(1)}, f32[128,256]{1,0:T(8,128)S(1)}, u32[]{:S(2)}, u32[]{:S(2)}) collective-permute-start(f32[128,256]{1,0:T(8,128)S(1)} %get-tuple-element.68), channel_id=1, source_target_pairs={{1,2},{2,1},{3,4},{4,3},{5,6},{6,5},{7,8},{8,7},{9,10},{10,9},{11,... | collective-permute-start | bytes 393224 | tf_op jit(solution)/shard_map/ppermute | solution.py:493
  23.5 0.8 %shard_map.135 = (bf16[4,1024,128]{2,1,0:T(8,128)(2,1)S(1)}, bf16[4,1024,128]{2,1,0:T(8,128)(2,1)S(1)}, f32[8,512]{1,0:T(8,128)S(1)}, f32[8,1536]{1,0:T(8,128)S(1)}) custom-call(s32[1]{0:T(128)} %bitcast.place, s32[1]{0:T(128)S(6)} %copy.14.length, f32[136,256]{1,0:T(8,128)S(1)} %collective-permute-done.near, f32[136,256]{1,0:T(8,128)S(1)} %collective-permute-done.1.far, ...), custom_call_target="tpu_custom_call" | custom-call | flops 536870912 | bytes 2478088 | tf_op jit(solution)/shard_map/pallas_call | solution.py:470
  24.3 1.1 %shard_map.136 = (bf16[8,1024,128]{2,1,0:T(8,128)(2,1)S(1)}, bf16[8,1024,128]{2,1,0:T(8,128)(2,1)S(1)}) custom-call(f32[8,1536]{1,0:T(8,128)S(1)} %get-tuple-element.75.found), custom_call_target="tpu_custom_call" | custom-call | flops 536870912 | bytes 4243456 | tf_op jit(solution)/shard_map/pallas_call | solution.py:470
  25.4 1.3 %shard_map.133.partial = f32[64,1024]{1,0:T(8,128)S(1)} custom-call(f32[2,64,1024]{2,1,0:T(8,128)S(1)} %get-tuple-element.67.flow.field, bf16[8,1024,128]{2,1,0:T(8,128)(2,1)S(1)} %get-tuple-element.59.eh, bf16[8,1024,128]{2,1,0:T(8,128)(2,1)S(1)} %get-tuple-element.60.el, bf16[8,1024,128]{2,1,0:T(8,128)(2,1)S(1)} %get-tuple-element.61.nh, ...), custom_call_target="tpu_custom_call" | custom-call | flops 536870912 | bytes 9183232 | tf_op jit(solution)/shard_map/pallas_call | solution.py:470
  26.8 2.5 %collective-permute-done.5.far = f32[128,256]{1,0:T(8,128)S(1)} collective-permute-done((f32[128,256]{1,0:T(8,128)S(1)}, f32[128,256]{1,0:T(8,128)S(1)}, u32[]{:S(2)}, u32[]{:S(2)}) %collective-permute-start.5) | collective-permute-done | bytes 131104 | tf_op jit(solution)/shard_map/ppermute | solution.py:493
  29.2 1.4 %shard_map.137 = (f32[64,1024]{1,0:T(8,128)S(1)}, f32[72,384]{1,0:T(8,128)S(1)}) custom-call(s32[1]{0:T(128)} %bitcast.place, f32[64,1024]{1,0:T(8,128)S(1)} %get-tuple-element.58.level.field.held, f32[64,1024]{1,0:T(8,128)S(1)} %shard_map.133.partial, f32[1,1024]{1,0:T(1,128)S(1)} %get-tuple-element.50.depth, f32[128,256]{1,0:T(8,128)S(1)} %collective-permute-done.4.near, ...), custom_call_target="tpu_custom_call" | custom-call | flops 536870912 | bytes 9570308 | tf_op jit(solution)/shard_map/pallas_call | solution.py:470
  30.6 0.7 %shard_map.140 = f32[72,384]{1,0:T(8,128)S(1)} custom-call(s32[1]{0:T(128)} %bitcast.place, f32[64,1024]{1,0:T(8,128)S(1)} %get-tuple-element.79.level, s32[2,256]{1,0:T(2,128)S(1)} %get-tuple-element.57.lists, bf16[8,1024,128]{2,1,0:T(8,128)(2,1)S(1)} %get-tuple-element.76.high, bf16[8,1024,128]{2,1,0:T(8,128)(2,1)S(1)} %get-tuple-element.77.low, ...), custom_call_target="tpu_custom_call" | custom-call | flops 536870912 | bytes 4585476 | tf_op jit(solution)/shard_map/pallas_call | solution.py:470
  31.4 2.1 %collective-permute-start.7 = (f32[72,384]{1,0:T(8,128)S(1)}, f32[72,384]{1,0:T(8,128)S(1)}, u32[]{:S(2)}, u32[]{:S(2)}) collective-permute-start(f32[72,384]{1,0:T(8,128)S(1)} %get-tuple-element.84), channel_id=1, source_target_pairs={{1,2},{2,1},{3,4},{4,3},{5,6},{6,5},{7,8},{8,7},{9,10},{10,9},{11,... | collective-permute-start | bytes 331784 | tf_op jit(solution)/shard_map/ppermute | solution.py:493
  33.5 1.3 %shard_map.138 = (f32[64,1024]{1,0:T(8,128)S(1)}, f32[64,1024]{1,0:T(8,128)S(1)}) custom-call(f32[64,1024]{1,0:T(8,128)S(1)} %get-tuple-element.79.level, bf16[8,1024,128]{2,1,0:T(8,128)(2,1)S(1)} %get-tuple-element.59.eh, bf16[8,1024,128]{2,1,0:T(8,128)(2,1)S(1)} %get-tuple-element.60.el, bf16[8,1024,128]{2,1,0:T(8,128)(2,1)S(1)} %get-tuple-element.61.nh, ...), custom_call_target="tpu_custom_call" | custom-call | flops 536870912 | bytes 9183232 | tf_op jit(solution)/shard_map/pallas_call | solution.py:470
  34.8 0.7 %shard_map.139.sums = f32[72,64]{1,0:T(8,128)S(1)} custom-call(f32[64,1024]{1,0:T(8,128)S(1)} %get-tuple-element.79.level, bf16[4,1024,128]{2,1,0:T(8,128)(2,1)S(1)} %get-tuple-element.82.high, bf16[4,1024,128]{2,1,0:T(8,128)(2,1)S(1)} %get-tuple-element.83.low, f32[8,512]{1,0:T(8,128)S(1)} %get-tuple-element.78.tables), custom_call_target="tpu_custom_call" | custom-call | flops 536870912 | bytes 2394112 | tf_op jit(solution)/shard_map/pallas_call | solution.py:470
  35.6 3.1 %collective-permute-done.7.far = f32[72,384]{1,0:T(8,128)S(1)} collective-permute-done((f32[72,384]{1,0:T(8,128)S(1)}, f32[72,384]{1,0:T(8,128)S(1)}, u32[]{:S(2)}, u32[]{:S(2)}) %collective-permute-start.7) | collective-permute-done | bytes 110624 | tf_op jit(solution)/shard_map/ppermute | solution.py:493
  38.7 3.7 %shard_map.141 = f32[3,64,1024]{2,1,0:T(8,128)} custom-call(f32[2,64,1024]{2,1,0:T(8,128)S(1)} %get-tuple-element.67.flow.field, f32[64,1024]{1,0:T(8,128)S(1)} %get-tuple-element.79.level, f32[64,1024]{1,0:T(8,128)S(1)} %get-tuple-element.80.east, f32[64,1024]{1,0:T(8,128)S(1)} %get-tuple-element.81.north, f32[72,64]{1,0:T(8,128)S(1)} %shard_map.139.sums, ...), custom_call_target="tpu_custom_call" | custom-call | flops 536870912 | bytes 6531072 | tf_op jit(solution)/shard_map/pallas_call | solution.py:470
  (7 shorter events, 0.3 us)
Async XLA Ops:
  2.7 9.1 %collective-permute-start = (f32[136,256]{1,0:T(8,128)S(1)}, f32[136,256]{1,0:T(8,128)S(1)}, u32[]{:S(2)}, u32[]{:S(2)}) collective-permute-start(f32[136,256]{1,0:T(8,128)S(1)} %get-tuple-element.51), channel_id=1, source_target_pairs={{0,1},{1,0},{2,3},{3,2},{4,5},{5,4},{6,7},{7,6},{8,9},{9,8},{10,11... | collective-permute-start | bytes 417800 | tf_op jit(solution)/shard_map/ppermute | solution.py:487
  3.4 8.3 %collective-permute-start.1 = (f32[136,256]{1,0:T(8,128)S(1)}, f32[136,256]{1,0:T(8,128)S(1)}, u32[]{:S(2)}, u32[]{:S(2)}) collective-permute-start(f32[136,256]{1,0:T(8,128)S(1)} %get-tuple-element.52), channel_id=1, source_target_pairs={{1,2},{2,1},{3,4},{4,3},{5,6},{6,5},{7,8},{8,7},{9,10},{10,9},{11,... | collective-permute-start | bytes 417800 | tf_op jit(solution)/shard_map/ppermute | solution.py:493
  12.9 3.9 %collective-permute-start.2 = (f32[64,256]{1,0:T(8,128)S(1)}, f32[64,256]{1,0:T(8,128)S(1)}, u32[]{:S(2)}, u32[]{:S(2)}) collective-permute-start(f32[64,256]{1,0:T(8,128)S(1)} %shard_map.131), channel_id=1, source_target_pairs={{0,1},{1,0},{2,3},{3,2},{4,5},{5,4},{6,7},{7,6},{8,9},{9,8},{10,11... | collective-permute-start | bytes 196616 | tf_op jit(solution)/shard_map/ppermute | solution.py:487
  13.4 6.3 %collective-permute-start.3 = (f32[64,256]{1,0:T(8,128)S(1)}, f32[64,256]{1,0:T(8,128)S(1)}, u32[]{:S(2)}, u32[]{:S(2)}) collective-permute-start(f32[64,256]{1,0:T(8,128)S(1)} %get-tuple-element.66), channel_id=1, source_target_pairs={{1,2},{2,1},{3,4},{4,3},{5,6},{6,5},{7,8},{8,7},{9,10},{10,9},{11,... | collective-permute-start | bytes 196616 | tf_op jit(solution)/shard_map/ppermute | solution.py:493
  21.0 5.7 %collective-permute-start.4 = (f32[128,256]{1,0:T(8,128)S(1)}, f32[128,256]{1,0:T(8,128)S(1)}, u32[]{:S(2)}, u32[]{:S(2)}) collective-permute-start(f32[128,256]{1,0:T(8,128)S(1)} %shard_map.134), channel_id=1, source_target_pairs={{0,1},{1,0},{2,3},{3,2},{4,5},{5,4},{6,7},{7,6},{8,9},{9,8},{10,11... | collective-permute-start | bytes 393224 | tf_op jit(solution)/shard_map/ppermute | solution.py:487
  21.5 7.7 %collective-permute-start.5 = (f32[128,256]{1,0:T(8,128)S(1)}, f32[128,256]{1,0:T(8,128)S(1)}, u32[]{:S(2)}, u32[]{:S(2)}) collective-permute-start(f32[128,256]{1,0:T(8,128)S(1)} %get-tuple-element.68), channel_id=1, source_target_pairs={{1,2},{2,1},{3,4},{4,3},{5,6},{6,5},{7,8},{8,7},{9,10},{10,9},{11,... | collective-permute-start | bytes 393224 | tf_op jit(solution)/shard_map/ppermute | solution.py:493
  31.4 4.2 %collective-permute-start.6 = (f32[72,384]{1,0:T(8,128)S(1)}, f32[72,384]{1,0:T(8,128)S(1)}, u32[]{:S(2)}, u32[]{:S(2)}) collective-permute-start(f32[72,384]{1,0:T(8,128)S(1)} %shard_map.140), channel_id=1, source_target_pairs={{0,1},{1,0},{2,3},{3,2},{4,5},{5,4},{6,7},{7,6},{8,9},{9,8},{10,11... | collective-permute-start | bytes 331784 | tf_op jit(solution)/shard_map/ppermute | solution.py:487
  31.4 7.3 %collective-permute-start.7 = (f32[72,384]{1,0:T(8,128)S(1)}, f32[72,384]{1,0:T(8,128)S(1)}, u32[]{:S(2)}, u32[]{:S(2)}) collective-permute-start(f32[72,384]{1,0:T(8,128)S(1)} %get-tuple-element.84), channel_id=1, source_target_pairs={{1,2},{2,1},{3,4},{4,3},{5,6},{6,5},{7,8},{8,7},{9,10},{10,9},{11,... | collective-permute-start | bytes 331784 | tf_op jit(solution)/shard_map/ppermute | solution.py:493

commit v6 on v5

--- a/solution.py
+++ b/solution.py
@@ -150,8 +150,9 @@
     ghosts = geh.shape[1]
     turned = (1 - (place[0] & 1)) * (ghosts // 2)
     count = nodes // LANES
-    for tile in range(count):
-        cut = slice(tile * LANES, (tile + 1) * LANES)
+    stride = min(4 * LANES, nodes)
+    for begin in range(0, nodes, stride):
+        cut = slice(begin, begin + stride)
         targets = []
         for s in range(slots):
             raw = conn[s : s + 1, cut]
@@ -167,17 +168,22 @@
             targets_at[s : s + 1, cut] = targets[s]
             for d in range(2):
                 weights_at[d, s : s + 1, cut] = weights[d][s]
-        build_operator(targets, weights, (eh, el, nh, nl), 0, nodes, tile, 8)
+
+    def held(tile):
+        cut = slice(tile * LANES, (tile + 1) * LANES)
+        return [targets_at[s : s + 1, cut] for s in range(slots)], [
+            [weights_at[d, s : s + 1, cut] for s in range(slots)] for d in range(2)
+        ]
+
+    for tile in range(count):
+        build_operator(*held(tile), (eh, el, nh, nl), 0, nodes, tile, 8)
     for d in range(2):
         stacks[d] = stacked(state[1 + d])
     for tile in range(count):
         pair, d = divmod(tile, 2)
         span = slice(2 * pair * LANES, 2 * (pair + 1) * LANES)
         found = product(stacks[d], *((eh, el), (nh, nl))[d], 2 * pair, 2) - state[1 + d, :, span] * totals[d : d + 1, span]
-        cut = slice(tile * LANES, (tile + 1) * LANES)
-        targets = [targets_at[s : s + 1, cut] for s in range(slots)]
-        weights = [[weights_at[g, s : s + 1, cut] for s in range(slots)] for g in range(2)]
-        build_operator(targets, weights, (geh, gel, gnh, gnl), nodes, ghosts, tile, True)
+        build_operator(*held(tile), (geh, gel, gnh, gnl), nodes, ghosts, tile, True)
         partial[:, span] = found if d == 0 else partial[:, span] + found
 
 
@@ -345,7 +351,8 @@
     )
 
 
-def own_sums_kernel(level, high, low, tables, sums):
+def last_slope_kernel(level, eh, el, nh, nl, totals, high, low, tables, east, north, sums):
+    slope_kernel(level, eh, el, nh, nl, totals, east, north)
     sums[...] = list_sums(product(stacked(level[...]), high, low), tables[4:5, :], tables[5:6, :])
 
 
@@ -595,8 +602,12 @@
     from_far = to_other(far)
     (near,) = call(near_sums_kernel, [payload], [place, level, send_list, high, low, tables], scalars=1, flops=work)
     from_near = to_partner(near)
-    east, north = call(slope_kernel, [field] * 2, [level, *operators, totals], flops=work)
-    (sums,) = call(own_sums_kernel, [shape(members + ROWS, members)], [level, own_high, own_low, tables], flops=work)
+    east, north, sums = call(
+        last_slope_kernel,
+        [field] * 2 + [shape(members + ROWS, members)],
+        [level, *operators, totals, own_high, own_low, tables],
+        flops=work,
+    )
     (out,) = call(
         analysis_kernel,
         [shape(3, members, nodes)],

time: 42.7 us -> 42.5 us (level)
    pallas_call x15 -> x14, Pallas kernels: 22.2 us -> 21.8 us  [call(): pl.pallas_call(kernel, out_shape=outs, in_specs=in_specs, out_specs=[pl.B...]
  transfers between devices with their start and end apart: 8 -> 8, of which waited for: 3 -> 3; matrix products, arithmetic and copies ran while one was open for 0% -> 0% of each run, Pallas kernels for 28% -> 27%
where the time goes in v6:
time: 42.5 us; the launch traced here: 42.3 us
  Pallas kernels  21.8 us (51%)
  starting transfers between devices  11 us (26%)
  waiting for transfers between devices  8.6 us (20%)
  between operations  0.97 us (2%)
    pallas_call x14, Pallas kernels, call(): pl.pallas_call(kernel, out_shape=outs, in_specs=in_specs, out_specs=[pl.B...  21.8 us
    ppermute x4, starting transfers between devices, to_other(): return lax.ppermute(value, 'mesh', others)  9.2 us
    ppermute x4, waiting for transfers between devices, to_other(): return lax.ppermute(value, 'mesh', others)  8.58 us
    ppermute x4, starting transfers between devices, to_partner(): return lax.ppermute(value, 'mesh', pairs)  1.76 us
  transfers between devices with their start and end apart: 8, of which 3 were waited for; matrix products, arithmetic and copies ran while one was open for 0% of the time, Pallas kernels for 27%

profile of v6, /device:TPU:25, one launch (start us, length us, event | category | flops | bytes accessed | tf_op | source)
XLA Modules:
  0.0 42.3 jit_solution(13776491523733431207)
XLA Ops:
  0.7 2.0 %shard_map.127 = (f32[136,256]{1,0:T(8,128)S(1)}, f32[136,256]{1,0:T(8,128)S(1)}, f32[3,64,1024]{2,1,0:T(8,128)S(1)}, s32[2,256]{1,0:T(2,128)S(1)}, s32[1,512]{1...) custom-call(s32[1]{0:T(128)} %bitcast.place, ...), custom_call_target="tpu_custom_call" | custom-call | bytes 2134024 | tf_op jit(solution)/shard_map/pallas_call | solution.py:477
  2.7 0.7 %collective-permute-start = (f32[136,256]{1,0:T(8,128)S(1)}, f32[136,256]{1,0:T(8,128)S(1)}, u32[]{:S(2)}, u32[]{:S(2)}) collective-permute-start(f32[136,256]{1,0:T(8,128)S(1)} %get-tuple-element.52), channel_id=1, source_target_pairs={{0,1},{1,0},{2,3},{3,2},{4,5},{5,4},{6,7},{7,6},{8,9},{9,8},{10,11... | collective-permute-start | bytes 417800 | tf_op jit(solution)/shard_map/ppermute | solution.py:494
  3.4 3.0 %collective-permute-start.1 = (f32[136,256]{1,0:T(8,128)S(1)}, f32[136,256]{1,0:T(8,128)S(1)}, u32[]{:S(2)}, u32[]{:S(2)}) collective-permute-start(f32[136,256]{1,0:T(8,128)S(1)} %get-tuple-element.53), channel_id=1, source_target_pairs={{1,2},{2,1},{3,4},{4,3},{5,6},{6,5},{7,8},{8,7},{9,10},{10,9},{11,... | collective-permute-start | bytes 417800 | tf_op jit(solution)/shard_map/ppermute | solution.py:500
  6.5 5.1 %shard_map.128 = (bf16[8,1024,128]{2,1,0:T(8,128)(2,1)S(1)}, bf16[8,1024,128]{2,1,0:T(8,128)(2,1)S(1)}, bf16[8,1024,128]{2,1,0:T(8,128)(2,1)S(1)}, bf16[8,1024,1...) custom-call(s32[1]{0:T(128)} %bitcast.place, ...), custom_call_target="tpu_custom_call" | custom-call | flops 1610612736 | bytes 13737988 | tf_op jit(solution)/shard_map/pallas_call | solution.py:477
  11.6 0.9 %shard_map.129 = (f32[64,1024]{1,0:T(8,128)S(1)}, f32[64,256]{1,0:T(8,128)S(1)}) custom-call(s32[1]{0:T(128)} %bitcast.place, f32[3,64,1024]{2,1,0:T(8,128)S(1)} %get-tuple-element.46.state.held.flow, f32[64,1024]{1,0:T(8,128)S(1)} %get-tuple-element.50.partial, f32[1,1024]{1,0:T(1,128)S(1)} %get-tuple-element.51.depth, ...), custom_call_target="tpu_custom_call" | custom-call | flops 536870912 | bytes 5855236 | tf_op jit(solution)/shard_map/pallas_call | solution.py:477
  12.5 0.3 shard_map.131
  12.7 0.4 %collective-permute-start.2 = (f32[64,256]{1,0:T(8,128)S(1)}, f32[64,256]{1,0:T(8,128)S(1)}, u32[]{:S(2)}, u32[]{:S(2)}) collective-permute-start(f32[64,256]{1,0:T(8,128)S(1)} %shard_map.131), channel_id=1, source_target_pairs={{0,1},{1,0},{2,3},{3,2},{4,5},{5,4},{6,7},{7,6},{8,9},{9,8},{10,11... | collective-permute-start | bytes 196616 | tf_op jit(solution)/shard_map/ppermute | solution.py:494
  13.2 2.1 %collective-permute-start.3 = (f32[64,256]{1,0:T(8,128)S(1)}, f32[64,256]{1,0:T(8,128)S(1)}, u32[]{:S(2)}, u32[]{:S(2)}) collective-permute-start(f32[64,256]{1,0:T(8,128)S(1)} %get-tuple-element.67), channel_id=1, source_target_pairs={{1,2},{2,1},{3,4},{4,3},{5,6},{6,5},{7,8},{8,7},{9,10},{10,9},{11,... | collective-permute-start | bytes 196616 | tf_op jit(solution)/shard_map/ppermute | solution.py:500
  15.3 1.3 %shard_map.130 = (f32[64,1024]{1,0:T(8,128)S(1)}, f32[64,1024]{1,0:T(8,128)S(1)}) custom-call(f32[64,1024]{1,0:T(8,128)S(1)} %get-tuple-element.59.level.field.held, bf16[8,1024,128]{2,1,0:T(8,128)(2,1)S(1)} %get-tuple-element.60.eh, bf16[8,1024,128]{2,1,0:T(8,128)(2,1)S(1)} %get-tuple-element.61.el, bf16[8,1024,128]{2,1,0:T(8,128)(2,1)S(1)} %get-tuple-element.62.nh, ...), custom_call_target="tpu_custom_call" | custom-call | flops 536870912 | bytes 9183232 | tf_op jit(solution)/shard_map/pallas_call | solution.py:477
  16.6 2.8 %collective-permute-done.3.far = f32[64,256]{1,0:T(8,128)S(1)} collective-permute-done((f32[64,256]{1,0:T(8,128)S(1)}, f32[64,256]{1,0:T(8,128)S(1)}, u32[]{:S(2)}, u32[]{:S(2)}) %collective-permute-start.3) | collective-permute-done | bytes 65568 | tf_op jit(solution)/shard_map/ppermute | solution.py:500
  19.4 0.9 %shard_map.132 = (f32[2,64,1024]{2,1,0:T(8,128)S(1)}, f32[128,256]{1,0:T(8,128)S(1)}) custom-call(s32[1]{0:T(128)} %bitcast.place, f32[3,64,1024]{2,1,0:T(8,128)S(1)} %get-tuple-element.46.state.held.flow, f32[64,1024]{1,0:T(8,128)S(1)} %get-tuple-element.65.east, f32[64,1024]{1,0:T(8,128)S(1)} %get-tuple-element.66.north, ...), custom_call_target="tpu_custom_call" | custom-call | flops 536870912 | bytes 6293508 | tf_op jit(solution)/shard_map/pallas_call | solution.py:477
  20.4 0.4 %shard_map.134 = f32[128,256]{1,0:T(8,128)S(1)} custom-call(s32[1]{0:T(128)} %bitcast.place, f32[2,64,1024]{2,1,0:T(8,128)S(1)} %get-tuple-element.68.flow.field, s32[2,256]{1,0:T(2,128)S(1)} %get-tuple-element.58.lists), custom_call_target="tpu_custom_call" | custom-call | bytes 657412 | tf_op jit(solution)/shard_map/pallas_call | solution.py:477
  20.8 0.5 %collective-permute-start.4 = (f32[128,256]{1,0:T(8,128)S(1)}, f32[128,256]{1,0:T(8,128)S(1)}, u32[]{:S(2)}, u32[]{:S(2)}) collective-permute-start(f32[128,256]{1,0:T(8,128)S(1)} %shard_map.134), channel_id=1, source_target_pairs={{0,1},{1,0},{2,3},{3,2},{4,5},{5,4},{6,7},{7,6},{8,9},{9,8},{10,11... | collective-permute-start | bytes 393224 | tf_op jit(solution)/shard_map/ppermute | solution.py:494
  21.3 1.9 %collective-permute-start.5 = (f32[128,256]{1,0:T(8,128)S(1)}, f32[128,256]{1,0:T(8,128)S(1)}, u32[]{:S(2)}, u32[]{:S(2)}) collective-permute-start(f32[128,256]{1,0:T(8,128)S(1)} %get-tuple-element.69), channel_id=1, source_target_pairs={{1,2},{2,1},{3,4},{4,3},{5,6},{6,5},{7,8},{8,7},{9,10},{10,9},{11,... | collective-permute-start | bytes 393224 | tf_op jit(solution)/shard_map/ppermute | solution.py:500
  23.3 0.8 %shard_map.135 = (bf16[4,1024,128]{2,1,0:T(8,128)(2,1)S(1)}, bf16[4,1024,128]{2,1,0:T(8,128)(2,1)S(1)}, f32[8,512]{1,0:T(8,128)S(1)}, f32[8,1536]{1,0:T(8,128)S(1)}) custom-call(s32[1]{0:T(128)} %bitcast.place, s32[1]{0:T(128)S(6)} %copy.14.length, f32[136,256]{1,0:T(8,128)S(1)} %collective-permute-done.near, f32[136,256]{1,0:T(8,128)S(1)} %collective-permute-done.1.far, ...), custom_call_target="tpu_custom_call" | custom-call | flops 536870912 | bytes 2478088 | tf_op jit(solution)/shard_map/pallas_call | solution.py:477
  24.1 1.1 %shard_map.136 = (bf16[8,1024,128]{2,1,0:T(8,128)(2,1)S(1)}, bf16[8,1024,128]{2,1,0:T(8,128)(2,1)S(1)}) custom-call(f32[8,1536]{1,0:T(8,128)S(1)} %get-tuple-element.76.found), custom_call_target="tpu_custom_call" | custom-call | flops 536870912 | bytes 4243456 | tf_op jit(solution)/shard_map/pallas_call | solution.py:477
  25.3 1.3 %shard_map.133.partial = f32[64,1024]{1,0:T(8,128)S(1)} custom-call(f32[2,64,1024]{2,1,0:T(8,128)S(1)} %get-tuple-element.68.flow.field, bf16[8,1024,128]{2,1,0:T(8,128)(2,1)S(1)} %get-tuple-element.60.eh, bf16[8,1024,128]{2,1,0:T(8,128)(2,1)S(1)} %get-tuple-element.61.el, bf16[8,1024,128]{2,1,0:T(8,128)(2,1)S(1)} %get-tuple-element.62.nh, ...), custom_call_target="tpu_custom_call" | custom-call | flops 536870912 | bytes 9183232 | tf_op jit(solution)/shard_map/pallas_call | solution.py:477
  26.5 2.5 %collective-permute-done.5.far = f32[128,256]{1,0:T(8,128)S(1)} collective-permute-done((f32[128,256]{1,0:T(8,128)S(1)}, f32[128,256]{1,0:T(8,128)S(1)}, u32[]{:S(2)}, u32[]{:S(2)}) %collective-permute-start.5) | collective-permute-done | bytes 131104 | tf_op jit(solution)/shard_map/ppermute | solution.py:500
  29.0 1.4 %shard_map.137 = (f32[64,1024]{1,0:T(8,128)S(1)}, f32[72,384]{1,0:T(8,128)S(1)}) custom-call(s32[1]{0:T(128)} %bitcast.place, f32[64,1024]{1,0:T(8,128)S(1)} %get-tuple-element.59.level.field.held, f32[64,1024]{1,0:T(8,128)S(1)} %shard_map.133.partial, f32[1,1024]{1,0:T(1,128)S(1)} %get-tuple-element.51.depth, f32[128,256]{1,0:T(8,128)S(1)} %collective-permute-done.4.near, ...), custom_call_target="tpu_custom_call" | custom-call | flops 536870912 | bytes 9570308 | tf_op jit(solution)/shard_map/pallas_call | solution.py:477
  30.4 0.7 %shard_map.139 = f32[72,384]{1,0:T(8,128)S(1)} custom-call(s32[1]{0:T(128)} %bitcast.place, f32[64,1024]{1,0:T(8,128)S(1)} %get-tuple-element.80.level, s32[2,256]{1,0:T(2,128)S(1)} %get-tuple-element.58.lists, bf16[8,1024,128]{2,1,0:T(8,128)(2,1)S(1)} %get-tuple-element.77.high, bf16[8,1024,128]{2,1,0:T(8,128)(2,1)S(1)} %get-tuple-element.78.low, ...), custom_call_target="tpu_custom_call" | custom-call | flops 536870912 | bytes 4585476 | tf_op jit(solution)/shard_map/pallas_call | solution.py:477
  31.2 2.1 %collective-permute-start.7 = (f32[72,384]{1,0:T(8,128)S(1)}, f32[72,384]{1,0:T(8,128)S(1)}, u32[]{:S(2)}, u32[]{:S(2)}) collective-permute-start(f32[72,384]{1,0:T(8,128)S(1)} %get-tuple-element.86), channel_id=1, source_target_pairs={{1,2},{2,1},{3,4},{4,3},{5,6},{6,5},{7,8},{8,7},{9,10},{10,9},{11,... | collective-permute-start | bytes 331784 | tf_op jit(solution)/shard_map/ppermute | solution.py:500
  33.3 1.9 %shard_map.138 = (f32[64,1024]{1,0:T(8,128)S(1)}, f32[64,1024]{1,0:T(8,128)S(1)}, f32[72,64]{1,0:T(8,128)S(1)}) custom-call(f32[64,1024]{1,0:T(8,128)S(1)} %get-tuple-element.80.level, bf16[8,1024,128]{2,1,0:T(8,128)(2,1)S(1)} %get-tuple-element.60.eh, bf16[8,1024,128]{2,1,0:T(8,128)(2,1)S(1)} %get-tuple-element.61.el, ...), custom_call_target="tpu_custom_call" | custom-call | flops 536870912 | bytes 11315200 | tf_op jit(solution)/shard_map/pallas_call | solution.py:477
  35.2 3.3 %collective-permute-done.7.far = f32[72,384]{1,0:T(8,128)S(1)} collective-permute-done((f32[72,384]{1,0:T(8,128)S(1)}, f32[72,384]{1,0:T(8,128)S(1)}, u32[]{:S(2)}, u32[]{:S(2)}) %collective-permute-start.7) | collective-permute-done | bytes 110624 | tf_op jit(solution)/shard_map/ppermute | solution.py:500
  38.5 3.7 %shard_map.140 = f32[3,64,1024]{2,1,0:T(8,128)} custom-call(f32[2,64,1024]{2,1,0:T(8,128)S(1)} %get-tuple-element.68.flow.field, f32[64,1024]{1,0:T(8,128)S(1)} %get-tuple-element.80.level, f32[64,1024]{1,0:T(8,128)S(1)} %get-tuple-element.83.east, f32[64,1024]{1,0:T(8,128)S(1)} %get-tuple-element.84.north, f32[72,64]{1,0:T(8,128)S(1)} %get-tuple-element.85.sums, ...), custom_call_target="tpu_custom_call" | custom-call | flops 536870912 | bytes 6531072 | tf_op jit(solution)/shard_map/pallas_call | solution.py:477
  (6 shorter events, 0.1 us)
Async XLA Ops:
  2.7 8.9 %collective-permute-start = (f32[136,256]{1,0:T(8,128)S(1)}, f32[136,256]{1,0:T(8,128)S(1)}, u32[]{:S(2)}, u32[]{:S(2)}) collective-permute-start(f32[136,256]{1,0:T(8,128)S(1)} %get-tuple-element.52), channel_id=1, source_target_pairs={{0,1},{1,0},{2,3},{3,2},{4,5},{5,4},{6,7},{7,6},{8,9},{9,8},{10,11... | collective-permute-start | bytes 417800 | tf_op jit(solution)/shard_map/ppermute | solution.py:494
  3.4 8.1 %collective-permute-start.1 = (f32[136,256]{1,0:T(8,128)S(1)}, f32[136,256]{1,0:T(8,128)S(1)}, u32[]{:S(2)}, u32[]{:S(2)}) collective-permute-start(f32[136,256]{1,0:T(8,128)S(1)} %get-tuple-element.53), channel_id=1, source_target_pairs={{1,2},{2,1},{3,4},{4,3},{5,6},{6,5},{7,8},{8,7},{9,10},{10,9},{11,... | collective-permute-start | bytes 417800 | tf_op jit(solution)/shard_map/ppermute | solution.py:500
  12.7 3.9 %collective-permute-start.2 = (f32[64,256]{1,0:T(8,128)S(1)}, f32[64,256]{1,0:T(8,128)S(1)}, u32[]{:S(2)}, u32[]{:S(2)}) collective-permute-start(f32[64,256]{1,0:T(8,128)S(1)} %shard_map.131), channel_id=1, source_target_pairs={{0,1},{1,0},{2,3},{3,2},{4,5},{5,4},{6,7},{7,6},{8,9},{9,8},{10,11... | collective-permute-start | bytes 196616 | tf_op jit(solution)/shard_map/ppermute | solution.py:494
  13.2 6.3 %collective-permute-start.3 = (f32[64,256]{1,0:T(8,128)S(1)}, f32[64,256]{1,0:T(8,128)S(1)}, u32[]{:S(2)}, u32[]{:S(2)}) collective-permute-start(f32[64,256]{1,0:T(8,128)S(1)} %get-tuple-element.67), channel_id=1, source_target_pairs={{1,2},{2,1},{3,4},{4,3},{5,6},{6,5},{7,8},{8,7},{9,10},{10,9},{11,... | collective-permute-start | bytes 196616 | tf_op jit(solution)/shard_map/ppermute | solution.py:500
  20.8 5.7 %collective-permute-start.4 = (f32[128,256]{1,0:T(8,128)S(1)}, f32[128,256]{1,0:T(8,128)S(1)}, u32[]{:S(2)}, u32[]{:S(2)}) collective-permute-start(f32[128,256]{1,0:T(8,128)S(1)} %shard_map.134), channel_id=1, source_target_pairs={{0,1},{1,0},{2,3},{3,2},{4,5},{5,4},{6,7},{7,6},{8,9},{9,8},{10,11... | collective-permute-start | bytes 393224 | tf_op jit(solution)/shard_map/ppermute | solution.py:494
  21.3 7.7 %collective-permute-start.5 = (f32[128,256]{1,0:T(8,128)S(1)}, f32[128,256]{1,0:T(8,128)S(1)}, u32[]{:S(2)}, u32[]{:S(2)}) collective-permute-start(f32[128,256]{1,0:T(8,128)S(1)} %get-tuple-element.69), channel_id=1, source_target_pairs={{1,2},{2,1},{3,4},{4,3},{5,6},{6,5},{7,8},{8,7},{9,10},{10,9},{11,... | collective-permute-start | bytes 393224 | tf_op jit(solution)/shard_map/ppermute | solution.py:500
  31.2 4.1 %collective-permute-start.6 = (f32[72,384]{1,0:T(8,128)S(1)}, f32[72,384]{1,0:T(8,128)S(1)}, u32[]{:S(2)}, u32[]{:S(2)}) collective-permute-start(f32[72,384]{1,0:T(8,128)S(1)} %shard_map.139), channel_id=1, source_target_pairs={{0,1},{1,0},{2,3},{3,2},{4,5},{5,4},{6,7},{7,6},{8,9},{9,8},{10,11... | collective-permute-start | bytes 331784 | tf_op jit(solution)/shard_map/ppermute | solution.py:494
  31.2 7.3 %collective-permute-start.7 = (f32[72,384]{1,0:T(8,128)S(1)}, f32[72,384]{1,0:T(8,128)S(1)}, u32[]{:S(2)}, u32[]{:S(2)}) collective-permute-start(f32[72,384]{1,0:T(8,128)S(1)} %get-tuple-element.86), channel_id=1, source_target_pairs={{1,2},{2,1},{3,4},{4,3},{5,6},{6,5},{7,8},{8,7},{9,10},{10,9},{11,... | collective-permute-start | bytes 331784 | tf_op jit(solution)/shard_map/ppermute | solution.py:500
